TPU v7x, 512 devices: a whole 4x8x8 slice. The times are simulated.
512 devices in a mesh: up: 32 (over z, x_hi, core), down: 16 (over x_lo, y).
Axes of the slice: x: 4 (x_hi: 2, x_lo: 2; x = x_hi * 2 + x_lo), y: 8, z: 8, core: 2. Of those that a mesh axis runs over, the one named last changes fastest.
Arguments:
- deltas: bfloat16 [256, 16384], P('down', 'up'), may hold values from -6 to 6
- gradients: bfloat16 [256, 16384], P('up', 'down'), may hold values from -0.375 to 0.375
- up_blocks: int32 [8, 64], P(None, 'up'), may hold values from 0 to 3, as said below
- down_blocks: int32 [64], P('down'), may hold values from 0 to 7, as said below
- decoder: bfloat16 [16384, 4608], P('up', 'down'), may hold values from -0.09375 to 0.09375
- encoder: bfloat16 [4608, 16384], P('up', 'down'), may hold values from -6 to 6
Outputs:
- edge_scores: float32 [16384, 16384], P('up', 'down')
Inputs may be any that keep to these rules, and one draw needn't show every extreme that they name: `up_blocks`: for each window and each index i of up, the 2 entries in columns i * 2 to (i + 1) * 2 - 1 are distinct. `down_blocks`: for each index j of down, the 4 entries j * 4 to (j + 1) * 4 - 1 are distinct.
All inputs are finite; a program needn't handle non-finite values.
Results may differ from a plain program's by a relative error of at most 0.0003.
Values may be sent and summed in bfloat16 or wider, within the bound.
No kernel may reach another device: no remote copies, remote signals or barrier semaphores. Data moves between devices by JAX's collectives and lax.ppermute only.
A program may use at most 64 MiB of HBM per device.

v0:
```python
import jax
import jax.numpy as jnp
from jax import lax
from jax.sharding import Mesh
from jax.sharding import PartitionSpec as P

UF_DEV = 512
VF_DEV = 1024
BLOCK = 128
DACT = 4
WIN = 32
DOWN = ("down_0", "down_1")
UP = ("up_0", "up_1", "up_2")


def in_order(pieces, dim):
    pieces = jnp.moveaxis(pieces, 0, dim)
    lengths = pieces.shape
    return pieces.reshape(*lengths[:dim], lengths[dim] * lengths[dim + 1], *lengths[dim + 2 :])


def gather_in_order(value, axes, turns):
    pieces = value
    for k in turns:
        pieces = lax.all_gather(pieces, axes[k])
    done = turns[::-1]
    back = [done.index(k) for k in range(len(axes))]
    pieces = pieces.transpose(*back, *range(len(axes), pieces.ndim))
    return pieces.reshape(-1, *value.shape)


def whole_of(value, axes, turns, dim):
    return in_order(gather_in_order(value, axes, turns), dim)


def copy_for_each(value, axis):
    peers = lax.axis_size(axis)
    return lax.all_to_all(
        jnp.broadcast_to(value[None], (peers, *value.shape)), axis, 0, 0, tiled=True
    )


def collect(value, axis, dim):
    return in_order(copy_for_each(value, axis), dim)


def local(deltas, gradients, up_blocks, down_blocks, decoder, encoder):
    token_deltas = whole_of(deltas, DOWN, (0, 1), 0)
    token_grads = collect(gradients, UP, 0)
    tokens_all = token_deltas.shape[0]
    windows = tokens_all // WIN
    row_blocks = UF_DEV // BLOCK
    col_blocks = VF_DEV // BLOCK
    local_ids = jnp.arange(row_blocks, dtype=jnp.int32)
    block_on = jnp.any(up_blocks[:, :, None] == local_ids[None, None, :], axis=1)
    masked = token_deltas.reshape(windows, WIN, row_blocks, BLOCK) * block_on[
        :, None, :, None
    ].astype(token_deltas.dtype)
    masked = masked.reshape(tokens_all, UF_DEV)
    dec_whole = whole_of(decoder, DOWN, (0, 1), 1)
    enc_height = encoder.shape[0]
    enc_used = jnp.take(
        encoder.reshape(enc_height, col_blocks, BLOCK), down_blocks, axis=1
    ).reshape(enc_height, DACT * BLOCK)
    virtual = jnp.dot(
        dec_whole, whole_of(enc_used, UP, (1, 0, 2), 0), preferred_element_type=jnp.float32
    )
    grad_used = jnp.take(
        token_grads.reshape(tokens_all, col_blocks, BLOCK), down_blocks, axis=1
    ).reshape(tokens_all, DACT * BLOCK)
    product = lax.dot_general(
        masked, grad_used, (((0,), (0,)), ((), ())), preferred_element_type=jnp.float32
    )
    scored = (product * virtual).reshape(UF_DEV, DACT, BLOCK)
    filled = jnp.zeros((UF_DEV, col_blocks, BLOCK), jnp.float32).at[:, down_blocks, :].set(scored)
    return filled.reshape(UF_DEV, VF_DEV)


def solution(mesh):
    torus = Mesh(mesh.devices.reshape(8, 2, 2, 2, 8), ("up_0", "up_1", "up_2", "down_0", "down_1"))
    return jax.shard_map(
        local,
        mesh=torus,
        in_specs=(P(DOWN, UP), P(UP, DOWN), P(None, UP), P(DOWN), P(UP, DOWN), P(UP, DOWN)),
        out_specs=P(UP, DOWN),
        check_vma=False,
    )
```

profile of v0, /device:TPU:1, one launch (start us, length us, event | category | flops | bytes accessed | tf_op | source)
XLA Modules:
  0.0 176.5 jit_solution(16812434283706417548)
XLA Ops:
  6.5 0.0 copy-start
  6.5 0.0 copy-start.2
  6.5 0.0 copy-start.4
  6.5 0.0 copy-start.3
  6.5 0.0 all-gather.10.cloned.1.call-start
  6.6 0.7 compare_and_fusion
  7.3 0.7 compare_select_fusion
  7.9 0.1 broadcast_bitcast_fusion
  8.0 0.0 copy-done
  8.0 0.1 copy_bitcast_fusion.1
  8.1 0.6 gather_fusion.1
  8.7 0.1 copy.58
  8.7 0.1 gather.12
  8.8 6.9 %all_gather.43 = bf16[2,144,512]{2,1,0:T(8,128)(2,1)} all-gather(bf16[1,144,512]{2,1,0:T(8,128)(2,1)S(1)} %broadcast_select_fusion), channel_id=1, replica_groups=mesh['up_0'=8,'up_1'=2,'up_2'=2,'down_0'=2,'down_1'=8] {'up_1'}, dimensions={0}, use_global_device_ids=true | all-gather | bytes 442368 | tf_op jit(solution)/shard_map/all_gather | solution.py:25
  15.7 0.0 all-gather.10.cloned.1.call-update
  15.7 0.0 all-gather.14.cloned.1.call-start
  15.8 7.2 %all-gather.4 = bf16[1024,288]{0,1:T(8,128)(2,1)S(1)} all-gather(bf16[512,288]{0,1:T(8,128)(2,1)} %param.10), channel_id=6, replica_groups=mesh['up_0'=8,'up_1'=2,'up_2'=2,'down_0'=2,'down_1'=8] {'down_0'}, dimensions={0}, use_global_device_ids=true | all-gather | bytes 884736 | tf_op jit(solution)/shard_map/all_gather | solution.py:25
  23.0 0.9 copy.70
  23.9 0.0 all-gather.14.cloned.1.call-update
  23.9 0.0 all-gather.12.cloned.1.call-start
  23.9 40.4 %all-gather.10.cloned.1.call-done = bf16[16,144,512]{2,1,0:T(8,128)(2,1)} async-done(((bf16[2,144,512]{2,1,0:T(8,128)(2,1)}), bf16[16,144,512]{2,1,0:T(8,128)(2,1)}) %all-gather.10.cloned.1.call-update) | async-done | bytes 2359312 | tf_op jit(solution)/shard_map/all_gather | solution.py:25
  64.3 0.0 all-gather.12.cloned.1.call-update
  64.3 0.0 copy-done.2
  64.3 0.9 broadcast_in_dim.42
  65.2 10.6 %all-to-all-start = ((bf16[32,8,1024]{2,1,0:T(8,128)(2,1)}), bf16[32,8,1024]{2,1,0:T(8,128)(2,1)S(1)}, u32[]{:S(2)}, u32[]{:S(2)}) async-start(bf16[32,8,1024]{2,1,0:T(8,128)(2,1)} %broadcast_in_dim.42), calls=%async_computation | async-start | bytes 1048576 | tf_op jit(solution)/shard_map/all_to_all | solution.py:38
  75.8 0.0 copy-done.4
  75.8 0.1 copy.52
  75.9 0.1 mul.19
  76.0 0.0 copy-done.3
  76.1 3.6 %all-gather = bf16[32,512]{1,0:T(8,128)(2,1)S(1)} all-gather(bf16[16,512]{1,0:T(8,128)(2,1)S(1)} %copy-done.3), channel_id=2, replica_groups=mesh['up_0'=8,'up_1'=2,'up_2'=2,'down_0'=2,'down_1'=8] {'down_0'}, dimensions={0}, use_global_device_ids=true | all-gather | bytes 49152 | tf_op jit(solution)/shard_map/all_gather | solution.py:25
  79.6 23.1 %all-gather.1 = bf16[16,16,512]{2,1,0:T(8,128)(2,1)S(1)} all-gather(bf16[2,16,512]{2,1,0:T(8,128)(2,1)S(1)} %bitcast.64), channel_id=3, replica_groups=mesh['up_0'=8,'up_1'=2,'up_2'=2,'down_0'=2,'down_1'=8] {'down_1'}, dimensions={0}, use_global_device_ids=true | all-gather | bytes 294912 | tf_op jit(solution)/shard_map/all_gather | solution.py:25
  102.8 0.0 all-to-all-done
  102.8 0.1 copy.67
  102.9 0.1 copy.55
  103.0 0.6 gather_fusion
  103.6 0.1 select_bitcast_fusion
  103.7 0.1 copy.56
  103.8 0.3 fusion.2
  104.1 28.5 %all-gather.14.cloned.1.call-done = bf16[16,512,288]{1,2,0:T(8,128)(2,1)} async-done(((bf16[2,512,288]{1,2,0:T(8,128)(2,1)}), bf16[16,512,288]{1,2,0:T(8,128)(2,1)}) %all-gather.14.cloned.1.call-update) | async-done | bytes 4718608 | tf_op jit(solution)/shard_map/all_gather | solution.py:25
  132.6 5.0 %copy.61 = bf16[2,8,512,288]{2,3,1,0:T(8,128)(2,1)} copy(bf16[2,8,512,288]{2,3,0,1:T(8,128)(2,1)} %bitcast.51) | data formatting | bytes 9437184 | tf_op jit(solution)/shard_map/transpose | solution.py:28
  137.5 20.0 %all-gather.12.cloned.1.call-done = bf16[16,2,144,512]{3,2,1,0:T(8,128)(2,1)} async-done(((bf16[8,2,144,512]{3,2,1,0:T(8,128)(2,1)}), bf16[16,2,144,512]{3,2,1,0:T(8,128)(2,1)}) %all-gather.12.cloned.1.call-update) | async-done | bytes 4718608 | tf_op jit(solution)/shard_map/all_gather | solution.py:25
  157.6 0.0 copy-start.1
  157.6 2.8 %copy.59 = bf16[8,2,2,144,512]{4,3,2,1,0:T(8,128)(2,1)S(1)} copy(bf16[8,2,2,144,512]{4,3,1,0,2:T(8,128)(2,1)} %bitcast.52) | data formatting | bytes 9437184 | tf_op jit(solution)/shard_map/transpose | solution.py:28
  160.4 0.9 copy-done.1
  161.3 2.6 %fusion = f32[512,512]{0,1:T(8,128)S(1)} fusion(f32[512,512]{0,1:T(8,128)S(1)} %fusion.2, bf16[4608,512]{1,0:T(8,128)(2,1)S(1)} %bitcast.49, bf16[512,4608]{0,1:T(8,128)(2,1)S(1)} %bitcast.48), kind=kOutput, calls=%fused_computation.4 | convolution fusion | flops 2416181248 | bytes 11534336 | tf_op jit(solution)/shard_map/dot_general | solution.py:65
  164.0 0.3 copy.62
  164.3 0.1 broadcast_in_dim.39
  164.4 0.8 scatter_fusion
  165.2 1.8 %copy.63 = f32[512,8,128]{0,2,1:T(8,128)} copy(f32[512,8,128]{2,0,1:T(8,128)S(1)} %scatter_fusion) | data formatting | bytes 4194304 | tf_op jit(solution)/shard_map/scatter | solution.py:75
  167.1 2.9 %copy.64 = f32[512,1024]{1,0:T(8,128)} copy(f32[512,1024]{0,1:T(8,128)} %bitcast.50) | data formatting | bytes 4194304 | tf_op jit(solution)/shard_map/reshape | solution.py:76
  (8 shorter events, 0.1 us)
Async XLA Ops:
  6.5 1.5 copy-start
  6.5 57.8 %copy-start.2 = (bf16[8,1024]{1,0:T(8,128)(2,1)S(1)}, bf16[8,1024]{1,0:T(8,128)(2,1)}, u32[]{:S(2)}) copy-start(bf16[8,1024]{1,0:T(8,128)(2,1)} %param.7) | copy-start | bytes 49156
  6.5 69.2 %copy-start.4 = (s32[8,2]{0,1:T(2,128)S(1)}, s32[8,2]{0,1:T(2,128)}, u32[]{:S(2)}) copy-start(s32[8,2]{0,1:T(2,128)} %param.8) | copy-start | bytes 196
  6.5 69.5 %copy-start.3 = (bf16[16,512]{1,0:T(8,128)(2,1)S(1)}, bf16[16,512]{1,0:T(8,128)(2,1)}, u32[]{:S(2)}) copy-start(bf16[16,512]{1,0:T(8,128)(2,1)} %param.6) | copy-start | bytes 49156
  6.5 57.7 %all-gather.10.cloned.1.call-start = ((), (), s32[]{:S(2)}) async-start(), calls=%async_computation.1 | async-start | bytes 2654208 | tf_op jit(solution)/shard_map/all_gather | solution.py:25
  15.7 116.9 %all-gather.14.cloned.1.call-start = ((), (), s32[]{:S(2)}) async-start(), calls=%async_computation.3 | async-start | bytes 5308416 | tf_op jit(solution)/shard_map/all_gather | solution.py:25
  23.9 133.7 %all-gather.12.cloned.1.call-start = ((), (), s32[]{:S(2)}) async-start(), calls=%async_computation.2 | async-start | bytes 7077888 | tf_op jit(solution)/shard_map/all_gather | solution.py:25
  65.2 37.6 %all-to-all-start = ((bf16[32,8,1024]{2,1,0:T(8,128)(2,1)}), bf16[32,8,1024]{2,1,0:T(8,128)(2,1)S(1)}, u32[]{:S(2)}, u32[]{:S(2)}) async-start(bf16[32,8,1024]{2,1,0:T(8,128)(2,1)} %broadcast_in_dim.42), calls=%async_computation | async-start | bytes 1048576 | tf_op jit(solution)/shard_map/all_to_all | solution.py:38
  157.6 3.8 %copy-start.1 = (bf16[2,8,512,288]{2,3,1,0:T(8,128)(2,1)S(1)}, bf16[2,8,512,288]{2,3,1,0:T(8,128)(2,1)}, u32[]{:S(2)}) copy-start(bf16[2,8,512,288]{2,3,1,0:T(8,128)(2,1)} %copy.61) | copy-start | bytes 14155780
Sparse Core Ops, SparseCore 0:
  15.8 48.3 all-gather.9
  66.4 66.1 all-gather.13
  134.7 22.8 all-gather.11
where the time goes:
time: 177 us; the launch traced here: 176 us
  waiting for transfers between devices  88.9 us (50%)
  blocking collectives  40.7 us (23%)
  local copies, waits for them, and re-layouts  18.4 us (10%)
  between operations  13.3 us (8%)
  starting transfers between devices  10.7 us (6%)
  matrix products  2.9 us (2%)
    all_gather x3, waiting for transfers between devices, gather_in_order(): pieces = lax.all_gather(pieces, axes[k])  88.9 us
    all_gather x4, blocking collectives, gather_in_order(): pieces = lax.all_gather(pieces, axes[k])  40.7 us
    all_to_all x1, starting transfers between devices, copy_for_each(): lax.all_to_all(jnp.broadcast_to(value[None], (peers, *value.shape)), axis...  10.6 us
    transpose x2, local copies, waits for them, and re-layouts, gather_in_order(): pieces = pieces.transpose(*back, *range(len(axes), pieces.ndim))  7.77 us
  transfers between devices with their start and end apart: 4, of which 3 were waited for; matrix products, arithmetic and copies ran while one was open for 5% of the time, Pallas kernels for 0%

commit v1 on v0

v1 whole, which is shorter than its diff:
```python
import jax
import jax.numpy as jnp
from jax import lax
from jax.experimental import pallas as pl
from jax.experimental.pallas import tpu as pltpu
from jax.sharding import Mesh
from jax.sharding import PartitionSpec as P

UF_DEV = 512
VF_DEV = 1024
BLOCK = 128
DACT = 4
UACT = 2
KD = 288
KE = 144
TD = 16
TE = 8
RD = KD + TD
RE = KE + TE
DOWN = ("xl", "y")
UP = ("z", "xh", "c")
NY = 8
VMEM = pl.BlockSpec(memory_space=pltpu.VMEM)
SMEM = pl.BlockSpec(memory_space=pltpu.SMEM)
ANY = pl.BlockSpec(memory_space=pl.ANY)


def pack_kernel(down_ref, dec_ref, delta_ref, enc_ref, grad_ref, d_ref, e_ref, active, sems):
    def move(source, target):
        copy = pltpu.make_async_copy(source, target, sems.at[len(copies)])
        copies.append(copy)
        copy.start()

    copies = []
    for i in range(DACT):
        cols = pl.ds(pl.multiple_of(down_ref[i] * BLOCK, BLOCK), BLOCK)
        move(enc_ref.at[:, cols], active.at[:KE, i * BLOCK : (i + 1) * BLOCK])
        move(grad_ref.at[:, cols], active.at[KE:, i * BLOCK : (i + 1) * BLOCK])
    first = len(copies)
    move(dec_ref, d_ref.at[:KD])
    move(delta_ref, d_ref.at[KD:])
    for copy in copies[:first]:
        copy.wait()
    for n in range(e_ref.shape[0]):
        move(active, e_ref.at[n])
    for copy in copies[first:]:
        copy.wait()


def pack(down_blocks, dec_t, deltas, encoder, gradients, copies):
    cols = DACT * BLOCK
    return pl.pallas_call(
        pack_kernel,
        out_shape=(
            jax.ShapeDtypeStruct((RD, UF_DEV), jnp.bfloat16),
            jax.ShapeDtypeStruct((copies, RE, cols), jnp.bfloat16),
        ),
        in_specs=[SMEM, ANY, ANY, ANY, ANY],
        out_specs=(VMEM, ANY),
        scratch_shapes=[
            pltpu.VMEM((RE, cols), jnp.bfloat16),
            pltpu.SemaphoreType.DMA((2 * DACT + 2 + copies,)),
        ],
        compiler_params=pltpu.CompilerParams(vmem_limit_bytes=60 << 20),
    )(down_blocks, dec_t, deltas, encoder, gradients)


def score_kernel(pos_ref, up_ref, down_ref, *refs):
    shards = refs[: NY + 1]
    own, swapped, out_ref, dec, tok, enc, grad, sems = refs[NY + 1 :]
    y, core = pos_ref[0], pos_ref[1]
    copies = []

    def fetch(source, target):
        copies.append(pltpu.make_async_copy(source, target, sems.at[len(copies)]))
        copies[-1].start()

    for source, part in ((own, core), (swapped, 1 - core)):
        fetch(source.at[:, :KE], enc.at[:, part])
        fetch(source.at[:, KE:], grad.at[:, part])
    for shard, by in zip(shards, (0, -1, 1, -2, 2, -3, 3)):
        at = lax.rem(y + by + NY, NY)
        fetch(shard.at[:, :KD], dec.at[:, at])
        fetch(shard.at[:, KD:], tok.at[:, at])
    far = lax.rem(y + NY // 2, NY)
    for xl in range(2):
        fetch(shards[NY - 1 + xl].at[0, :KD], dec.at[xl, far])
        fetch(shards[NY - 1 + xl].at[0, KD:], tok.at[xl, far])
    out_ref[...] = jnp.zeros_like(out_ref)
    for copy in copies:
        copy.wait()
    lane_block = lax.broadcasted_iota(jnp.int32, (2 * TD, UF_DEV), 1) // BLOCK
    masked = []
    for w in range(NY):
        on = (lane_block == up_ref[w, 0]) | (lane_block == up_ref[w, 1])
        delta = tok[w // 4, 2 * (w % 4) : 2 * (w % 4) + 2].reshape(2 * TD, UF_DEV)
        masked.append(jnp.where(on, delta.astype(jnp.float32), 0.0))
    masked = jnp.concatenate(masked, 0).astype(jnp.bfloat16)
    kept = grad[...].astype(jnp.float32).reshape(NY * 2 * TD, DACT * BLOCK).astype(jnp.bfloat16)
    dims = (((0,), (0,)), ((), ()))
    product = lax.dot_general(masked, kept, dims, preferred_element_type=jnp.float32)
    virtual = None
    for xl in range(2):
        term = lax.dot_general(
            dec[xl].reshape(NY * KD, UF_DEV),
            enc[xl * NY : (xl + 1) * NY].reshape(NY * KD, DACT * BLOCK),
            dims,
            preferred_element_type=jnp.float32,
        )
        virtual = term if virtual is None else virtual + term
    scored = product * virtual
    for i in range(DACT):
        cols = pl.ds(pl.multiple_of(down_ref[i] * BLOCK, BLOCK), BLOCK)
        out_ref[:, cols] = scored[:, i * BLOCK : (i + 1) * BLOCK]


def score(pos, up_blocks, down_blocks, shards, own, swapped):
    cols = DACT * BLOCK
    return pl.pallas_call(
        score_kernel,
        out_shape=jax.ShapeDtypeStruct((UF_DEV, VF_DEV), jnp.float32),
        in_specs=[SMEM, SMEM, SMEM] + [ANY] * (NY + 3),
        out_specs=VMEM,
        scratch_shapes=[
            pltpu.VMEM((2, NY, KD, UF_DEV), jnp.bfloat16),
            pltpu.VMEM((2, NY, TD, UF_DEV), jnp.bfloat16),
            pltpu.VMEM((2 * NY, 2, KE, cols), jnp.bfloat16),
            pltpu.VMEM((2 * NY, 2, TE, cols), jnp.bfloat16),
            pltpu.SemaphoreType.DMA((4 + 2 * (NY + 1),)),
        ],
        compiler_params=pltpu.CompilerParams(vmem_limit_bytes=60 << 20),
    )(pos, up_blocks, down_blocks, *shards, own, swapped)


def turn(value, axis, by):
    n = lax.axis_size(axis)
    return lax.ppermute(value, axis, [(i, (i + by) % n) for i in range(n)])


def ring(pair):
    right = left = pair
    held = [pair]
    for _ in range(NY // 2 - 1):
        right, left = turn(right, "y", 1), turn(left, "y", -1)
        held += [right, left]
    return held + [turn(right[:1], "y", 1), turn(left[1:], "y", -1)]


def local(deltas, gradients, up_blocks, down_blocks, decoder, encoder):
    d, e = pack(down_blocks, decoder.T, deltas, encoder, gradients, 16)
    own = lax.all_to_all(e, ("z", "xh"), 0, 0, tiled=True)
    pair = lax.all_gather(d, "xl", axis=0)
    shards = ring(pair)
    own, shards[5], shards[6] = lax.optimization_barrier((own, shards[5], shards[6]))
    swapped = turn(own, "c", 1)
    pos = jnp.stack([lax.axis_index("y"), lax.axis_index("c")]).astype(jnp.int32)
    return score(pos, up_blocks, down_blocks, shards, own, swapped)


def solution(mesh):
    torus = Mesh(mesh.devices.reshape(8, 2, 2, 2, 8), ("z", "xh", "c", "xl", "y"))
    return jax.shard_map(
        local,
        mesh=torus,
        in_specs=(P(DOWN, UP), P(UP, DOWN), P(None, UP), P(DOWN), P(UP, DOWN), P(UP, DOWN)),
        out_specs=P(UP, DOWN),
        check_vma=False,
    )
```

time: 177 us -> 115 us (0.65)
  waiting for transfers between devices: 88.9 us -> 38.7 us
  starting transfers between devices: 10.7 us -> 46.8 us
  blocking collectives: 40.7 us -> 10.5 us
  local copies, waits for them, and re-layouts: 18.4 us -> 4.98 us
  between operations: 13.3 us -> 0.19 us
  Pallas kernels: 0 us -> 12.9 us
  matrix products: 2.9 us -> 0 us
    all_gather x3 -> x0, waiting for transfers between devices: 88.9 us -> none  [gather_in_order(): pieces = lax.all_gather(pieces, axes[k])]
    ppermute x0 -> x9, waiting for transfers between devices: none -> 38.7 us  [turn(): return lax.ppermute(value, axis, [(i, (i + by) % n) for i in range(n)])]
    ppermute x0 -> x9, starting transfers between devices: none -> 33.2 us  [turn(): return lax.ppermute(value, axis, [(i, (i + by) % n) for i in range(n)])]
    all_gather x4 -> x1, blocking collectives: 40.7 us -> 10.5 us  [local(): pair = lax.all_gather(d, 'xl', axis=0)]
    pallas_call x0 -> x2, Pallas kernels: none -> 12.9 us  [the longest x1 8.94 us: score(): pl.pallas_call(score_kernel, out_shape=jax.ShapeDtypeStruct((UF_DEV, VF_D...]
    transpose x2 -> x0, local copies, waits for them, and re-layouts: 7.77 us -> none  [gather_in_order(): pieces = pieces.transpose(*back, *range(len(axes), pieces.ndim))]
    slice x0 -> x2, local copies, waits for them, and re-layouts: none -> 3.41 us  [ring(): return held + [turn(right[:1], 'y', 1), turn(left[1:], 'y', -1)]]
    reshape x3 -> x0, local copies, waits for them, and re-layouts: 3.26 us -> none  [the longest x1 2.88 us: local(): return filled.reshape(UF_DEV, VF_DEV)]
  transfers between devices with their start and end apart: 4 -> 10, of which waited for: 3 -> 6; matrix products, arithmetic and copies ran while one was open for 5% -> 4% of each run, Pallas kernels for 0% -> 0%
where the time goes in v1:
time: 115 us
  starting transfers between devices  46.8 us (41%)
  waiting for transfers between devices  38.7 us (34%)
  Pallas kernels  12.9 us (11%)
  blocking collectives  10.5 us (9%)
  local copies, waits for them, and re-layouts  4.98 us (4%)
    ppermute x9, waiting for transfers between devices, turn(): return lax.ppermute(value, axis, [(i, (i + by) % n) for i in range(n)])  38.7 us
    ppermute x9, starting transfers between devices, turn(): return lax.ppermute(value, axis, [(i, (i + by) % n) for i in range(n)])  33.2 us
    all_to_all x1, starting transfers between devices, local(): own = lax.all_to_all(e, ('z', 'xh'), 0, 0, tiled=True)  13.6 us
    all_gather x1, blocking collectives, local(): pair = lax.all_gather(d, 'xl', axis=0)  10.5 us
    pallas_call x1, Pallas kernels, score(): pl.pallas_call(score_kernel, out_shape=jax.ShapeDtypeStruct((UF_DEV, VF_D...  8.94 us
    pallas_call x1, Pallas kernels, pack(): pl.pallas_call(pack_kernel, out_shape=(jax.ShapeDtypeStruct((RD, UF_DEV),...  3.96 us
    slice x2, local copies, waits for them, and re-layouts, ring(): return held + [turn(right[:1], 'y', 1), turn(left[1:], 'y', -1)]  3.41 us
  transfers between devices with their start and end apart: 10, of which 6 were waited for; matrix products, arithmetic and copies ran while one was open for 4% of the time, Pallas kernels for 0%

profile of v1, /device:TPU:1, one launch (start us, length us, event | category | flops | bytes accessed | tf_op | source)
XLA Modules:
  0.0 114.7 jit_solution(13949219780995174710)
XLA Ops:
  0.0 4.0 %shard_map.64 = (bf16[304,512]{1,0:T(8,128)(2,1)}, bf16[16,152,512]{2,1,0:T(8,128)(2,1)}) custom-call(s32[4]{0:T(128)} %down_ref.3, bf16[288,512]{1,0:T(8,128)(2,1)} %bitcast.7, bf16[16,512]{1,0:T(8,128)(2,1)} %delta_ref.1, bf16[144,1024]{1,0:T(8,128)(2,1)} %enc_ref.1, bf16[8,1024]{1,0:T(8,128)(2,1)} %grad_ref.1), custom_call_target="tpu_custom_call" | custom-call | tf_op jit(solution)/shard_map/pallas_call | solution.py:52
  4.0 0.0 copy-start.8
  4.0 0.0 copy-start.9
  4.0 13.6 %all-to-all-start = ((bf16[16,152,512]{2,1,0:T(8,128)(2,1)}), bf16[16,152,512]{2,1,0:T(8,128)(2,1)S(1)}, u32[]{:S(2)}, u32[]{:S(2)}) async-start(bf16[16,152,512]{2,1,0:T(8,128)(2,1)} %get-tuple-element.11), calls=%async_computation | async-start | bytes 4980736 | tf_op jit(solution)/shard_map/all_to_all | solution.py:151
  17.6 0.0 copy-done.8
  17.6 10.5 %all-gather = bf16[608,512]{1,0:T(8,128)(2,1)S(1)} all-gather(bf16[304,512]{1,0:T(8,128)(2,1)S(1)} %copy-done.8), channel_id=2, replica_groups=mesh['z'=8,'xh'=2,'c'=2,'xl'=2,'y'=8] {'xl'}, dimensions={0}, use_global_device_ids=true | all-gather | bytes 933888 | tf_op jit(solution)/shard_map/all_gather | solution.py:152
  28.1 0.0 copy-start.1
  28.1 5.1 %collective-permute-start.1 = (bf16[2,304,512]{2,1,0:T(8,128)(2,1)S(1)}, bf16[2,304,512]{2,1,0:T(8,128)(2,1)S(1)}, u32[]{:S(2)}, u32[]{:S(2)}) collective-permute-start(bf16[2,304,512]{2,1,0:T(8,128)(2,1)S(1)} %bitcast.4), channel_id=1, source_target_pairs={{0,7},{1,0},{2,1},{3,2},{4,3},{5,4},{6,5},{7,6},{8,15},{9,8},{10,9... | collective-permute-start | bytes 1867784 | tf_op jit(solution)/shard_map/ppermute | solution.py:137
  33.2 1.9 %collective-permute-start = (bf16[2,304,512]{2,1,0:T(8,128)(2,1)S(1)}, bf16[2,304,512]{2,1,0:T(8,128)(2,1)S(1)}, u32[]{:S(2)}, u32[]{:S(2)}) collective-permute-start(bf16[2,304,512]{2,1,0:T(8,128)(2,1)S(1)} %bitcast.5), channel_id=1, source_target_pairs={{0,1},{1,2},{2,3},{3,4},{4,5},{5,6},{6,7},{7,0},{8,9},{9,10},{10,1... | collective-permute-start | bytes 1867784 | tf_op jit(solution)/shard_map/ppermute | solution.py:137
  35.1 9.8 %collective-permute-done.1.refs_2_ = bf16[2,304,512]{2,1,0:T(8,128)(2,1)S(1)} collective-permute-done((bf16[2,304,512]{2,1,0:T(8,128)(2,1)S(1)}, bf16[2,304,512]{2,1,0:T(8,128)(2,1)S(1)}, u32[]{:S(2)}, u32[]{:S(2)}) %collective-permute-start.1) | collective-permute-done | bytes 622624 | tf_op jit(solution)/shard_map/ppermute | solution.py:137
  45.0 0.0 copy-start.3
  45.0 5.3 %collective-permute-start.3 = (bf16[2,304,512]{2,1,0:T(8,128)(2,1)S(1)}, bf16[2,304,512]{2,1,0:T(8,128)(2,1)S(1)}, u32[]{:S(2)}, u32[]{:S(2)}) collective-permute-start(bf16[2,304,512]{2,1,0:T(8,128)(2,1)S(1)} %collective-permute-done.1.refs_2_), channel_id=1, source_target_pairs={{0,7},{1,0},{2,1},{3,2},{4,3},{5,4},{6,5},{7,6},{8,15},{9,8},{10,9... | collective-permute-start | bytes 1867784 | tf_op jit(solution)/shard_map/ppermute | solution.py:137
  50.3 0.0 collective-permute-done.refs_1_
  50.3 0.0 copy-start.4
  50.3 1.9 %collective-permute-start.2 = (bf16[2,304,512]{2,1,0:T(8,128)(2,1)S(1)}, bf16[2,304,512]{2,1,0:T(8,128)(2,1)S(1)}, u32[]{:S(2)}, u32[]{:S(2)}) collective-permute-start(bf16[2,304,512]{2,1,0:T(8,128)(2,1)S(1)} %collective-permute-done.refs_1_), channel_id=1, source_target_pairs={{0,1},{1,2},{2,3},{3,4},{4,5},{5,6},{6,7},{7,0},{8,9},{9,10},{10,1... | collective-permute-start | bytes 1867784 | tf_op jit(solution)/shard_map/ppermute | solution.py:137
  52.2 0.0 copy-done.3
  52.2 8.9 %collective-permute-done.3.refs_4_ = bf16[2,304,512]{2,1,0:T(8,128)(2,1)S(1)} collective-permute-done((bf16[2,304,512]{2,1,0:T(8,128)(2,1)S(1)}, bf16[2,304,512]{2,1,0:T(8,128)(2,1)S(1)}, u32[]{:S(2)}, u32[]{:S(2)}) %collective-permute-start.3) | collective-permute-done | bytes 622624 | tf_op jit(solution)/shard_map/ppermute | solution.py:137
  61.1 0.0 copy-start.5
  61.1 5.3 %collective-permute-start.5 = (bf16[2,304,512]{2,1,0:T(8,128)(2,1)S(1)}, bf16[2,304,512]{2,1,0:T(8,128)(2,1)S(1)}, u32[]{:S(2)}, u32[]{:S(2)}) collective-permute-start(bf16[2,304,512]{2,1,0:T(8,128)(2,1)S(1)} %collective-permute-done.3.refs_4_), channel_id=1, source_target_pairs={{0,7},{1,0},{2,1},{3,2},{4,3},{5,4},{6,5},{7,6},{8,15},{9,8},{10,9... | collective-permute-start | bytes 1867784 | tf_op jit(solution)/shard_map/ppermute | solution.py:137
  66.4 0.0 collective-permute-done.2.refs_3_
  66.5 0.0 copy-start.6
  66.5 1.9 %collective-permute-start.4 = (bf16[2,304,512]{2,1,0:T(8,128)(2,1)S(1)}, bf16[2,304,512]{2,1,0:T(8,128)(2,1)}, u32[]{:S(2)}, u32[]{:S(2)}) collective-permute-start(bf16[2,304,512]{2,1,0:T(8,128)(2,1)S(1)} %collective-permute-done.2.refs_3_), channel_id=1, source_target_pairs={{0,1},{1,2},{2,3},{3,4},{4,5},{5,6},{6,7},{7,0},{8,9},{9,10},{10,1... | collective-permute-start | bytes 1867784 | tf_op jit(solution)/shard_map/ppermute | solution.py:137
  68.4 8.0 %collective-permute-done.5.refs_6_ = bf16[2,304,512]{2,1,0:T(8,128)(2,1)S(1)} collective-permute-done((bf16[2,304,512]{2,1,0:T(8,128)(2,1)S(1)}, bf16[2,304,512]{2,1,0:T(8,128)(2,1)S(1)}, u32[]{:S(2)}, u32[]{:S(2)}) %collective-permute-start.5) | collective-permute-done | bytes 622624 | tf_op jit(solution)/shard_map/ppermute | solution.py:137
  76.4 0.0 copy-done.4
  76.4 0.0 copy-done.5
  76.4 0.0 copy-done.6
  76.4 0.0 copy-start.2
  76.4 0.9 copy-done.2
  77.2 4.3 %collective-permute-done.4.refs_5_ = bf16[2,304,512]{2,1,0:T(8,128)(2,1)} collective-permute-done((bf16[2,304,512]{2,1,0:T(8,128)(2,1)S(1)}, bf16[2,304,512]{2,1,0:T(8,128)(2,1)}, u32[]{:S(2)}, u32[]{:S(2)}) %collective-permute-start.4) | collective-permute-done | bytes 622624 | tf_op jit(solution)/shard_map/ppermute | solution.py:137
  81.5 0.0 all-to-all-done.refs_9_
  81.5 0.0 copy-start
  81.5 6.5 %collective-permute-start.8 = (bf16[16,152,512]{2,1,0:T(8,128)(2,1)S(1)}, bf16[16,152,512]{2,1,0:T(8,128)(2,1)}, u32[]{:S(2)}, u32[]{:S(2)}) collective-permute-start(bf16[16,152,512]{2,1,0:T(8,128)(2,1)S(1)} %all-to-all-done.refs_9_), channel_id=1, source_target_pairs={{0,16},{16,0},{1,17},{17,1},{2,18},{18,2},{3,19},{19,3},{4,20},{20... | collective-permute-start | bytes 7471112 | tf_op jit(solution)/shard_map/ppermute | solution.py:137
  88.0 1.7 %slice.9 = bf16[1,304,512]{2,1,0:T(8,128)(2,1)} slice(bf16[2,304,512]{2,1,0:T(8,128)(2,1)} %copy-done.2), slice={[1:2], [0:304], [0:512]} | slice | bytes 622592 | tf_op jit(solution)/shard_map/slice | solution.py:146
  89.7 1.9 %collective-permute-start.7 = (bf16[1,304,512]{2,1,0:T(8,128)(2,1)}, bf16[1,304,512]{2,1,0:T(8,128)(2,1)S(1)}, u32[]{:S(2)}, u32[]{:S(2)}) collective-permute-start(bf16[1,304,512]{2,1,0:T(8,128)(2,1)} %slice.9), channel_id=1, source_target_pairs={{0,7},{1,0},{2,1},{3,2},{4,3},{5,4},{6,5},{7,6},{8,15},{9,8},{10,9... | collective-permute-start | bytes 933896 | tf_op jit(solution)/shard_map/ppermute | solution.py:137
  91.6 1.7 %slice.8 = bf16[1,304,512]{2,1,0:T(8,128)(2,1)} slice(bf16[2,304,512]{2,1,0:T(8,128)(2,1)} %collective-permute-done.4.refs_5_), slice={[0:1], [0:304], [0:512]} | slice | bytes 622592 | tf_op jit(solution)/shard_map/slice | solution.py:146
  93.4 3.4 %collective-permute-start.6 = (bf16[1,304,512]{2,1,0:T(8,128)(2,1)}, bf16[1,304,512]{2,1,0:T(8,128)(2,1)}, u32[]{:S(2)}, u32[]{:S(2)}) collective-permute-start(bf16[1,304,512]{2,1,0:T(8,128)(2,1)} %slice.8), channel_id=1, source_target_pairs={{0,1},{1,2},{2,3},{3,4},{4,5},{5,6},{6,7},{7,0},{8,9},{9,10},{10,1... | collective-permute-start | bytes 933896 | tf_op jit(solution)/shard_map/ppermute | solution.py:137
  96.7 0.0 copy-done.9
  96.7 0.7 copy.7.up_ref
  97.4 0.6 pad_add_fusion.pos_ref
  98.0 2.9 %collective-permute-done.7.refs_8_ = bf16[1,304,512]{2,1,0:T(8,128)(2,1)S(1)} collective-permute-done((bf16[1,304,512]{2,1,0:T(8,128)(2,1)}, bf16[1,304,512]{2,1,0:T(8,128)(2,1)S(1)}, u32[]{:S(2)}, u32[]{:S(2)}) %collective-permute-start.7) | collective-permute-done | bytes 311328 | tf_op jit(solution)/shard_map/ppermute | solution.py:137
  100.9 0.0 copy-start.7
  100.9 4.8 %collective-permute-done.6.refs_7_ = bf16[1,304,512]{2,1,0:T(8,128)(2,1)} collective-permute-done((bf16[1,304,512]{2,1,0:T(8,128)(2,1)}, bf16[1,304,512]{2,1,0:T(8,128)(2,1)}, u32[]{:S(2)}, u32[]{:S(2)}) %collective-permute-start.6) | collective-permute-done | bytes 311328 | tf_op jit(solution)/shard_map/ppermute | solution.py:137
  105.7 0.0 collective-permute-done.8.refs_10_
  105.7 0.0 copy-done.1
  105.7 0.0 copy-done
  105.8 0.0 copy-done.7
  105.8 8.9 %shard_map.65 = f32[512,1024]{1,0:T(8,128)} custom-call(s32[2]{0:T(128)} %pad_add_fusion.pos_ref, s32[8,2]{1,0:T(8,128)} %copy.7.up_ref, s32[4]{0:T(128)} %down_ref.3, bf16[2,304,512]{2,1,0:T(8,128)(2,1)} %bitcast.6, bf16[2,304,512]{2,1,0:T(8,128)(2,1)} %copy-done.4, bf16[2,304,512]{2,1,0:T(8,128)(2,1)} %copy-done.3, bf16[2,304,512]{2,1,0:T(8,128)(2,1)} %copy-done.6, ...), custom_call_target="tpu_custom_call" | custom-call | tf_op jit(solution)/shard_map/pallas_call | solution.py:119
Async XLA Ops:
  4.0 13.6 %copy-start.8 = (bf16[304,512]{1,0:T(8,128)(2,1)S(1)}, bf16[304,512]{1,0:T(8,128)(2,1)}, u32[]{:S(2)}) copy-start(bf16[304,512]{1,0:T(8,128)(2,1)} %get-tuple-element.10) | copy-start | bytes 933892
  4.0 92.7 %copy-start.9 = (s32[8,2]{0,1:T(2,128)S(1)}, s32[8,2]{0,1:T(2,128)}, u32[]{:S(2)}) copy-start(s32[8,2]{0,1:T(2,128)} %param.8) | copy-start | bytes 196
  4.0 77.5 %all-to-all-start = ((bf16[16,152,512]{2,1,0:T(8,128)(2,1)}), bf16[16,152,512]{2,1,0:T(8,128)(2,1)S(1)}, u32[]{:S(2)}, u32[]{:S(2)}) async-start(bf16[16,152,512]{2,1,0:T(8,128)(2,1)} %get-tuple-element.11), calls=%async_computation | async-start | bytes 4980736 | tf_op jit(solution)/shard_map/all_to_all | solution.py:151
  28.1 77.6 %copy-start.1 = (bf16[608,512]{1,0:T(8,128)(2,1)}, bf16[608,512]{1,0:T(8,128)(2,1)S(1)}, u32[]{:S(2)}) copy-start(bf16[608,512]{1,0:T(8,128)(2,1)S(1)} %all-gather) | copy-start | bytes 1867780
  28.1 16.8 %collective-permute-start.1 = (bf16[2,304,512]{2,1,0:T(8,128)(2,1)S(1)}, bf16[2,304,512]{2,1,0:T(8,128)(2,1)S(1)}, u32[]{:S(2)}, u32[]{:S(2)}) collective-permute-start(bf16[2,304,512]{2,1,0:T(8,128)(2,1)S(1)} %bitcast.4), channel_id=1, source_target_pairs={{0,7},{1,0},{2,1},{3,2},{4,3},{5,4},{6,5},{7,6},{8,15},{9,8},{10,9... | collective-permute-start | bytes 1867784 | tf_op jit(solution)/shard_map/ppermute | solution.py:137
  33.2 17.1 %collective-permute-start = (bf16[2,304,512]{2,1,0:T(8,128)(2,1)S(1)}, bf16[2,304,512]{2,1,0:T(8,128)(2,1)S(1)}, u32[]{:S(2)}, u32[]{:S(2)}) collective-permute-start(bf16[2,304,512]{2,1,0:T(8,128)(2,1)S(1)} %bitcast.5), channel_id=1, source_target_pairs={{0,1},{1,2},{2,3},{3,4},{4,5},{5,6},{6,7},{7,0},{8,9},{9,10},{10,1... | collective-permute-start | bytes 1867784 | tf_op jit(solution)/shard_map/ppermute | solution.py:137
  45.0 7.3 %copy-start.3 = (bf16[2,304,512]{2,1,0:T(8,128)(2,1)}, bf16[2,304,512]{2,1,0:T(8,128)(2,1)S(1)}, u32[]{:S(2)}) copy-start(bf16[2,304,512]{2,1,0:T(8,128)(2,1)S(1)} %collective-permute-done.1.refs_2_) | copy-start | bytes 1867780
  45.0 16.1 %collective-permute-start.3 = (bf16[2,304,512]{2,1,0:T(8,128)(2,1)S(1)}, bf16[2,304,512]{2,1,0:T(8,128)(2,1)S(1)}, u32[]{:S(2)}, u32[]{:S(2)}) collective-permute-start(bf16[2,304,512]{2,1,0:T(8,128)(2,1)S(1)} %collective-permute-done.1.refs_2_), channel_id=1, source_target_pairs={{0,7},{1,0},{2,1},{3,2},{4,3},{5,4},{6,5},{7,6},{8,15},{9,8},{10,9... | collective-permute-start | bytes 1867784 | tf_op jit(solution)/shard_map/ppermute | solution.py:137
  50.3 26.1 %copy-start.4 = (bf16[2,304,512]{2,1,0:T(8,128)(2,1)}, bf16[2,304,512]{2,1,0:T(8,128)(2,1)S(1)}, u32[]{:S(2)}) copy-start(bf16[2,304,512]{2,1,0:T(8,128)(2,1)S(1)} %collective-permute-done.refs_1_) | copy-start | bytes 1867780
  50.3 16.1 %collective-permute-start.2 = (bf16[2,304,512]{2,1,0:T(8,128)(2,1)S(1)}, bf16[2,304,512]{2,1,0:T(8,128)(2,1)S(1)}, u32[]{:S(2)}, u32[]{:S(2)}) collective-permute-start(bf16[2,304,512]{2,1,0:T(8,128)(2,1)S(1)} %collective-permute-done.refs_1_), channel_id=1, source_target_pairs={{0,1},{1,2},{2,3},{3,4},{4,5},{5,6},{6,7},{7,0},{8,9},{9,10},{10,1... | collective-permute-start | bytes 1867784 | tf_op jit(solution)/shard_map/ppermute | solution.py:137
  61.1 15.2 %copy-start.5 = (bf16[2,304,512]{2,1,0:T(8,128)(2,1)}, bf16[2,304,512]{2,1,0:T(8,128)(2,1)S(1)}, u32[]{:S(2)}) copy-start(bf16[2,304,512]{2,1,0:T(8,128)(2,1)S(1)} %collective-permute-done.3.refs_4_) | copy-start | bytes 1867780
  61.1 15.2 %collective-permute-start.5 = (bf16[2,304,512]{2,1,0:T(8,128)(2,1)S(1)}, bf16[2,304,512]{2,1,0:T(8,128)(2,1)S(1)}, u32[]{:S(2)}, u32[]{:S(2)}) collective-permute-start(bf16[2,304,512]{2,1,0:T(8,128)(2,1)S(1)} %collective-permute-done.3.refs_4_), channel_id=1, source_target_pairs={{0,7},{1,0},{2,1},{3,2},{4,3},{5,4},{6,5},{7,6},{8,15},{9,8},{10,9... | collective-permute-start | bytes 1867784 | tf_op jit(solution)/shard_map/ppermute | solution.py:137
  66.5 9.9 %copy-start.6 = (bf16[2,304,512]{2,1,0:T(8,128)(2,1)}, bf16[2,304,512]{2,1,0:T(8,128)(2,1)S(1)}, u32[]{:S(2)}) copy-start(bf16[2,304,512]{2,1,0:T(8,128)(2,1)S(1)} %collective-permute-done.2.refs_3_) | copy-start | bytes 1867780
  66.5 15.1 %collective-permute-start.4 = (bf16[2,304,512]{2,1,0:T(8,128)(2,1)S(1)}, bf16[2,304,512]{2,1,0:T(8,128)(2,1)}, u32[]{:S(2)}, u32[]{:S(2)}) collective-permute-start(bf16[2,304,512]{2,1,0:T(8,128)(2,1)S(1)} %collective-permute-done.2.refs_3_), channel_id=1, source_target_pairs={{0,1},{1,2},{2,3},{3,4},{4,5},{5,6},{6,7},{7,0},{8,9},{9,10},{10,1... | collective-permute-start | bytes 1867784 | tf_op jit(solution)/shard_map/ppermute | solution.py:137
  76.4 0.9 copy-start.2
  81.5 24.2 %copy-start = (bf16[16,152,512]{2,1,0:T(8,128)(2,1)}, bf16[16,152,512]{2,1,0:T(8,128)(2,1)S(1)}, u32[]{:S(2)}) copy-start(bf16[16,152,512]{2,1,0:T(8,128)(2,1)S(1)} %all-to-all-done.refs_9_) | copy-start | bytes 7471108
  81.5 24.2 %collective-permute-start.8 = (bf16[16,152,512]{2,1,0:T(8,128)(2,1)S(1)}, bf16[16,152,512]{2,1,0:T(8,128)(2,1)}, u32[]{:S(2)}, u32[]{:S(2)}) collective-permute-start(bf16[16,152,512]{2,1,0:T(8,128)(2,1)S(1)} %all-to-all-done.refs_9_), channel_id=1, source_target_pairs={{0,16},{16,0},{1,17},{17,1},{2,18},{18,2},{3,19},{19,3},{4,20},{20... | collective-permute-start | bytes 7471112 | tf_op jit(solution)/shard_map/ppermute | solution.py:137
  89.7 11.2 %collective-permute-start.7 = (bf16[1,304,512]{2,1,0:T(8,128)(2,1)}, bf16[1,304,512]{2,1,0:T(8,128)(2,1)S(1)}, u32[]{:S(2)}, u32[]{:S(2)}) collective-permute-start(bf16[1,304,512]{2,1,0:T(8,128)(2,1)} %slice.9), channel_id=1, source_target_pairs={{0,7},{1,0},{2,1},{3,2},{4,3},{5,4},{6,5},{7,6},{8,15},{9,8},{10,9... | collective-permute-start | bytes 933896 | tf_op jit(solution)/shard_map/ppermute | solution.py:137
  93.4 12.4 %collective-permute-start.6 = (bf16[1,304,512]{2,1,0:T(8,128)(2,1)}, bf16[1,304,512]{2,1,0:T(8,128)(2,1)}, u32[]{:S(2)}, u32[]{:S(2)}) collective-permute-start(bf16[1,304,512]{2,1,0:T(8,128)(2,1)} %slice.8), channel_id=1, source_target_pairs={{0,1},{1,2},{2,3},{3,4},{4,5},{5,6},{6,7},{7,0},{8,9},{9,10},{10,1... | collective-permute-start | bytes 933896 | tf_op jit(solution)/shard_map/ppermute | solution.py:137
  100.9 4.8 %copy-start.7 = (bf16[1,304,512]{2,1,0:T(8,128)(2,1)}, bf16[1,304,512]{2,1,0:T(8,128)(2,1)S(1)}, u32[]{:S(2)}) copy-start(bf16[1,304,512]{2,1,0:T(8,128)(2,1)S(1)} %collective-permute-done.7.refs_8_) | copy-start | bytes 933892

commit v2 on v1

v2 whole, which is shorter than its diff:
```python
import jax
import jax.numpy as jnp
from jax import lax
from jax.experimental import pallas as pl
from jax.experimental.pallas import tpu as pltpu
from jax.sharding import Mesh
from jax.sharding import PartitionSpec as P

UF_DEV = 512
VF_DEV = 1024
BLOCK = 128
DACT = 4
UACT = 2
KD = 288
KE = 144
TD = 16
TE = 8
RD = KD + TD
RE = KE + TE
DOWN = ("xl", "y")
UP = ("z", "xh", "c")
NY = 8
TURNS = (0, -1, 1, -2, 2, -3, 3, 4)
STEP = 4
VMEM = pl.BlockSpec(memory_space=pltpu.VMEM)
SMEM = pl.BlockSpec(memory_space=pltpu.SMEM)
ANY = pl.BlockSpec(memory_space=pl.ANY)


def pack_kernel(down_ref, dec_ref, delta_ref, enc_ref, grad_ref, d_ref, e_ref, sems):
    copies = []

    def move(source, target):
        copies.append(pltpu.make_async_copy(source, target, sems.at[len(copies)]))
        copies[-1].start()

    for i in range(DACT):
        cols = pl.ds(pl.multiple_of(down_ref[i] * BLOCK, BLOCK), BLOCK)
        move(enc_ref.at[:, cols], e_ref.at[:KE, i * BLOCK : (i + 1) * BLOCK])
        move(grad_ref.at[:, cols], e_ref.at[KE:, i * BLOCK : (i + 1) * BLOCK])
    move(dec_ref, d_ref.at[:KD])
    move(delta_ref, d_ref.at[KD:])
    for copy in copies:
        copy.wait()


def pack(down_blocks, dec_t, deltas, encoder, gradients):
    return pl.pallas_call(
        pack_kernel,
        out_shape=(
            jax.ShapeDtypeStruct((RD, UF_DEV), jnp.bfloat16),
            jax.ShapeDtypeStruct((RE, DACT * BLOCK), jnp.bfloat16),
        ),
        in_specs=[SMEM, ANY, ANY, ANY, ANY],
        out_specs=(VMEM, VMEM),
        scratch_shapes=[pltpu.SemaphoreType.DMA((2 * DACT + 2,))],
        compiler_params=pltpu.CompilerParams(vmem_limit_bytes=60 << 20),
    )(down_blocks, dec_t, deltas, encoder, gradients)


def score_kernel(up_ref, down_ref, *refs):
    shards = refs[: 2 * NY]
    own, swapped, out_ref, dec, tok, enc, grad, dec_sem, tok_sem, enc_sem, grad_sem = refs[2 * NY :]
    y, xl, core = lax.axis_index("y"), lax.axis_index("xl"), lax.axis_index("c")
    grads = []
    for source, part in ((own, core), (swapped, 1 - core)):
        grads.append(
            pltpu.make_async_copy(
                source.at[:, KE:], grad.at[:, part], grad_sem.at[len(grads)]
            )
        )
        grads[-1].start()
    blocks, tokens = [], []
    for slot in range(2 * NY):
        turned, column = TURNS[slot // 2], xl if slot % 2 == 0 else 1 - xl
        k = column * NY + lax.rem(y + turned + NY, NY)
        mine = [
            pltpu.make_async_copy(
                source.at[k, :KE], enc.at[slot, part], enc_sem.at[slot, i]
            )
            for i, (source, part) in enumerate(((own, core), (swapped, 1 - core)))
        ]
        mine.append(
            pltpu.make_async_copy(shards[slot].at[:KD], dec.at[slot], dec_sem.at[slot])
        )
        tokens.append(
            pltpu.make_async_copy(shards[slot].at[KD:], tok.at[k], tok_sem.at[slot])
        )
        for copy in mine + tokens[-1:]:
            copy.start()
        blocks.append(mine)
    out_ref[...] = jnp.zeros_like(out_ref)
    dims = (((0,), (0,)), ((), ()))
    virtual = None
    for first in range(0, 2 * NY, STEP):
        for slot in range(first, first + STEP):
            for copy in blocks[slot]:
                copy.wait()
        term = lax.dot_general(
            dec[first : first + STEP].reshape(STEP * KD, UF_DEV),
            enc[first : first + STEP].reshape(STEP * KD, DACT * BLOCK),
            dims,
            preferred_element_type=jnp.float32,
        )
        virtual = term if virtual is None else virtual + term
    for copy in grads + tokens:
        copy.wait()
    lane_block = lax.broadcasted_iota(jnp.int32, (2 * TD, UF_DEV), 1) // BLOCK
    masked = []
    for w in range(NY):
        on = (lane_block == up_ref[0, w]) | (lane_block == up_ref[1, w])
        delta = tok[2 * w : 2 * w + 2].reshape(2 * TD, UF_DEV)
        masked.append(jnp.where(on, delta.astype(jnp.float32), 0.0))
    masked = jnp.concatenate(masked, 0).astype(jnp.bfloat16)
    kept = grad[...].astype(jnp.float32).reshape(NY * 2 * TD, DACT * BLOCK).astype(jnp.bfloat16)
    product = lax.dot_general(masked, kept, dims, preferred_element_type=jnp.float32)
    scored = product * virtual
    for i in range(DACT):
        cols = pl.ds(pl.multiple_of(down_ref[i] * BLOCK, BLOCK), BLOCK)
        out_ref[:, cols] = scored[:, i * BLOCK : (i + 1) * BLOCK]


def score(up_blocks, down_blocks, shards, own, swapped):
    cols = DACT * BLOCK
    return pl.pallas_call(
        score_kernel,
        out_shape=jax.ShapeDtypeStruct((UF_DEV, VF_DEV), jnp.float32),
        in_specs=[SMEM, SMEM] + [ANY] * (2 * NY + 2),
        out_specs=VMEM,
        scratch_shapes=[
            pltpu.VMEM((2 * NY, KD, UF_DEV), jnp.bfloat16),
            pltpu.VMEM((2 * NY, TD, UF_DEV), jnp.bfloat16),
            pltpu.VMEM((2 * NY, 2, KE, cols), jnp.bfloat16),
            pltpu.VMEM((2 * NY, 2, TE, cols), jnp.bfloat16),
            pltpu.SemaphoreType.DMA((2 * NY,)),
            pltpu.SemaphoreType.DMA((2 * NY,)),
            pltpu.SemaphoreType.DMA((2 * NY, 2)),
            pltpu.SemaphoreType.DMA((2,)),
        ],
        compiler_params=pltpu.CompilerParams(vmem_limit_bytes=60 << 20),
    )(up_blocks.T, down_blocks, *shards, own, swapped)


def turn(value, axis, by):
    n = lax.axis_size(axis)
    return lax.ppermute(value, axis, [(i, (i + by) % n) for i in range(n)])


def ring(value, last):
    right = left = value
    held = [value]
    for _ in range(NY // 2 - 1):
        right, left = turn(right, "y", 1), turn(left, "y", -1)
        held += [right, left]
    return held + [turn(right if last > 0 else left, "y", last)]


def local(deltas, gradients, up_blocks, down_blocks, decoder, encoder):
    d, e = pack(down_blocks, decoder.T, deltas, encoder, gradients)
    pair = lax.all_gather(e, "xh")
    own = lax.all_to_all(jnp.broadcast_to(pair[None], (NY, *pair.shape)), "z", 0, 0, tiled=True)
    near = ring(d, 1)
    across = ring(turn(d, "xl", 1), -1)
    own, near[5:], across[5:7] = lax.optimization_barrier((own, near[5:], across[5:7]))
    shards = [shard for both in zip(near, across) for shard in both]
    swapped = turn(own, "c", 1)
    own, swapped = (v.reshape(2 * NY, RE, DACT * BLOCK) for v in (own, swapped))
    return score(up_blocks, down_blocks, shards, own, swapped)


def solution(mesh):
    torus = Mesh(mesh.devices.reshape(8, 2, 2, 2, 8), ("z", "xh", "c", "xl", "y"))
    return jax.shard_map(
        local,
        mesh=torus,
        in_specs=(P(DOWN, UP), P(UP, DOWN), P(None, UP), P(DOWN), P(UP, DOWN), P(UP, DOWN)),
        out_specs=P(UP, DOWN),
        check_vma=False,
    )
```

time: 115 us -> 109 us (0.948)
  waiting for transfers between devices: 38.7 us -> 21.6 us
  starting transfers between devices: 46.8 us -> 63.2 us
  blocking collectives: 10.5 us -> 7.12 us
  Pallas kernels: 12.9 us -> 11.6 us
    ppermute x9 -> x16, waiting for transfers between devices: 38.7 us -> 16.2 us  [turn(): return lax.ppermute(value, axis, [(i, (i + by) % n) for i in range(n)])]
    ppermute x9 -> x16, starting transfers between devices: 33.2 us -> 52 us  [turn(): return lax.ppermute(value, axis, [(i, (i + by) % n) for i in range(n)])]
    all_to_all x1, waiting for transfers between devices: 0.01 us -> 5.35 us  [local(): lax.all_to_all(jnp.broadcast_to(pair[None], (NY, *pair.shape)), 'z', 0, 0...]
    all_gather x1, blocking collectives: 10.5 us -> 7.12 us  [local(): pair = lax.all_gather(e, 'xh')]
    slice x2 -> x0, local copies, waits for them, and re-layouts: 3.41 us -> none  [ring(): return held + [turn(right[:1], 'y', 1), turn(left[1:], 'y', -1)]]
    all_to_all x1, starting transfers between devices: 13.6 us -> 11.2 us  [local(): lax.all_to_all(jnp.broadcast_to(pair[None], (NY, *pair.shape)), 'z', 0, 0...]
    broadcast_in_dim x0 -> x1, local copies, waits for them, and re-layouts: none -> 1.71 us  [local(): jnp.broadcast_to(pair[None], (NY, *pair.shape))]
    pallas_call x1, Pallas kernels: 3.96 us -> 2.64 us  [pack(): pl.pallas_call(pack_kernel, out_shape=(jax.ShapeDtypeStruct((RD, UF_DEV),...]
  transfers between devices with their start and end apart: 10 -> 17, of which waited for: 6 -> 6; matrix products, arithmetic and copies ran while one was open for 4% -> 0% of each run, Pallas kernels for 0% -> 0%
where the time goes in v2:
time: 109 us; the launch traced here: 108 us
  starting transfers between devices  63.2 us (58%)
  waiting for transfers between devices  21.6 us (20%)
  Pallas kernels  11.6 us (11%)
  blocking collectives  7.12 us (7%)
  local copies, waits for them, and re-layouts  4.04 us (4%)
    ppermute x16, starting transfers between devices, turn(): return lax.ppermute(value, axis, [(i, (i + by) % n) for i in range(n)])  52 us
    ppermute x16, waiting for transfers between devices, turn(): return lax.ppermute(value, axis, [(i, (i + by) % n) for i in range(n)])  16.2 us
    all_to_all x1, starting transfers between devices, local(): lax.all_to_all(jnp.broadcast_to(pair[None], (NY, *pair.shape)), 'z', 0, 0...  11.2 us
    pallas_call x1, Pallas kernels, score(): pl.pallas_call(score_kernel, out_shape=jax.ShapeDtypeStruct((UF_DEV, VF_D...  8.94 us
    all_gather x1, blocking collectives, local(): pair = lax.all_gather(e, 'xh')  7.12 us
    all_to_all x1, waiting for transfers between devices, local(): lax.all_to_all(jnp.broadcast_to(pair[None], (NY, *pair.shape)), 'z', 0, 0...  5.35 us
    pallas_call x1, Pallas kernels, pack(): pl.pallas_call(pack_kernel, out_shape=(jax.ShapeDtypeStruct((RD, UF_DEV),...  2.64 us
    unnamed x34, local copies, waits for them, and re-layouts  2.33 us
  transfers between devices with their start and end apart: 17, of which 6 were waited for; matrix products, arithmetic and copies ran while one was open for 0% of the time, Pallas kernels for 0%

profile of v2, /device:TPU:1, one launch (start us, length us, event | category | flops | bytes accessed | tf_op | source)
XLA Modules:
  0.0 107.9 jit_solution(16544183592403070397)
XLA Ops:
  0.0 2.6 %shard_map.64 = (bf16[304,512]{1,0:T(8,128)(2,1)}, bf16[152,512]{1,0:T(8,128)(2,1)}) custom-call(s32[4]{0:T(128)} %down_ref.3, bf16[288,512]{1,0:T(8,128)(2,1)} %bitcast.8, bf16[16,512]{1,0:T(8,128)(2,1)} %delta_ref.1, bf16[144,1024]{1,0:T(8,128)(2,1)} %enc_ref.1, bf16[8,1024]{1,0:T(8,128)(2,1)} %grad_ref.1), custom_call_target="tpu_custom_call" | custom-call | tf_op jit(solution)/shard_map/pallas_call | solution.py:48
  2.6 7.1 %all-gather = bf16[304,512]{1,0:T(8,128)(2,1)S(1)} all-gather(bf16[152,512]{1,0:T(8,128)(2,1)} %get-tuple-element.14), channel_id=2, replica_groups=mesh['z'=8,'xh'=2,'c'=2,'xl'=2,'y'=8] {'xh'}, dimensions={0}, use_global_device_ids=true | all-gather | bytes 466944 | tf_op jit(solution)/shard_map/all_gather | solution.py:160
  9.8 1.7 %broadcast_in_dim.2 = bf16[8,2,152,512]{3,2,1,0:T(8,128)(2,1)} broadcast(bf16[2,152,512]{2,1,0:T(8,128)(2,1)S(1)} %bitcast.7), dimensions={1,2,3} | broadcast | bytes 2801664 | tf_op jit(solution)/shard_map/broadcast_in_dim | solution.py:161
  11.5 11.2 %all-to-all-start = ((bf16[8,2,152,512]{3,2,1,0:T(8,128)(2,1)}), bf16[8,2,152,512]{3,2,1,0:T(8,128)(2,1)S(1)}, u32[]{:S(2)}, u32[]{:S(2)}) async-start(bf16[8,2,152,512]{3,2,1,0:T(8,128)(2,1)} %broadcast_in_dim.2), calls=%async_computation | async-start | bytes 4980736 | tf_op jit(solution)/shard_map/all_to_all | solution.py:161
  22.6 0.0 copy-done.2
  22.6 3.2 %collective-permute-start.1 = (bf16[304,512]{1,0:T(8,128)(2,1)S(1)}, bf16[304,512]{1,0:T(8,128)(2,1)S(1)}, u32[]{:S(2)}, u32[]{:S(2)}) collective-permute-start(bf16[304,512]{1,0:T(8,128)(2,1)S(1)} %copy-done.2), channel_id=1, source_target_pairs={{0,1},{1,2},{2,3},{3,4},{4,5},{5,6},{6,7},{7,0},{8,9},{9,10},{10,1... | collective-permute-start | bytes 933896 | tf_op jit(solution)/shard_map/ppermute | solution.py:146
  25.9 3.1 %collective-permute-start = (bf16[304,512]{1,0:T(8,128)(2,1)S(1)}, bf16[304,512]{1,0:T(8,128)(2,1)S(1)}, u32[]{:S(2)}, u32[]{:S(2)}) collective-permute-start(bf16[304,512]{1,0:T(8,128)(2,1)S(1)} %copy-done.2), channel_id=1, source_target_pairs={{0,8},{8,0},{1,9},{9,1},{2,10},{10,2},{3,11},{11,3},{4,12},{12,4},... | collective-permute-start | bytes 933896 | tf_op jit(solution)/shard_map/ppermute | solution.py:146
  29.0 3.8 %collective-permute-start.3 = (bf16[304,512]{1,0:T(8,128)(2,1)S(1)}, bf16[304,512]{1,0:T(8,128)(2,1)S(1)}, u32[]{:S(2)}, u32[]{:S(2)}) collective-permute-start(bf16[304,512]{1,0:T(8,128)(2,1)S(1)} %copy-done.2), channel_id=1, source_target_pairs={{0,7},{1,0},{2,1},{3,2},{4,3},{5,4},{6,5},{7,6},{8,15},{9,8},{10,9... | collective-permute-start | bytes 933896 | tf_op jit(solution)/shard_map/ppermute | solution.py:146
  32.8 0.8 collective-permute-done.1.refs_2_
  33.6 1.9 %collective-permute-start.5 = (bf16[304,512]{1,0:T(8,128)(2,1)S(1)}, bf16[304,512]{1,0:T(8,128)(2,1)S(1)}, u32[]{:S(2)}, u32[]{:S(2)}) collective-permute-start(bf16[304,512]{1,0:T(8,128)(2,1)S(1)} %collective-permute-done.1.refs_2_), channel_id=1, source_target_pairs={{0,1},{1,2},{2,3},{3,4},{4,5},{5,6},{6,7},{7,0},{8,9},{9,10},{10,1... | collective-permute-start | bytes 933896 | tf_op jit(solution)/shard_map/ppermute | solution.py:146
  35.5 0.0 collective-permute-done.refs_1_
  35.5 0.0 copy-start.4
  35.5 4.6 %collective-permute-start.4 = (bf16[304,512]{1,0:T(8,128)(2,1)S(1)}, bf16[304,512]{1,0:T(8,128)(2,1)S(1)}, u32[]{:S(2)}, u32[]{:S(2)}) collective-permute-start(bf16[304,512]{1,0:T(8,128)(2,1)S(1)} %collective-permute-done.refs_1_), channel_id=1, source_target_pairs={{0,7},{1,0},{2,1},{3,2},{4,3},{5,4},{6,5},{7,6},{8,15},{9,8},{10,9... | collective-permute-start | bytes 933896 | tf_op jit(solution)/shard_map/ppermute | solution.py:146
  40.1 1.9 %collective-permute-start.2 = (bf16[304,512]{1,0:T(8,128)(2,1)S(1)}, bf16[304,512]{1,0:T(8,128)(2,1)S(1)}, u32[]{:S(2)}, u32[]{:S(2)}) collective-permute-start(bf16[304,512]{1,0:T(8,128)(2,1)S(1)} %collective-permute-done.refs_1_), channel_id=1, source_target_pairs={{0,1},{1,2},{2,3},{3,4},{4,5},{5,6},{6,7},{7,0},{8,9},{9,10},{10,1... | collective-permute-start | bytes 933896 | tf_op jit(solution)/shard_map/ppermute | solution.py:146
  42.0 0.0 collective-permute-done.3.refs_4_
  42.0 0.0 copy-start.5
  42.1 4.6 %collective-permute-start.7 = (bf16[304,512]{1,0:T(8,128)(2,1)S(1)}, bf16[304,512]{1,0:T(8,128)(2,1)S(1)}, u32[]{:S(2)}, u32[]{:S(2)}) collective-permute-start(bf16[304,512]{1,0:T(8,128)(2,1)S(1)} %collective-permute-done.3.refs_4_), channel_id=1, source_target_pairs={{0,7},{1,0},{2,1},{3,2},{4,3},{5,4},{6,5},{7,6},{8,15},{9,8},{10,9... | collective-permute-start | bytes 933896 | tf_op jit(solution)/shard_map/ppermute | solution.py:146
  46.6 0.0 collective-permute-done.5.refs_6_
  46.6 0.0 copy-start.6
  46.7 1.9 %collective-permute-start.9 = (bf16[304,512]{1,0:T(8,128)(2,1)S(1)}, bf16[304,512]{1,0:T(8,128)(2,1)S(1)}, u32[]{:S(2)}, u32[]{:S(2)}) collective-permute-start(bf16[304,512]{1,0:T(8,128)(2,1)S(1)} %collective-permute-done.5.refs_6_), channel_id=1, source_target_pairs={{0,1},{1,2},{2,3},{3,4},{4,5},{5,6},{6,7},{7,0},{8,9},{9,10},{10,1... | collective-permute-start | bytes 933896 | tf_op jit(solution)/shard_map/ppermute | solution.py:146
  48.6 0.0 collective-permute-done.4.refs_5_
  48.6 0.0 copy-start.7
  48.6 4.6 %collective-permute-start.8 = (bf16[304,512]{1,0:T(8,128)(2,1)S(1)}, bf16[304,512]{1,0:T(8,128)(2,1)S(1)}, u32[]{:S(2)}, u32[]{:S(2)}) collective-permute-start(bf16[304,512]{1,0:T(8,128)(2,1)S(1)} %collective-permute-done.4.refs_5_), channel_id=1, source_target_pairs={{0,7},{1,0},{2,1},{3,2},{4,3},{5,4},{6,5},{7,6},{8,15},{9,8},{10,9... | collective-permute-start | bytes 933896 | tf_op jit(solution)/shard_map/ppermute | solution.py:146
  53.2 0.0 collective-permute-done.2.refs_3_
  53.2 0.0 copy-start.8
  53.2 1.9 %collective-permute-start.6 = (bf16[304,512]{1,0:T(8,128)(2,1)S(1)}, bf16[304,512]{1,0:T(8,128)(2,1)S(1)}, u32[]{:S(2)}, u32[]{:S(2)}) collective-permute-start(bf16[304,512]{1,0:T(8,128)(2,1)S(1)} %collective-permute-done.2.refs_3_), channel_id=1, source_target_pairs={{0,1},{1,2},{2,3},{3,4},{4,5},{5,6},{6,7},{7,0},{8,9},{9,10},{10,1... | collective-permute-start | bytes 933896 | tf_op jit(solution)/shard_map/ppermute | solution.py:146
  55.1 0.0 collective-permute-done.7.refs_8_
  55.1 0.0 copy-start.9
  55.2 4.6 %collective-permute-start.10 = (bf16[304,512]{1,0:T(8,128)(2,1)S(1)}, bf16[304,512]{1,0:T(8,128)(2,1)S(1)}, u32[]{:S(2)}, u32[]{:S(2)}) collective-permute-start(bf16[304,512]{1,0:T(8,128)(2,1)S(1)} %collective-permute-done.7.refs_8_), channel_id=1, source_target_pairs={{0,7},{1,0},{2,1},{3,2},{4,3},{5,4},{6,5},{7,6},{8,15},{9,8},{10,9... | collective-permute-start | bytes 933896 | tf_op jit(solution)/shard_map/ppermute | solution.py:146
  59.7 0.0 collective-permute-done.9.refs_10_
  59.7 0.0 copy-start.10
  59.8 1.9 %collective-permute-start.11 = (bf16[304,512]{1,0:T(8,128)(2,1)S(1)}, bf16[304,512]{1,0:T(8,128)(2,1)S(1)}, u32[]{:S(2)}, u32[]{:S(2)}) collective-permute-start(bf16[304,512]{1,0:T(8,128)(2,1)S(1)} %collective-permute-done.9.refs_10_), channel_id=1, source_target_pairs={{0,1},{1,2},{2,3},{3,4},{4,5},{5,6},{6,7},{7,0},{8,9},{9,10},{10,1... | collective-permute-start | bytes 933896 | tf_op jit(solution)/shard_map/ppermute | solution.py:146
  61.7 0.0 collective-permute-done.8.refs_9_
  61.7 0.0 copy-start.11
  61.7 4.6 %collective-permute-start.13 = (bf16[304,512]{1,0:T(8,128)(2,1)S(1)}, bf16[304,512]{1,0:T(8,128)(2,1)S(1)}, u32[]{:S(2)}, u32[]{:S(2)}) collective-permute-start(bf16[304,512]{1,0:T(8,128)(2,1)S(1)} %collective-permute-done.8.refs_9_), channel_id=1, source_target_pairs={{0,7},{1,0},{2,1},{3,2},{4,3},{5,4},{6,5},{7,6},{8,15},{9,8},{10,9... | collective-permute-start | bytes 933896 | tf_op jit(solution)/shard_map/ppermute | solution.py:146
  66.3 0.0 collective-permute-done.6.refs_7_
  66.3 0.0 copy-start.12
  66.3 1.9 %collective-permute-start.12 = (bf16[304,512]{1,0:T(8,128)(2,1)S(1)}, bf16[304,512]{1,0:T(8,128)(2,1)}, u32[]{:S(2)}, u32[]{:S(2)}) collective-permute-start(bf16[304,512]{1,0:T(8,128)(2,1)S(1)} %collective-permute-done.6.refs_7_), channel_id=1, source_target_pairs={{0,1},{1,2},{2,3},{3,4},{4,5},{5,6},{6,7},{7,0},{8,9},{9,10},{10,1... | collective-permute-start | bytes 933896 | tf_op jit(solution)/shard_map/ppermute | solution.py:146
  68.2 0.0 collective-permute-done.10.refs_12_
  68.2 0.0 copy-start.13
  68.3 2.0 %collective-permute-done.11.refs_14_ = bf16[304,512]{1,0:T(8,128)(2,1)S(1)} collective-permute-done((bf16[304,512]{1,0:T(8,128)(2,1)S(1)}, bf16[304,512]{1,0:T(8,128)(2,1)S(1)}, u32[]{:S(2)}, u32[]{:S(2)}) %collective-permute-start.11) | collective-permute-done | bytes 311328 | tf_op jit(solution)/shard_map/ppermute | solution.py:146
  70.3 1.5 %collective-permute-done.13.refs_13_ = bf16[304,512]{1,0:T(8,128)(2,1)S(1)} collective-permute-done((bf16[304,512]{1,0:T(8,128)(2,1)S(1)}, bf16[304,512]{1,0:T(8,128)(2,1)S(1)}, u32[]{:S(2)}, u32[]{:S(2)}) %collective-permute-start.13) | collective-permute-done | bytes 311328 | tf_op jit(solution)/shard_map/ppermute | solution.py:146
  71.8 0.0 copy-done.5
  71.8 0.0 copy-done.6
  71.8 0.0 copy-done.7
  71.8 0.0 copy-done.8
  71.8 0.0 copy-done.10
  71.8 0.0 copy-done.11
  71.8 0.0 copy-done.12
  71.8 0.0 copy-done.13
  71.8 0.0 copy-done.14
  71.8 0.0 copy-start.15
  71.9 0.7 copy-done.15
  72.6 4.8 %collective-permute-done.12.refs_11_ = bf16[304,512]{1,0:T(8,128)(2,1)} collective-permute-done((bf16[304,512]{1,0:T(8,128)(2,1)S(1)}, bf16[304,512]{1,0:T(8,128)(2,1)}, u32[]{:S(2)}, u32[]{:S(2)}) %collective-permute-start.12) | collective-permute-done | bytes 311328 | tf_op jit(solution)/shard_map/ppermute | solution.py:146
  77.4 5.3 %all-to-all-done = bf16[8,2,152,512]{3,2,1,0:T(8,128)(2,1)S(1)} async-done(((bf16[8,2,152,512]{3,2,1,0:T(8,128)(2,1)}), bf16[8,2,152,512]{3,2,1,0:T(8,128)(2,1)S(1)}, u32[]{:S(2)}, u32[]{:S(2)}) %all-to-all-start) | async-done | bytes 2490400 | tf_op jit(solution)/shard_map/all_to_all | solution.py:161
  82.8 2.4 %collective-permute-start.15 = (bf16[8,2,152,512]{3,2,1,0:T(8,128)(2,1)S(1)}, bf16[8,2,152,512]{3,2,1,0:T(8,128)(2,1)S(1)}, u32[]{:S(2)}, u32[]{:S(2)}) collective-permute-start(bf16[8,2,152,512]{3,2,1,0:T(8,128)(2,1)S(1)} %all-to-all-done), channel_id=1, source_target_pairs={{0,16},{16,0},{1,17},{17,1},{2,18},{18,2},{3,19},{19,3},{4,20},{20... | collective-permute-start | bytes 7471112 | tf_op jit(solution)/shard_map/ppermute | solution.py:146
  85.2 5.1 %collective-permute-start.14 = (bf16[304,512]{1,0:T(8,128)(2,1)}, bf16[304,512]{1,0:T(8,128)(2,1)S(1)}, u32[]{:S(2)}, u32[]{:S(2)}) collective-permute-start(bf16[304,512]{1,0:T(8,128)(2,1)} %copy-done.15), channel_id=1, source_target_pairs={{0,7},{1,0},{2,1},{3,2},{4,3},{5,4},{6,5},{7,6},{8,15},{9,8},{10,9... | collective-permute-start | bytes 933896 | tf_op jit(solution)/shard_map/ppermute | solution.py:146
  90.3 7.1 %collective-permute-done.14.refs_15_ = bf16[304,512]{1,0:T(8,128)(2,1)S(1)} collective-permute-done((bf16[304,512]{1,0:T(8,128)(2,1)}, bf16[304,512]{1,0:T(8,128)(2,1)S(1)}, u32[]{:S(2)}, u32[]{:S(2)}) %collective-permute-start.14) | collective-permute-done | bytes 311328 | tf_op jit(solution)/shard_map/ppermute | solution.py:146
  97.4 0.0 collective-permute-done.15
  97.4 1.5 %copy-done.1 = bf16[8,2,152,512]{3,2,1,0:T(8,128)(2,1)} copy-done((bf16[8,2,152,512]{3,2,1,0:T(8,128)(2,1)}, bf16[8,2,152,512]{3,2,1,0:T(8,128)(2,1)S(1)}, u32[]{:S(2)}) %copy-start.1) | copy-done | bytes 2490392
  98.9 0.0 copy-done.3
  98.9 0.0 copy-done.4
  98.9 0.0 copy-done.16
  99.0 8.9 %shard_map.65 = f32[512,1024]{1,0:T(8,128)} custom-call(s32[2,8]{1,0:T(2,128)} %bitcast.9, s32[4]{0:T(128)} %down_ref.3, bf16[304,512]{1,0:T(8,128)(2,1)} %get-tuple-element.13.refs_0_, bf16[304,512]{1,0:T(8,128)(2,1)} %copy-done.4, bf16[304,512]{1,0:T(8,128)(2,1)} %copy-done.3, bf16[304,512]{1,0:T(8,128)(2,1)} %copy-done.8, bf16[304,512]{1,0:T(8,128)(2,1)} %copy-done.5, ...), custom_call_target="tpu_custom_call" | custom-call | tf_op jit(solution)/shard_map/pallas_call | solution.py:125
  (8 shorter events, 0.0 us)
Async XLA Ops:
  11.5 11.2 %copy-start.2 = (bf16[304,512]{1,0:T(8,128)(2,1)S(1)}, bf16[304,512]{1,0:T(8,128)(2,1)}, u32[]{:S(2)}) copy-start(bf16[304,512]{1,0:T(8,128)(2,1)} %get-tuple-element.13.refs_0_) | copy-start | bytes 933892
  11.5 71.3 %all-to-all-start = ((bf16[8,2,152,512]{3,2,1,0:T(8,128)(2,1)}), bf16[8,2,152,512]{3,2,1,0:T(8,128)(2,1)S(1)}, u32[]{:S(2)}, u32[]{:S(2)}) async-start(bf16[8,2,152,512]{3,2,1,0:T(8,128)(2,1)} %broadcast_in_dim.2), calls=%async_computation | async-start | bytes 4980736 | tf_op jit(solution)/shard_map/all_to_all | solution.py:161
  22.6 10.9 %collective-permute-start.1 = (bf16[304,512]{1,0:T(8,128)(2,1)S(1)}, bf16[304,512]{1,0:T(8,128)(2,1)S(1)}, u32[]{:S(2)}, u32[]{:S(2)}) collective-permute-start(bf16[304,512]{1,0:T(8,128)(2,1)S(1)} %copy-done.2), channel_id=1, source_target_pairs={{0,1},{1,2},{2,3},{3,4},{4,5},{5,6},{6,7},{7,0},{8,9},{9,10},{10,1... | collective-permute-start | bytes 933896 | tf_op jit(solution)/shard_map/ppermute | solution.py:146
  25.9 9.6 %collective-permute-start = (bf16[304,512]{1,0:T(8,128)(2,1)S(1)}, bf16[304,512]{1,0:T(8,128)(2,1)S(1)}, u32[]{:S(2)}, u32[]{:S(2)}) collective-permute-start(bf16[304,512]{1,0:T(8,128)(2,1)S(1)} %copy-done.2), channel_id=1, source_target_pairs={{0,8},{8,0},{1,9},{9,1},{2,10},{10,2},{3,11},{11,3},{4,12},{12,4},... | collective-permute-start | bytes 933896 | tf_op jit(solution)/shard_map/ppermute | solution.py:146
  29.0 13.0 %collective-permute-start.3 = (bf16[304,512]{1,0:T(8,128)(2,1)S(1)}, bf16[304,512]{1,0:T(8,128)(2,1)S(1)}, u32[]{:S(2)}, u32[]{:S(2)}) collective-permute-start(bf16[304,512]{1,0:T(8,128)(2,1)S(1)} %copy-done.2), channel_id=1, source_target_pairs={{0,7},{1,0},{2,1},{3,2},{4,3},{5,4},{6,5},{7,6},{8,15},{9,8},{10,9... | collective-permute-start | bytes 933896 | tf_op jit(solution)/shard_map/ppermute | solution.py:146
  33.6 65.3 %copy-start.3 = (bf16[304,512]{1,0:T(8,128)(2,1)}, bf16[304,512]{1,0:T(8,128)(2,1)S(1)}, u32[]{:S(2)}) copy-start(bf16[304,512]{1,0:T(8,128)(2,1)S(1)} %collective-permute-done.1.refs_2_) | copy-start | bytes 933892
  33.6 13.1 %collective-permute-start.5 = (bf16[304,512]{1,0:T(8,128)(2,1)S(1)}, bf16[304,512]{1,0:T(8,128)(2,1)S(1)}, u32[]{:S(2)}, u32[]{:S(2)}) collective-permute-start(bf16[304,512]{1,0:T(8,128)(2,1)S(1)} %collective-permute-done.1.refs_2_), channel_id=1, source_target_pairs={{0,1},{1,2},{2,3},{3,4},{4,5},{5,6},{6,7},{7,0},{8,9},{9,10},{10,1... | collective-permute-start | bytes 933896 | tf_op jit(solution)/shard_map/ppermute | solution.py:146
  35.5 63.4 %copy-start.4 = (bf16[304,512]{1,0:T(8,128)(2,1)}, bf16[304,512]{1,0:T(8,128)(2,1)S(1)}, u32[]{:S(2)}) copy-start(bf16[304,512]{1,0:T(8,128)(2,1)S(1)} %collective-permute-done.refs_1_) | copy-start | bytes 933892
  35.5 13.1 %collective-permute-start.4 = (bf16[304,512]{1,0:T(8,128)(2,1)S(1)}, bf16[304,512]{1,0:T(8,128)(2,1)S(1)}, u32[]{:S(2)}, u32[]{:S(2)}) collective-permute-start(bf16[304,512]{1,0:T(8,128)(2,1)S(1)} %collective-permute-done.refs_1_), channel_id=1, source_target_pairs={{0,7},{1,0},{2,1},{3,2},{4,3},{5,4},{6,5},{7,6},{8,15},{9,8},{10,9... | collective-permute-start | bytes 933896 | tf_op jit(solution)/shard_map/ppermute | solution.py:146
  40.1 13.1 %collective-permute-start.2 = (bf16[304,512]{1,0:T(8,128)(2,1)S(1)}, bf16[304,512]{1,0:T(8,128)(2,1)S(1)}, u32[]{:S(2)}, u32[]{:S(2)}) collective-permute-start(bf16[304,512]{1,0:T(8,128)(2,1)S(1)} %collective-permute-done.refs_1_), channel_id=1, source_target_pairs={{0,1},{1,2},{2,3},{3,4},{4,5},{5,6},{6,7},{7,0},{8,9},{9,10},{10,1... | collective-permute-start | bytes 933896 | tf_op jit(solution)/shard_map/ppermute | solution.py:146
  42.0 29.7 %copy-start.5 = (bf16[304,512]{1,0:T(8,128)(2,1)}, bf16[304,512]{1,0:T(8,128)(2,1)S(1)}, u32[]{:S(2)}) copy-start(bf16[304,512]{1,0:T(8,128)(2,1)S(1)} %collective-permute-done.3.refs_4_) | copy-start | bytes 933892
  42.1 13.1 %collective-permute-start.7 = (bf16[304,512]{1,0:T(8,128)(2,1)S(1)}, bf16[304,512]{1,0:T(8,128)(2,1)S(1)}, u32[]{:S(2)}, u32[]{:S(2)}) collective-permute-start(bf16[304,512]{1,0:T(8,128)(2,1)S(1)} %collective-permute-done.3.refs_4_), channel_id=1, source_target_pairs={{0,7},{1,0},{2,1},{3,2},{4,3},{5,4},{6,5},{7,6},{8,15},{9,8},{10,9... | collective-permute-start | bytes 933896 | tf_op jit(solution)/shard_map/ppermute | solution.py:146
  46.6 25.1 %copy-start.6 = (bf16[304,512]{1,0:T(8,128)(2,1)}, bf16[304,512]{1,0:T(8,128)(2,1)S(1)}, u32[]{:S(2)}) copy-start(bf16[304,512]{1,0:T(8,128)(2,1)S(1)} %collective-permute-done.5.refs_6_) | copy-start | bytes 933892
  46.7 13.1 %collective-permute-start.9 = (bf16[304,512]{1,0:T(8,128)(2,1)S(1)}, bf16[304,512]{1,0:T(8,128)(2,1)S(1)}, u32[]{:S(2)}, u32[]{:S(2)}) collective-permute-start(bf16[304,512]{1,0:T(8,128)(2,1)S(1)} %collective-permute-done.5.refs_6_), channel_id=1, source_target_pairs={{0,1},{1,2},{2,3},{3,4},{4,5},{5,6},{6,7},{7,0},{8,9},{9,10},{10,1... | collective-permute-start | bytes 933896 | tf_op jit(solution)/shard_map/ppermute | solution.py:146
  48.6 23.2 %copy-start.7 = (bf16[304,512]{1,0:T(8,128)(2,1)}, bf16[304,512]{1,0:T(8,128)(2,1)S(1)}, u32[]{:S(2)}) copy-start(bf16[304,512]{1,0:T(8,128)(2,1)S(1)} %collective-permute-done.4.refs_5_) | copy-start | bytes 933892
  48.6 13.1 %collective-permute-start.8 = (bf16[304,512]{1,0:T(8,128)(2,1)S(1)}, bf16[304,512]{1,0:T(8,128)(2,1)S(1)}, u32[]{:S(2)}, u32[]{:S(2)}) collective-permute-start(bf16[304,512]{1,0:T(8,128)(2,1)S(1)} %collective-permute-done.4.refs_5_), channel_id=1, source_target_pairs={{0,7},{1,0},{2,1},{3,2},{4,3},{5,4},{6,5},{7,6},{8,15},{9,8},{10,9... | collective-permute-start | bytes 933896 | tf_op jit(solution)/shard_map/ppermute | solution.py:146
  53.2 18.6 %copy-start.8 = (bf16[304,512]{1,0:T(8,128)(2,1)}, bf16[304,512]{1,0:T(8,128)(2,1)S(1)}, u32[]{:S(2)}) copy-start(bf16[304,512]{1,0:T(8,128)(2,1)S(1)} %collective-permute-done.2.refs_3_) | copy-start | bytes 933892
  53.2 13.1 %collective-permute-start.6 = (bf16[304,512]{1,0:T(8,128)(2,1)S(1)}, bf16[304,512]{1,0:T(8,128)(2,1)S(1)}, u32[]{:S(2)}, u32[]{:S(2)}) collective-permute-start(bf16[304,512]{1,0:T(8,128)(2,1)S(1)} %collective-permute-done.2.refs_3_), channel_id=1, source_target_pairs={{0,1},{1,2},{2,3},{3,4},{4,5},{5,6},{6,7},{7,0},{8,9},{9,10},{10,1... | collective-permute-start | bytes 933896 | tf_op jit(solution)/shard_map/ppermute | solution.py:146
  55.1 43.8 %copy-start.9 = (bf16[304,512]{1,0:T(8,128)(2,1)}, bf16[304,512]{1,0:T(8,128)(2,1)S(1)}, u32[]{:S(2)}) copy-start(bf16[304,512]{1,0:T(8,128)(2,1)S(1)} %collective-permute-done.7.refs_8_) | copy-start | bytes 933892
  55.2 13.1 %collective-permute-start.10 = (bf16[304,512]{1,0:T(8,128)(2,1)S(1)}, bf16[304,512]{1,0:T(8,128)(2,1)S(1)}, u32[]{:S(2)}, u32[]{:S(2)}) collective-permute-start(bf16[304,512]{1,0:T(8,128)(2,1)S(1)} %collective-permute-done.7.refs_8_), channel_id=1, source_target_pairs={{0,7},{1,0},{2,1},{3,2},{4,3},{5,4},{6,5},{7,6},{8,15},{9,8},{10,9... | collective-permute-start | bytes 933896 | tf_op jit(solution)/shard_map/ppermute | solution.py:146
  59.7 12.1 %copy-start.10 = (bf16[304,512]{1,0:T(8,128)(2,1)}, bf16[304,512]{1,0:T(8,128)(2,1)S(1)}, u32[]{:S(2)}) copy-start(bf16[304,512]{1,0:T(8,128)(2,1)S(1)} %collective-permute-done.9.refs_10_) | copy-start | bytes 933892
  59.8 10.5 %collective-permute-start.11 = (bf16[304,512]{1,0:T(8,128)(2,1)S(1)}, bf16[304,512]{1,0:T(8,128)(2,1)S(1)}, u32[]{:S(2)}, u32[]{:S(2)}) collective-permute-start(bf16[304,512]{1,0:T(8,128)(2,1)S(1)} %collective-permute-done.9.refs_10_), channel_id=1, source_target_pairs={{0,1},{1,2},{2,3},{3,4},{4,5},{5,6},{6,7},{7,0},{8,9},{9,10},{10,1... | collective-permute-start | bytes 933896 | tf_op jit(solution)/shard_map/ppermute | solution.py:146
  61.7 10.1 %copy-start.11 = (bf16[304,512]{1,0:T(8,128)(2,1)}, bf16[304,512]{1,0:T(8,128)(2,1)S(1)}, u32[]{:S(2)}) copy-start(bf16[304,512]{1,0:T(8,128)(2,1)S(1)} %collective-permute-done.8.refs_9_) | copy-start | bytes 933892
  61.7 10.1 %collective-permute-start.13 = (bf16[304,512]{1,0:T(8,128)(2,1)S(1)}, bf16[304,512]{1,0:T(8,128)(2,1)S(1)}, u32[]{:S(2)}, u32[]{:S(2)}) collective-permute-start(bf16[304,512]{1,0:T(8,128)(2,1)S(1)} %collective-permute-done.8.refs_9_), channel_id=1, source_target_pairs={{0,7},{1,0},{2,1},{3,2},{4,3},{5,4},{6,5},{7,6},{8,15},{9,8},{10,9... | collective-permute-start | bytes 933896 | tf_op jit(solution)/shard_map/ppermute | solution.py:146
  66.3 5.5 %copy-start.12 = (bf16[304,512]{1,0:T(8,128)(2,1)}, bf16[304,512]{1,0:T(8,128)(2,1)S(1)}, u32[]{:S(2)}) copy-start(bf16[304,512]{1,0:T(8,128)(2,1)S(1)} %collective-permute-done.6.refs_7_) | copy-start | bytes 933892
  66.3 11.1 %collective-permute-start.12 = (bf16[304,512]{1,0:T(8,128)(2,1)S(1)}, bf16[304,512]{1,0:T(8,128)(2,1)}, u32[]{:S(2)}, u32[]{:S(2)}) collective-permute-start(bf16[304,512]{1,0:T(8,128)(2,1)S(1)} %collective-permute-done.6.refs_7_), channel_id=1, source_target_pairs={{0,1},{1,2},{2,3},{3,4},{4,5},{5,6},{6,7},{7,0},{8,9},{9,10},{10,1... | collective-permute-start | bytes 933896 | tf_op jit(solution)/shard_map/ppermute | solution.py:146
  68.2 3.6 %copy-start.13 = (bf16[304,512]{1,0:T(8,128)(2,1)}, bf16[304,512]{1,0:T(8,128)(2,1)S(1)}, u32[]{:S(2)}) copy-start(bf16[304,512]{1,0:T(8,128)(2,1)S(1)} %collective-permute-done.10.refs_12_) | copy-start | bytes 933892
  70.3 1.5 %copy-start.14 = (bf16[304,512]{1,0:T(8,128)(2,1)}, bf16[304,512]{1,0:T(8,128)(2,1)S(1)}, u32[]{:S(2)}) copy-start(bf16[304,512]{1,0:T(8,128)(2,1)S(1)} %collective-permute-done.11.refs_14_) | copy-start | bytes 933892
  71.8 0.7 copy-start.15
  82.8 16.1 %copy-start = (bf16[8,2,152,512]{3,2,1,0:T(8,128)(2,1)}, bf16[8,2,152,512]{3,2,1,0:T(8,128)(2,1)S(1)}, u32[]{:S(2)}) copy-start(bf16[8,2,152,512]{3,2,1,0:T(8,128)(2,1)S(1)} %all-to-all-done) | copy-start | bytes 7471108
  82.8 14.6 %collective-permute-start.15 = (bf16[8,2,152,512]{3,2,1,0:T(8,128)(2,1)S(1)}, bf16[8,2,152,512]{3,2,1,0:T(8,128)(2,1)S(1)}, u32[]{:S(2)}, u32[]{:S(2)}) collective-permute-start(bf16[8,2,152,512]{3,2,1,0:T(8,128)(2,1)S(1)} %all-to-all-done), channel_id=1, source_target_pairs={{0,16},{16,0},{1,17},{17,1},{2,18},{18,2},{3,19},{19,3},{4,20},{20... | collective-permute-start | bytes 7471112 | tf_op jit(solution)/shard_map/ppermute | solution.py:146
  85.2 12.2 %collective-permute-start.14 = (bf16[304,512]{1,0:T(8,128)(2,1)}, bf16[304,512]{1,0:T(8,128)(2,1)S(1)}, u32[]{:S(2)}, u32[]{:S(2)}) collective-permute-start(bf16[304,512]{1,0:T(8,128)(2,1)} %copy-done.15), channel_id=1, source_target_pairs={{0,7},{1,0},{2,1},{3,2},{4,3},{5,4},{6,5},{7,6},{8,15},{9,8},{10,9... | collective-permute-start | bytes 933896 | tf_op jit(solution)/shard_map/ppermute | solution.py:146
  97.4 1.6 %copy-start.16 = (bf16[304,512]{1,0:T(8,128)(2,1)}, bf16[304,512]{1,0:T(8,128)(2,1)S(1)}, u32[]{:S(2)}) copy-start(bf16[304,512]{1,0:T(8,128)(2,1)S(1)} %collective-permute-done.14.refs_15_) | copy-start | bytes 933892
  97.4 1.5 %copy-start.1 = (bf16[8,2,152,512]{3,2,1,0:T(8,128)(2,1)}, bf16[8,2,152,512]{3,2,1,0:T(8,128)(2,1)S(1)}, u32[]{:S(2)}) copy-start(bf16[8,2,152,512]{3,2,1,0:T(8,128)(2,1)S(1)} %collective-permute-done.15) | copy-start | bytes 7471108

commit v3 on v2

--- a/solution.py
+++ b/solution.py
@@ -27,7 +27,7 @@
 ANY = pl.BlockSpec(memory_space=pl.ANY)
 
 
-def pack_kernel(down_ref, dec_ref, delta_ref, enc_ref, grad_ref, d_ref, e_ref, sems):
+def pack_kernel(down_ref, dec_ref, delta_ref, enc_ref, grad_ref, d_ref, e_ref, active, sems):
     copies = []
 
     def move(source, target):
@@ -36,11 +36,16 @@
 
     for i in range(DACT):
         cols = pl.ds(pl.multiple_of(down_ref[i] * BLOCK, BLOCK), BLOCK)
-        move(enc_ref.at[:, cols], e_ref.at[:KE, i * BLOCK : (i + 1) * BLOCK])
-        move(grad_ref.at[:, cols], e_ref.at[KE:, i * BLOCK : (i + 1) * BLOCK])
+        move(enc_ref.at[:, cols], active.at[:KE, i * BLOCK : (i + 1) * BLOCK])
+        move(grad_ref.at[:, cols], active.at[KE:, i * BLOCK : (i + 1) * BLOCK])
+    loads = len(copies)
     move(dec_ref, d_ref.at[:KD])
     move(delta_ref, d_ref.at[KD:])
-    for copy in copies:
+    for copy in copies[:loads]:
+        copy.wait()
+    for n in range(2 * NY):
+        move(active, e_ref.at[n])
+    for copy in copies[loads:]:
         copy.wait()
 
 
@@ -49,18 +54,22 @@
         pack_kernel,
         out_shape=(
             jax.ShapeDtypeStruct((RD, UF_DEV), jnp.bfloat16),
-            jax.ShapeDtypeStruct((RE, DACT * BLOCK), jnp.bfloat16),
+            jax.ShapeDtypeStruct((2 * NY, RE, DACT * BLOCK), jnp.bfloat16),
         ),
         in_specs=[SMEM, ANY, ANY, ANY, ANY],
-        out_specs=(VMEM, VMEM),
-        scratch_shapes=[pltpu.SemaphoreType.DMA((2 * DACT + 2,))],
+        out_specs=(VMEM, ANY),
+        scratch_shapes=[
+            pltpu.VMEM((RE, DACT * BLOCK), jnp.bfloat16),
+            pltpu.SemaphoreType.DMA((2 * DACT + 2 + 2 * NY,)),
+        ],
         compiler_params=pltpu.CompilerParams(vmem_limit_bytes=60 << 20),
     )(down_blocks, dec_t, deltas, encoder, gradients)
 
 
 def score_kernel(up_ref, down_ref, *refs):
     shards = refs[: 2 * NY]
-    own, swapped, out_ref, dec, tok, enc, grad, dec_sem, tok_sem, enc_sem, grad_sem = refs[2 * NY :]
+    own, swapped, out_ref, dec, tok, enc, grad, zero, scored = refs[2 * NY : 2 * NY + 9]
+    dec_sem, tok_sem, enc_sem, grad_sem, zero_sem, out_sem = refs[2 * NY + 9 :]
     y, xl, core = lax.axis_index("y"), lax.axis_index("xl"), lax.axis_index("c")
     grads = []
     for source, part in ((own, core), (swapped, 1 - core)):
@@ -89,7 +98,20 @@
         for copy in mine + tokens[-1:]:
             copy.start()
         blocks.append(mine)
-    out_ref[...] = jnp.zeros_like(out_ref)
+    zero[...] = jnp.zeros_like(zero)
+
+    def blank(b):
+        return pltpu.make_async_copy(
+            zero, out_ref.at[:, b * BLOCK : (b + 1) * BLOCK], zero_sem.at[b]
+        )
+
+    idle = []
+    for b in range(VF_DEV // BLOCK):
+        used = down_ref[0] == b
+        for i in range(1, DACT):
+            used = used | (down_ref[i] == b)
+        idle.append(jnp.logical_not(used))
+        pl.when(idle[b])(blank(b).start)
     dims = (((0,), (0,)), ((), ()))
     virtual = None
     for first in range(0, 2 * NY, STEP):
@@ -114,10 +136,19 @@
     masked = jnp.concatenate(masked, 0).astype(jnp.bfloat16)
     kept = grad[...].astype(jnp.float32).reshape(NY * 2 * TD, DACT * BLOCK).astype(jnp.bfloat16)
     product = lax.dot_general(masked, kept, dims, preferred_element_type=jnp.float32)
-    scored = product * virtual
+    filled = []
     for i in range(DACT):
+        part = slice(i * BLOCK, (i + 1) * BLOCK)
+        scored[i] = product[:, part] * virtual[:, part]
         cols = pl.ds(pl.multiple_of(down_ref[i] * BLOCK, BLOCK), BLOCK)
-        out_ref[:, cols] = scored[:, i * BLOCK : (i + 1) * BLOCK]
+        filled.append(
+            pltpu.make_async_copy(scored.at[i], out_ref.at[:, cols], out_sem.at[i])
+        )
+        filled[i].start()
+    for b in range(VF_DEV // BLOCK):
+        pl.when(idle[b])(blank(b).wait)
+    for copy in filled:
+        copy.wait()
 
 
 def score(up_blocks, down_blocks, shards, own, swapped):
@@ -126,16 +157,20 @@
         score_kernel,
         out_shape=jax.ShapeDtypeStruct((UF_DEV, VF_DEV), jnp.float32),
         in_specs=[SMEM, SMEM] + [ANY] * (2 * NY + 2),
-        out_specs=VMEM,
+        out_specs=ANY,
         scratch_shapes=[
             pltpu.VMEM((2 * NY, KD, UF_DEV), jnp.bfloat16),
             pltpu.VMEM((2 * NY, TD, UF_DEV), jnp.bfloat16),
             pltpu.VMEM((2 * NY, 2, KE, cols), jnp.bfloat16),
             pltpu.VMEM((2 * NY, 2, TE, cols), jnp.bfloat16),
+            pltpu.VMEM((UF_DEV, BLOCK), jnp.float32),
+            pltpu.VMEM((DACT, UF_DEV, BLOCK), jnp.float32),
             pltpu.SemaphoreType.DMA((2 * NY,)),
             pltpu.SemaphoreType.DMA((2 * NY,)),
             pltpu.SemaphoreType.DMA((2 * NY, 2)),
             pltpu.SemaphoreType.DMA((2,)),
+            pltpu.SemaphoreType.DMA((VF_DEV // BLOCK,)),
+            pltpu.SemaphoreType.DMA((DACT,)),
         ],
         compiler_params=pltpu.CompilerParams(vmem_limit_bytes=60 << 20),
     )(up_blocks.T, down_blocks, *shards, own, swapped)
@@ -146,25 +181,25 @@
     return lax.ppermute(value, axis, [(i, (i + by) % n) for i in range(n)])
 
 
-def ring(value, last):
+def ring(value):
     right = left = value
     held = [value]
     for _ in range(NY // 2 - 1):
         right, left = turn(right, "y", 1), turn(left, "y", -1)
         held += [right, left]
-    return held + [turn(right if last > 0 else left, "y", last)]
+    return held
 
 
 def local(deltas, gradients, up_blocks, down_blocks, decoder, encoder):
     d, e = pack(down_blocks, decoder.T, deltas, encoder, gradients)
-    pair = lax.all_gather(e, "xh")
-    own = lax.all_to_all(jnp.broadcast_to(pair[None], (NY, *pair.shape)), "z", 0, 0, tiled=True)
-    near = ring(d, 1)
-    across = ring(turn(d, "xl", 1), -1)
-    own, near[5:], across[5:7] = lax.optimization_barrier((own, near[5:], across[5:7]))
-    shards = [shard for both in zip(near, across) for shard in both]
+    own = lax.all_to_all(e, ("z", "xh"), 0, 0, tiled=True)
+    near = ring(d)
+    across = ring(turn(d, "xl", 1))
+    far = turn(near[5], "y", 1)
+    beyond = turn(far, "xl", 1)
+    own, last, near[5:], across[5:] = lax.optimization_barrier((own, far, near[5:], across[5:]))
+    shards = [s for both in zip(near + [last], across + [beyond]) for s in both]
     swapped = turn(own, "c", 1)
-    own, swapped = (v.reshape(2 * NY, RE, DACT * BLOCK) for v in (own, swapped))
     return score(up_blocks, down_blocks, shards, own, swapped)
 
 

time: 109 us -> 103 us (0.945)
  blocking collectives: 7.12 us -> 0 us
  local copies, waits for them, and re-layouts: 4.04 us -> 2.33 us
  waiting for transfers between devices: 21.6 us -> 23 us
  Pallas kernels: 11.6 us -> 12.9 us
    all_gather x1 -> x0, blocking collectives: 7.12 us -> none  [local(): pair = lax.all_gather(e, 'xh')]
    ppermute x16, waiting for transfers between devices: 16.2 us -> 18.9 us  [turn(): return lax.ppermute(value, axis, [(i, (i + by) % n) for i in range(n)])]
    all_to_all x1, starting transfers between devices: 11.2 us -> 13.6 us  [local(): own = lax.all_to_all(e, ('z', 'xh'), 0, 0, tiled=True)]
    ppermute x16, starting transfers between devices: 52 us -> 50.1 us  [turn(): return lax.ppermute(value, axis, [(i, (i + by) % n) for i in range(n)])]
    broadcast_in_dim x1 -> x0, local copies, waits for them, and re-layouts: 1.71 us -> none  [local(): jnp.broadcast_to(pair[None], (NY, *pair.shape))]
    pallas_call x1, Pallas kernels: 2.64 us -> 3.97 us  [pack(): pl.pallas_call(pack_kernel, out_shape=(jax.ShapeDtypeStruct((RD, UF_DEV),...]
    all_to_all x1, waiting for transfers between devices: 5.35 us -> 4.11 us  [local(): own = lax.all_to_all(e, ('z', 'xh'), 0, 0, tiled=True)]
    unnamed x34 -> x32, local copies, waits for them, and re-layouts: 2.33 us -> 2.33 us
where the time goes in v3:
time: 103 us; the launch traced here: 102 us
  starting transfers between devices  63.6 us (62%)
  waiting for transfers between devices  23 us (22%)
  Pallas kernels  12.9 us (13%)
  local copies, waits for them, and re-layouts  2.33 us (2%)
    ppermute x16, starting transfers between devices, turn(): return lax.ppermute(value, axis, [(i, (i + by) % n) for i in range(n)])  50.1 us
    ppermute x16, waiting for transfers between devices, turn(): return lax.ppermute(value, axis, [(i, (i + by) % n) for i in range(n)])  18.9 us
    all_to_all x1, starting transfers between devices, local(): own = lax.all_to_all(e, ('z', 'xh'), 0, 0, tiled=True)  13.6 us
    pallas_call x1, Pallas kernels, score(): pl.pallas_call(score_kernel, out_shape=jax.ShapeDtypeStruct((UF_DEV, VF_D...  8.95 us
    all_to_all x1, waiting for transfers between devices, local(): own = lax.all_to_all(e, ('z', 'xh'), 0, 0, tiled=True)  4.11 us
    pallas_call x1, Pallas kernels, pack(): pl.pallas_call(pack_kernel, out_shape=(jax.ShapeDtypeStruct((RD, UF_DEV),...  3.97 us
    unnamed x32, local copies, waits for them, and re-layouts  2.33 us
  transfers between devices with their start and end apart: 17, of which 6 were waited for; matrix products, arithmetic and copies ran while one was open for 0% of the time, Pallas kernels for 0%

profile of v3, /device:TPU:1, one launch (start us, length us, event | category | flops | bytes accessed | tf_op | source)
XLA Modules:
  0.0 102.3 jit_solution(2604322923970197509)
XLA Ops:
  0.0 4.0 %shard_map.64 = (bf16[304,512]{1,0:T(8,128)(2,1)}, bf16[16,152,512]{2,1,0:T(8,128)(2,1)}) custom-call(s32[4]{0:T(128)} %down_ref.3, bf16[288,512]{1,0:T(8,128)(2,1)} %bitcast.2, bf16[16,512]{1,0:T(8,128)(2,1)} %delta_ref.1, bf16[144,1024]{1,0:T(8,128)(2,1)} %enc_ref.1, bf16[8,1024]{1,0:T(8,128)(2,1)} %grad_ref.1), custom_call_target="tpu_custom_call" | custom-call | tf_op jit(solution)/shard_map/pallas_call | solution.py:53
  4.0 0.0 copy-start.2
  4.0 13.6 %all-to-all-start = ((bf16[16,152,512]{2,1,0:T(8,128)(2,1)}), bf16[16,152,512]{2,1,0:T(8,128)(2,1)S(1)}, u32[]{:S(2)}, u32[]{:S(2)}) async-start(bf16[16,152,512]{2,1,0:T(8,128)(2,1)} %get-tuple-element.14), calls=%async_computation | async-start | bytes 4980736 | tf_op jit(solution)/shard_map/all_to_all | solution.py:195
  17.6 0.0 copy-done.2
  17.6 3.2 %collective-permute-start.1 = (bf16[304,512]{1,0:T(8,128)(2,1)S(1)}, bf16[304,512]{1,0:T(8,128)(2,1)S(1)}, u32[]{:S(2)}, u32[]{:S(2)}) collective-permute-start(bf16[304,512]{1,0:T(8,128)(2,1)S(1)} %copy-done.2), channel_id=1, source_target_pairs={{0,1},{1,2},{2,3},{3,4},{4,5},{5,6},{6,7},{7,0},{8,9},{9,10},{10,1... | collective-permute-start | bytes 933896 | tf_op jit(solution)/shard_map/ppermute | solution.py:181
  20.8 2.2 %collective-permute-start = (bf16[304,512]{1,0:T(8,128)(2,1)S(1)}, bf16[304,512]{1,0:T(8,128)(2,1)S(1)}, u32[]{:S(2)}, u32[]{:S(2)}) collective-permute-start(bf16[304,512]{1,0:T(8,128)(2,1)S(1)} %copy-done.2), channel_id=1, source_target_pairs={{0,8},{8,0},{1,9},{9,1},{2,10},{10,2},{3,11},{11,3},{4,12},{12,4},... | collective-permute-start | bytes 933896 | tf_op jit(solution)/shard_map/ppermute | solution.py:181
  23.0 3.8 %collective-permute-start.3 = (bf16[304,512]{1,0:T(8,128)(2,1)S(1)}, bf16[304,512]{1,0:T(8,128)(2,1)S(1)}, u32[]{:S(2)}, u32[]{:S(2)}) collective-permute-start(bf16[304,512]{1,0:T(8,128)(2,1)S(1)} %copy-done.2), channel_id=1, source_target_pairs={{0,7},{1,0},{2,1},{3,2},{4,3},{5,4},{6,5},{7,6},{8,15},{9,8},{10,9... | collective-permute-start | bytes 933896 | tf_op jit(solution)/shard_map/ppermute | solution.py:181
  26.8 2.6 %collective-permute-done.1.refs_2_ = bf16[304,512]{1,0:T(8,128)(2,1)S(1)} collective-permute-done((bf16[304,512]{1,0:T(8,128)(2,1)S(1)}, bf16[304,512]{1,0:T(8,128)(2,1)S(1)}, u32[]{:S(2)}, u32[]{:S(2)}) %collective-permute-start.1) | collective-permute-done | bytes 311328 | tf_op jit(solution)/shard_map/ppermute | solution.py:181
  29.4 1.9 %collective-permute-start.5 = (bf16[304,512]{1,0:T(8,128)(2,1)S(1)}, bf16[304,512]{1,0:T(8,128)(2,1)S(1)}, u32[]{:S(2)}, u32[]{:S(2)}) collective-permute-start(bf16[304,512]{1,0:T(8,128)(2,1)S(1)} %collective-permute-done.1.refs_2_), channel_id=1, source_target_pairs={{0,1},{1,2},{2,3},{3,4},{4,5},{5,6},{6,7},{7,0},{8,9},{9,10},{10,1... | collective-permute-start | bytes 933896 | tf_op jit(solution)/shard_map/ppermute | solution.py:181
  31.4 0.0 collective-permute-done.refs_1_
  31.4 0.0 copy-start.4
  31.4 4.6 %collective-permute-start.4 = (bf16[304,512]{1,0:T(8,128)(2,1)S(1)}, bf16[304,512]{1,0:T(8,128)(2,1)S(1)}, u32[]{:S(2)}, u32[]{:S(2)}) collective-permute-start(bf16[304,512]{1,0:T(8,128)(2,1)S(1)} %collective-permute-done.refs_1_), channel_id=1, source_target_pairs={{0,7},{1,0},{2,1},{3,2},{4,3},{5,4},{6,5},{7,6},{8,15},{9,8},{10,9... | collective-permute-start | bytes 933896 | tf_op jit(solution)/shard_map/ppermute | solution.py:181
  36.0 1.9 %collective-permute-start.2 = (bf16[304,512]{1,0:T(8,128)(2,1)S(1)}, bf16[304,512]{1,0:T(8,128)(2,1)S(1)}, u32[]{:S(2)}, u32[]{:S(2)}) collective-permute-start(bf16[304,512]{1,0:T(8,128)(2,1)S(1)} %collective-permute-done.refs_1_), channel_id=1, source_target_pairs={{0,1},{1,2},{2,3},{3,4},{4,5},{5,6},{6,7},{7,0},{8,9},{9,10},{10,1... | collective-permute-start | bytes 933896 | tf_op jit(solution)/shard_map/ppermute | solution.py:181
  37.9 0.0 collective-permute-done.3.refs_4_
  37.9 0.0 copy-start.5
  37.9 4.6 %collective-permute-start.7 = (bf16[304,512]{1,0:T(8,128)(2,1)S(1)}, bf16[304,512]{1,0:T(8,128)(2,1)S(1)}, u32[]{:S(2)}, u32[]{:S(2)}) collective-permute-start(bf16[304,512]{1,0:T(8,128)(2,1)S(1)} %collective-permute-done.3.refs_4_), channel_id=1, source_target_pairs={{0,7},{1,0},{2,1},{3,2},{4,3},{5,4},{6,5},{7,6},{8,15},{9,8},{10,9... | collective-permute-start | bytes 933896 | tf_op jit(solution)/shard_map/ppermute | solution.py:181
  42.5 0.0 collective-permute-done.5.refs_6_
  42.5 0.0 copy-start.6
  42.5 1.9 %collective-permute-start.9 = (bf16[304,512]{1,0:T(8,128)(2,1)S(1)}, bf16[304,512]{1,0:T(8,128)(2,1)S(1)}, u32[]{:S(2)}, u32[]{:S(2)}) collective-permute-start(bf16[304,512]{1,0:T(8,128)(2,1)S(1)} %collective-permute-done.5.refs_6_), channel_id=1, source_target_pairs={{0,1},{1,2},{2,3},{3,4},{4,5},{5,6},{6,7},{7,0},{8,9},{9,10},{10,1... | collective-permute-start | bytes 933896 | tf_op jit(solution)/shard_map/ppermute | solution.py:181
  44.4 0.0 collective-permute-done.4.refs_5_
  44.4 0.0 copy-start.7
  44.5 4.6 %collective-permute-start.8 = (bf16[304,512]{1,0:T(8,128)(2,1)S(1)}, bf16[304,512]{1,0:T(8,128)(2,1)S(1)}, u32[]{:S(2)}, u32[]{:S(2)}) collective-permute-start(bf16[304,512]{1,0:T(8,128)(2,1)S(1)} %collective-permute-done.4.refs_5_), channel_id=1, source_target_pairs={{0,7},{1,0},{2,1},{3,2},{4,3},{5,4},{6,5},{7,6},{8,15},{9,8},{10,9... | collective-permute-start | bytes 933896 | tf_op jit(solution)/shard_map/ppermute | solution.py:181
  49.0 0.0 collective-permute-done.2.refs_3_
  49.0 0.0 copy-start.8
  49.1 1.9 %collective-permute-start.6 = (bf16[304,512]{1,0:T(8,128)(2,1)S(1)}, bf16[304,512]{1,0:T(8,128)(2,1)S(1)}, u32[]{:S(2)}, u32[]{:S(2)}) collective-permute-start(bf16[304,512]{1,0:T(8,128)(2,1)S(1)} %collective-permute-done.2.refs_3_), channel_id=1, source_target_pairs={{0,1},{1,2},{2,3},{3,4},{4,5},{5,6},{6,7},{7,0},{8,9},{9,10},{10,1... | collective-permute-start | bytes 933896 | tf_op jit(solution)/shard_map/ppermute | solution.py:181
  51.0 0.0 collective-permute-done.7.refs_8_
  51.0 0.0 copy-start.9
  51.0 4.6 %collective-permute-start.11 = (bf16[304,512]{1,0:T(8,128)(2,1)S(1)}, bf16[304,512]{1,0:T(8,128)(2,1)S(1)}, u32[]{:S(2)}, u32[]{:S(2)}) collective-permute-start(bf16[304,512]{1,0:T(8,128)(2,1)S(1)} %collective-permute-done.7.refs_8_), channel_id=1, source_target_pairs={{0,7},{1,0},{2,1},{3,2},{4,3},{5,4},{6,5},{7,6},{8,15},{9,8},{10,9... | collective-permute-start | bytes 933896 | tf_op jit(solution)/shard_map/ppermute | solution.py:181
  55.6 0.0 collective-permute-done.9.refs_10_
  55.6 0.0 copy-start.10
  55.6 1.9 %collective-permute-start.10 = (bf16[304,512]{1,0:T(8,128)(2,1)S(1)}, bf16[304,512]{1,0:T(8,128)(2,1)}, u32[]{:S(2)}, u32[]{:S(2)}) collective-permute-start(bf16[304,512]{1,0:T(8,128)(2,1)S(1)} %collective-permute-done.9.refs_10_), channel_id=1, source_target_pairs={{0,1},{1,2},{2,3},{3,4},{4,5},{5,6},{6,7},{7,0},{8,9},{9,10},{10,1... | collective-permute-start | bytes 933896 | tf_op jit(solution)/shard_map/ppermute | solution.py:181
  57.5 0.0 collective-permute-done.8.refs_9_
  57.5 0.0 copy-start.11
  57.6 4.6 %collective-permute-start.13 = (bf16[304,512]{1,0:T(8,128)(2,1)S(1)}, bf16[304,512]{1,0:T(8,128)(2,1)S(1)}, u32[]{:S(2)}, u32[]{:S(2)}) collective-permute-start(bf16[304,512]{1,0:T(8,128)(2,1)S(1)} %collective-permute-done.8.refs_9_), channel_id=1, source_target_pairs={{0,7},{1,0},{2,1},{3,2},{4,3},{5,4},{6,5},{7,6},{8,15},{9,8},{10,9... | collective-permute-start | bytes 933896 | tf_op jit(solution)/shard_map/ppermute | solution.py:181
  62.1 0.0 collective-permute-done.6.refs_7_
  62.2 0.0 copy-start.12
  62.2 1.9 %collective-permute-start.12 = (bf16[304,512]{1,0:T(8,128)(2,1)S(1)}, bf16[304,512]{1,0:T(8,128)(2,1)}, u32[]{:S(2)}, u32[]{:S(2)}) collective-permute-start(bf16[304,512]{1,0:T(8,128)(2,1)S(1)} %collective-permute-done.6.refs_7_), channel_id=1, source_target_pairs={{0,1},{1,2},{2,3},{3,4},{4,5},{5,6},{6,7},{7,0},{8,9},{9,10},{10,1... | collective-permute-start | bytes 933896 | tf_op jit(solution)/shard_map/ppermute | solution.py:181
  64.1 0.0 collective-permute-done.11.refs_12_
  64.1 0.0 copy-start.13
  64.1 1.2 %collective-permute-done.10.refs_14_ = bf16[304,512]{1,0:T(8,128)(2,1)} collective-permute-done((bf16[304,512]{1,0:T(8,128)(2,1)S(1)}, bf16[304,512]{1,0:T(8,128)(2,1)}, u32[]{:S(2)}, u32[]{:S(2)}) %collective-permute-start.10) | collective-permute-done | bytes 311328 | tf_op jit(solution)/shard_map/ppermute | solution.py:181
  65.3 1.4 %collective-permute-done.13.refs_13_ = bf16[304,512]{1,0:T(8,128)(2,1)S(1)} collective-permute-done((bf16[304,512]{1,0:T(8,128)(2,1)S(1)}, bf16[304,512]{1,0:T(8,128)(2,1)S(1)}, u32[]{:S(2)}, u32[]{:S(2)}) %collective-permute-start.13) | collective-permute-done | bytes 311328 | tf_op jit(solution)/shard_map/ppermute | solution.py:181
  66.7 0.0 copy-done.5
  66.7 0.0 copy-done.6
  66.7 0.0 copy-done.7
  66.7 0.0 copy-done.8
  66.7 0.0 copy-done.10
  66.7 0.0 copy-done.11
  66.7 0.0 copy-done.12
  66.8 0.0 copy-done.13
  66.8 0.0 copy-start.14
  66.8 0.7 copy-done.14
  67.5 4.8 %collective-permute-done.12.refs_11_ = bf16[304,512]{1,0:T(8,128)(2,1)} collective-permute-done((bf16[304,512]{1,0:T(8,128)(2,1)S(1)}, bf16[304,512]{1,0:T(8,128)(2,1)}, u32[]{:S(2)}, u32[]{:S(2)}) %collective-permute-start.12) | collective-permute-done | bytes 311328 | tf_op jit(solution)/shard_map/ppermute | solution.py:181
  72.3 4.1 %all-to-all-done.refs_16_ = bf16[16,152,512]{2,1,0:T(8,128)(2,1)S(1)} async-done(((bf16[16,152,512]{2,1,0:T(8,128)(2,1)}), bf16[16,152,512]{2,1,0:T(8,128)(2,1)S(1)}, u32[]{:S(2)}, u32[]{:S(2)}) %all-to-all-start) | async-done | bytes 2490400 | tf_op jit(solution)/shard_map/all_to_all | solution.py:195
  76.5 4.2 %collective-permute-start.15 = (bf16[16,152,512]{2,1,0:T(8,128)(2,1)S(1)}, bf16[16,152,512]{2,1,0:T(8,128)(2,1)S(1)}, u32[]{:S(2)}, u32[]{:S(2)}) collective-permute-start(bf16[16,152,512]{2,1,0:T(8,128)(2,1)S(1)} %all-to-all-done.refs_16_), channel_id=1, source_target_pairs={{0,16},{16,0},{1,17},{17,1},{2,18},{18,2},{3,19},{19,3},{4,20},{20... | collective-permute-start | bytes 7471112 | tf_op jit(solution)/shard_map/ppermute | solution.py:181
  80.7 2.2 %collective-permute-start.14 = (bf16[304,512]{1,0:T(8,128)(2,1)}, bf16[304,512]{1,0:T(8,128)(2,1)S(1)}, u32[]{:S(2)}, u32[]{:S(2)}) collective-permute-start(bf16[304,512]{1,0:T(8,128)(2,1)} %collective-permute-done.10.refs_14_), channel_id=1, source_target_pairs={{0,8},{8,0},{1,9},{9,1},{2,10},{10,2},{3,11},{11,3},{4,12},{12,4},... | collective-permute-start | bytes 933896 | tf_op jit(solution)/shard_map/ppermute | solution.py:181
  82.9 8.9 %collective-permute-done.14.refs_15_ = bf16[304,512]{1,0:T(8,128)(2,1)S(1)} collective-permute-done((bf16[304,512]{1,0:T(8,128)(2,1)}, bf16[304,512]{1,0:T(8,128)(2,1)S(1)}, u32[]{:S(2)}, u32[]{:S(2)}) %collective-permute-start.14) | collective-permute-done | bytes 311328 | tf_op jit(solution)/shard_map/ppermute | solution.py:181
  91.8 0.0 collective-permute-done.15.refs_17_
  91.8 1.5 %copy-done.1 = bf16[16,152,512]{2,1,0:T(8,128)(2,1)} copy-done((bf16[16,152,512]{2,1,0:T(8,128)(2,1)}, bf16[16,152,512]{2,1,0:T(8,128)(2,1)S(1)}, u32[]{:S(2)}) %copy-start.1) | copy-done | bytes 2490392
  93.3 0.0 copy-done.3
  93.3 0.0 copy-done.4
  93.3 0.0 copy-done.9
  93.3 0.0 copy-done
  93.3 0.0 copy-done.15
  93.3 9.0 %shard_map.65 = f32[512,1024]{1,0:T(8,128)} custom-call(s32[2,8]{1,0:T(2,128)} %bitcast.3, s32[4]{0:T(128)} %down_ref.3, bf16[304,512]{1,0:T(8,128)(2,1)} %get-tuple-element.13.refs_0_, bf16[304,512]{1,0:T(8,128)(2,1)} %copy-done.4, bf16[304,512]{1,0:T(8,128)(2,1)} %copy-done.3, bf16[304,512]{1,0:T(8,128)(2,1)} %copy-done.8, bf16[304,512]{1,0:T(8,128)(2,1)} %copy-done.5, ...), custom_call_target="tpu_custom_call" | custom-call | tf_op jit(solution)/shard_map/pallas_call | solution.py:156
  (4 shorter events, 0.0 us)
Async XLA Ops:
  4.0 13.6 %copy-start.2 = (bf16[304,512]{1,0:T(8,128)(2,1)S(1)}, bf16[304,512]{1,0:T(8,128)(2,1)}, u32[]{:S(2)}) copy-start(bf16[304,512]{1,0:T(8,128)(2,1)} %get-tuple-element.13.refs_0_) | copy-start | bytes 933892
  4.0 72.5 %all-to-all-start = ((bf16[16,152,512]{2,1,0:T(8,128)(2,1)}), bf16[16,152,512]{2,1,0:T(8,128)(2,1)S(1)}, u32[]{:S(2)}, u32[]{:S(2)}) async-start(bf16[16,152,512]{2,1,0:T(8,128)(2,1)} %get-tuple-element.14), calls=%async_computation | async-start | bytes 4980736 | tf_op jit(solution)/shard_map/all_to_all | solution.py:195
  17.6 11.9 %collective-permute-start.1 = (bf16[304,512]{1,0:T(8,128)(2,1)S(1)}, bf16[304,512]{1,0:T(8,128)(2,1)S(1)}, u32[]{:S(2)}, u32[]{:S(2)}) collective-permute-start(bf16[304,512]{1,0:T(8,128)(2,1)S(1)} %copy-done.2), channel_id=1, source_target_pairs={{0,1},{1,2},{2,3},{3,4},{4,5},{5,6},{6,7},{7,0},{8,9},{9,10},{10,1... | collective-permute-start | bytes 933896 | tf_op jit(solution)/shard_map/ppermute | solution.py:181
  20.8 10.6 %collective-permute-start = (bf16[304,512]{1,0:T(8,128)(2,1)S(1)}, bf16[304,512]{1,0:T(8,128)(2,1)S(1)}, u32[]{:S(2)}, u32[]{:S(2)}) collective-permute-start(bf16[304,512]{1,0:T(8,128)(2,1)S(1)} %copy-done.2), channel_id=1, source_target_pairs={{0,8},{8,0},{1,9},{9,1},{2,10},{10,2},{3,11},{11,3},{4,12},{12,4},... | collective-permute-start | bytes 933896 | tf_op jit(solution)/shard_map/ppermute | solution.py:181
  23.0 14.9 %collective-permute-start.3 = (bf16[304,512]{1,0:T(8,128)(2,1)S(1)}, bf16[304,512]{1,0:T(8,128)(2,1)S(1)}, u32[]{:S(2)}, u32[]{:S(2)}) collective-permute-start(bf16[304,512]{1,0:T(8,128)(2,1)S(1)} %copy-done.2), channel_id=1, source_target_pairs={{0,7},{1,0},{2,1},{3,2},{4,3},{5,4},{6,5},{7,6},{8,15},{9,8},{10,9... | collective-permute-start | bytes 933896 | tf_op jit(solution)/shard_map/ppermute | solution.py:181
  29.4 63.8 %copy-start.3 = (bf16[304,512]{1,0:T(8,128)(2,1)}, bf16[304,512]{1,0:T(8,128)(2,1)S(1)}, u32[]{:S(2)}) copy-start(bf16[304,512]{1,0:T(8,128)(2,1)S(1)} %collective-permute-done.1.refs_2_) | copy-start | bytes 933892
  29.4 13.1 %collective-permute-start.5 = (bf16[304,512]{1,0:T(8,128)(2,1)S(1)}, bf16[304,512]{1,0:T(8,128)(2,1)S(1)}, u32[]{:S(2)}, u32[]{:S(2)}) collective-permute-start(bf16[304,512]{1,0:T(8,128)(2,1)S(1)} %collective-permute-done.1.refs_2_), channel_id=1, source_target_pairs={{0,1},{1,2},{2,3},{3,4},{4,5},{5,6},{6,7},{7,0},{8,9},{9,10},{10,1... | collective-permute-start | bytes 933896 | tf_op jit(solution)/shard_map/ppermute | solution.py:181
  31.4 61.9 %copy-start.4 = (bf16[304,512]{1,0:T(8,128)(2,1)}, bf16[304,512]{1,0:T(8,128)(2,1)S(1)}, u32[]{:S(2)}) copy-start(bf16[304,512]{1,0:T(8,128)(2,1)S(1)} %collective-permute-done.refs_1_) | copy-start | bytes 933892
  31.4 13.1 %collective-permute-start.4 = (bf16[304,512]{1,0:T(8,128)(2,1)S(1)}, bf16[304,512]{1,0:T(8,128)(2,1)S(1)}, u32[]{:S(2)}, u32[]{:S(2)}) collective-permute-start(bf16[304,512]{1,0:T(8,128)(2,1)S(1)} %collective-permute-done.refs_1_), channel_id=1, source_target_pairs={{0,7},{1,0},{2,1},{3,2},{4,3},{5,4},{6,5},{7,6},{8,15},{9,8},{10,9... | collective-permute-start | bytes 933896 | tf_op jit(solution)/shard_map/ppermute | solution.py:181
  36.0 13.1 %collective-permute-start.2 = (bf16[304,512]{1,0:T(8,128)(2,1)S(1)}, bf16[304,512]{1,0:T(8,128)(2,1)S(1)}, u32[]{:S(2)}, u32[]{:S(2)}) collective-permute-start(bf16[304,512]{1,0:T(8,128)(2,1)S(1)} %collective-permute-done.refs_1_), channel_id=1, source_target_pairs={{0,1},{1,2},{2,3},{3,4},{4,5},{5,6},{6,7},{7,0},{8,9},{9,10},{10,1... | collective-permute-start | bytes 933896 | tf_op jit(solution)/shard_map/ppermute | solution.py:181
  37.9 28.8 %copy-start.5 = (bf16[304,512]{1,0:T(8,128)(2,1)}, bf16[304,512]{1,0:T(8,128)(2,1)S(1)}, u32[]{:S(2)}) copy-start(bf16[304,512]{1,0:T(8,128)(2,1)S(1)} %collective-permute-done.3.refs_4_) | copy-start | bytes 933892
  37.9 13.1 %collective-permute-start.7 = (bf16[304,512]{1,0:T(8,128)(2,1)S(1)}, bf16[304,512]{1,0:T(8,128)(2,1)S(1)}, u32[]{:S(2)}, u32[]{:S(2)}) collective-permute-start(bf16[304,512]{1,0:T(8,128)(2,1)S(1)} %collective-permute-done.3.refs_4_), channel_id=1, source_target_pairs={{0,7},{1,0},{2,1},{3,2},{4,3},{5,4},{6,5},{7,6},{8,15},{9,8},{10,9... | collective-permute-start | bytes 933896 | tf_op jit(solution)/shard_map/ppermute | solution.py:181
  42.5 24.2 %copy-start.6 = (bf16[304,512]{1,0:T(8,128)(2,1)}, bf16[304,512]{1,0:T(8,128)(2,1)S(1)}, u32[]{:S(2)}) copy-start(bf16[304,512]{1,0:T(8,128)(2,1)S(1)} %collective-permute-done.5.refs_6_) | copy-start | bytes 933892
  42.5 13.1 %collective-permute-start.9 = (bf16[304,512]{1,0:T(8,128)(2,1)S(1)}, bf16[304,512]{1,0:T(8,128)(2,1)S(1)}, u32[]{:S(2)}, u32[]{:S(2)}) collective-permute-start(bf16[304,512]{1,0:T(8,128)(2,1)S(1)} %collective-permute-done.5.refs_6_), channel_id=1, source_target_pairs={{0,1},{1,2},{2,3},{3,4},{4,5},{5,6},{6,7},{7,0},{8,9},{9,10},{10,1... | collective-permute-start | bytes 933896 | tf_op jit(solution)/shard_map/ppermute | solution.py:181
  44.4 22.3 %copy-start.7 = (bf16[304,512]{1,0:T(8,128)(2,1)}, bf16[304,512]{1,0:T(8,128)(2,1)S(1)}, u32[]{:S(2)}) copy-start(bf16[304,512]{1,0:T(8,128)(2,1)S(1)} %collective-permute-done.4.refs_5_) | copy-start | bytes 933892
  44.5 13.1 %collective-permute-start.8 = (bf16[304,512]{1,0:T(8,128)(2,1)S(1)}, bf16[304,512]{1,0:T(8,128)(2,1)S(1)}, u32[]{:S(2)}, u32[]{:S(2)}) collective-permute-start(bf16[304,512]{1,0:T(8,128)(2,1)S(1)} %collective-permute-done.4.refs_5_), channel_id=1, source_target_pairs={{0,7},{1,0},{2,1},{3,2},{4,3},{5,4},{6,5},{7,6},{8,15},{9,8},{10,9... | collective-permute-start | bytes 933896 | tf_op jit(solution)/shard_map/ppermute | solution.py:181
  49.0 17.7 %copy-start.8 = (bf16[304,512]{1,0:T(8,128)(2,1)}, bf16[304,512]{1,0:T(8,128)(2,1)S(1)}, u32[]{:S(2)}) copy-start(bf16[304,512]{1,0:T(8,128)(2,1)S(1)} %collective-permute-done.2.refs_3_) | copy-start | bytes 933892
  49.1 13.1 %collective-permute-start.6 = (bf16[304,512]{1,0:T(8,128)(2,1)S(1)}, bf16[304,512]{1,0:T(8,128)(2,1)S(1)}, u32[]{:S(2)}, u32[]{:S(2)}) collective-permute-start(bf16[304,512]{1,0:T(8,128)(2,1)S(1)} %collective-permute-done.2.refs_3_), channel_id=1, source_target_pairs={{0,1},{1,2},{2,3},{3,4},{4,5},{5,6},{6,7},{7,0},{8,9},{9,10},{10,1... | collective-permute-start | bytes 933896 | tf_op jit(solution)/shard_map/ppermute | solution.py:181
  51.0 42.3 %copy-start.9 = (bf16[304,512]{1,0:T(8,128)(2,1)}, bf16[304,512]{1,0:T(8,128)(2,1)S(1)}, u32[]{:S(2)}) copy-start(bf16[304,512]{1,0:T(8,128)(2,1)S(1)} %collective-permute-done.7.refs_8_) | copy-start | bytes 933892
  51.0 13.1 %collective-permute-start.11 = (bf16[304,512]{1,0:T(8,128)(2,1)S(1)}, bf16[304,512]{1,0:T(8,128)(2,1)S(1)}, u32[]{:S(2)}, u32[]{:S(2)}) collective-permute-start(bf16[304,512]{1,0:T(8,128)(2,1)S(1)} %collective-permute-done.7.refs_8_), channel_id=1, source_target_pairs={{0,7},{1,0},{2,1},{3,2},{4,3},{5,4},{6,5},{7,6},{8,15},{9,8},{10,9... | collective-permute-start | bytes 933896 | tf_op jit(solution)/shard_map/ppermute | solution.py:181
  55.6 11.1 %copy-start.10 = (bf16[304,512]{1,0:T(8,128)(2,1)}, bf16[304,512]{1,0:T(8,128)(2,1)S(1)}, u32[]{:S(2)}) copy-start(bf16[304,512]{1,0:T(8,128)(2,1)S(1)} %collective-permute-done.9.refs_10_) | copy-start | bytes 933892
  55.6 9.7 %collective-permute-start.10 = (bf16[304,512]{1,0:T(8,128)(2,1)S(1)}, bf16[304,512]{1,0:T(8,128)(2,1)}, u32[]{:S(2)}, u32[]{:S(2)}) collective-permute-start(bf16[304,512]{1,0:T(8,128)(2,1)S(1)} %collective-permute-done.9.refs_10_), channel_id=1, source_target_pairs={{0,1},{1,2},{2,3},{3,4},{4,5},{5,6},{6,7},{7,0},{8,9},{9,10},{10,1... | collective-permute-start | bytes 933896 | tf_op jit(solution)/shard_map/ppermute | solution.py:181
  57.5 9.2 %copy-start.11 = (bf16[304,512]{1,0:T(8,128)(2,1)}, bf16[304,512]{1,0:T(8,128)(2,1)S(1)}, u32[]{:S(2)}) copy-start(bf16[304,512]{1,0:T(8,128)(2,1)S(1)} %collective-permute-done.8.refs_9_) | copy-start | bytes 933892
  57.6 9.2 %collective-permute-start.13 = (bf16[304,512]{1,0:T(8,128)(2,1)S(1)}, bf16[304,512]{1,0:T(8,128)(2,1)S(1)}, u32[]{:S(2)}, u32[]{:S(2)}) collective-permute-start(bf16[304,512]{1,0:T(8,128)(2,1)S(1)} %collective-permute-done.8.refs_9_), channel_id=1, source_target_pairs={{0,7},{1,0},{2,1},{3,2},{4,3},{5,4},{6,5},{7,6},{8,15},{9,8},{10,9... | collective-permute-start | bytes 933896 | tf_op jit(solution)/shard_map/ppermute | solution.py:181
  62.2 4.6 %copy-start.12 = (bf16[304,512]{1,0:T(8,128)(2,1)}, bf16[304,512]{1,0:T(8,128)(2,1)S(1)}, u32[]{:S(2)}) copy-start(bf16[304,512]{1,0:T(8,128)(2,1)S(1)} %collective-permute-done.6.refs_7_) | copy-start | bytes 933892
  62.2 10.2 %collective-permute-start.12 = (bf16[304,512]{1,0:T(8,128)(2,1)S(1)}, bf16[304,512]{1,0:T(8,128)(2,1)}, u32[]{:S(2)}, u32[]{:S(2)}) collective-permute-start(bf16[304,512]{1,0:T(8,128)(2,1)S(1)} %collective-permute-done.6.refs_7_), channel_id=1, source_target_pairs={{0,1},{1,2},{2,3},{3,4},{4,5},{5,6},{6,7},{7,0},{8,9},{9,10},{10,1... | collective-permute-start | bytes 933896 | tf_op jit(solution)/shard_map/ppermute | solution.py:181
  64.1 2.7 %copy-start.13 = (bf16[304,512]{1,0:T(8,128)(2,1)}, bf16[304,512]{1,0:T(8,128)(2,1)S(1)}, u32[]{:S(2)}) copy-start(bf16[304,512]{1,0:T(8,128)(2,1)S(1)} %collective-permute-done.11.refs_12_) | copy-start | bytes 933892
  66.8 0.7 copy-start.14
  76.4 16.8 %copy-start = (bf16[16,152,512]{2,1,0:T(8,128)(2,1)}, bf16[16,152,512]{2,1,0:T(8,128)(2,1)S(1)}, u32[]{:S(2)}) copy-start(bf16[16,152,512]{2,1,0:T(8,128)(2,1)S(1)} %all-to-all-done.refs_16_) | copy-start | bytes 7471108
  76.5 15.3 %collective-permute-start.15 = (bf16[16,152,512]{2,1,0:T(8,128)(2,1)S(1)}, bf16[16,152,512]{2,1,0:T(8,128)(2,1)S(1)}, u32[]{:S(2)}, u32[]{:S(2)}) collective-permute-start(bf16[16,152,512]{2,1,0:T(8,128)(2,1)S(1)} %all-to-all-done.refs_16_), channel_id=1, source_target_pairs={{0,16},{16,0},{1,17},{17,1},{2,18},{18,2},{3,19},{19,3},{4,20},{20... | collective-permute-start | bytes 7471112 | tf_op jit(solution)/shard_map/ppermute | solution.py:181
  80.7 11.1 %collective-permute-start.14 = (bf16[304,512]{1,0:T(8,128)(2,1)}, bf16[304,512]{1,0:T(8,128)(2,1)S(1)}, u32[]{:S(2)}, u32[]{:S(2)}) collective-permute-start(bf16[304,512]{1,0:T(8,128)(2,1)} %collective-permute-done.10.refs_14_), channel_id=1, source_target_pairs={{0,8},{8,0},{1,9},{9,1},{2,10},{10,2},{3,11},{11,3},{4,12},{12,4},... | collective-permute-start | bytes 933896 | tf_op jit(solution)/shard_map/ppermute | solution.py:181
  91.8 1.6 %copy-start.15 = (bf16[304,512]{1,0:T(8,128)(2,1)}, bf16[304,512]{1,0:T(8,128)(2,1)S(1)}, u32[]{:S(2)}) copy-start(bf16[304,512]{1,0:T(8,128)(2,1)S(1)} %collective-permute-done.14.refs_15_) | copy-start | bytes 933892
  91.8 1.5 %copy-start.1 = (bf16[16,152,512]{2,1,0:T(8,128)(2,1)}, bf16[16,152,512]{2,1,0:T(8,128)(2,1)S(1)}, u32[]{:S(2)}) copy-start(bf16[16,152,512]{2,1,0:T(8,128)(2,1)S(1)} %collective-permute-done.15.refs_17_) | copy-start | bytes 7471108

commit v4 on v3

v4 whole, which is shorter than its diff:
```python
import jax
import jax.numpy as jnp
from jax import lax
from jax.experimental import pallas as pl
from jax.experimental.pallas import tpu as pltpu
from jax.sharding import Mesh
from jax.sharding import PartitionSpec as P

UF_DEV = 512
VF_DEV = 1024
BLOCK = 128
DACT = 4
UACT = 2
KD = 288
KE = 144
TD = 16
TE = 8
RD = KD + TD
RE = KE + TE
DOWN = ("xl", "y")
UP = ("z", "xh", "c")
NY = 8
TURNS = (0, -1, 1, -2, 2, -3, 3, 4)
STEP = 4
VMEM = pl.BlockSpec(memory_space=pltpu.VMEM)
SMEM = pl.BlockSpec(memory_space=pltpu.SMEM)
ANY = pl.BlockSpec(memory_space=pl.ANY)


def pack_kernel(down_ref, dec_ref, delta_ref, enc_ref, grad_ref, d_ref, e_ref, active, sems):
    copies = []

    def move(source, target):
        copies.append(pltpu.make_async_copy(source, target, sems.at[len(copies)]))
        copies[-1].start()

    for i in range(DACT):
        cols = pl.ds(pl.multiple_of(down_ref[i] * BLOCK, BLOCK), BLOCK)
        move(enc_ref.at[:, cols], active.at[:KE, i * BLOCK : (i + 1) * BLOCK])
        move(grad_ref.at[:, cols], active.at[KE:, i * BLOCK : (i + 1) * BLOCK])
    loads = len(copies)
    move(dec_ref, d_ref.at[:KD])
    move(delta_ref, d_ref.at[KD:])
    for copy in copies[:loads]:
        copy.wait()
    for n in range(2 * NY):
        move(active, e_ref.at[n])
    for copy in copies[loads:]:
        copy.wait()


def pack(down_blocks, dec_t, deltas, encoder, gradients):
    return pl.pallas_call(
        pack_kernel,
        out_shape=(
            jax.ShapeDtypeStruct((RD, UF_DEV), jnp.bfloat16),
            jax.ShapeDtypeStruct((2 * NY, RE, DACT * BLOCK), jnp.bfloat16),
        ),
        in_specs=[SMEM, ANY, ANY, ANY, ANY],
        out_specs=(VMEM, ANY),
        scratch_shapes=[
            pltpu.VMEM((RE, DACT * BLOCK), jnp.bfloat16),
            pltpu.SemaphoreType.DMA((2 * DACT + 2 + 2 * NY,)),
        ],
        compiler_params=pltpu.CompilerParams(vmem_limit_bytes=60 << 20),
    )(down_blocks, dec_t, deltas, encoder, gradients)


def accumulate(part, up_ref, shards, source, held, sems):
    dec, tok, enc, grad = held
    dec_sem, tok_sem, enc_sem, grad_sem = sems
    y, xl = lax.axis_index("y"), lax.axis_index("xl")
    rows = pl.ds(pl.multiple_of(part * KE, 16), KE)
    tokens = pl.ds(pl.multiple_of(KD + part * TE, TE), TE)
    rest = [pltpu.make_async_copy(source.at[:, KE:], grad, grad_sem)]
    blocks = []
    for slot, shard in enumerate(shards):
        column = xl if slot % 2 == 0 else 1 - xl
        k = column * NY + lax.rem(y + TURNS[slot // 2] + NY, NY)
        blocks.append(
            (
                pltpu.make_async_copy(shard.at[rows], dec.at[slot], dec_sem.at[slot]),
                pltpu.make_async_copy(source.at[k, :KE], enc.at[slot], enc_sem.at[slot]),
            )
        )
        rest.append(pltpu.make_async_copy(shard.at[tokens], tok.at[k], tok_sem.at[slot]))
        for copy in blocks[slot]:
            copy.start()
    for copy in rest:
        copy.start()
    dims = (((0,), (0,)), ((), ()))
    cols = DACT * BLOCK
    virtual = None
    for low in range(0, 2 * NY, STEP):
        for slot in range(low, low + STEP):
            for copy in blocks[slot]:
                copy.wait()
        term = lax.dot_general(
            dec[low : low + STEP].reshape(STEP * KE, UF_DEV),
            enc[low : low + STEP].reshape(STEP * KE, cols),
            dims,
            preferred_element_type=jnp.float32,
        )
        virtual = term if virtual is None else virtual + term
    for copy in rest:
        copy.wait()
    lane_block = lax.broadcasted_iota(jnp.int32, (2 * TE, UF_DEV), 1) // BLOCK
    masked = []
    for w in range(NY):
        on = (lane_block == up_ref[0, w]) | (lane_block == up_ref[1, w])
        delta = tok[2 * w : 2 * w + 2].astype(jnp.float32).reshape(2 * TE, UF_DEV)
        masked.append(jnp.where(on, delta, 0.0))
    masked = jnp.concatenate(masked, 0).astype(jnp.bfloat16)
    kept = grad[...].astype(jnp.float32).reshape(2 * NY * TE, cols).astype(jnp.bfloat16)
    product = lax.dot_general(masked, kept, dims, preferred_element_type=jnp.float32)
    return virtual, product


def half_kernel(up_ref, *refs):
    shards, (source, virtual_ref, product_ref) = refs[: 2 * NY], refs[2 * NY : 2 * NY + 3]
    held, sems = refs[2 * NY + 3 : 2 * NY + 7], refs[2 * NY + 7 :]
    virtual_ref[...], product_ref[...] = accumulate(
        lax.axis_index("c"), up_ref, shards, source, held, sems
    )


def score_kernel(up_ref, down_ref, *refs):
    shards, refs = refs[: 2 * NY], refs[2 * NY :]
    source, virtual_in, product_in, out_ref = refs[:4]
    held, sems = refs[4:8], refs[8:12]
    virtual, product, zero, scored, in_sem, zero_sem, out_sem = refs[12:]
    zero[...] = jnp.zeros_like(zero)

    def blank(b):
        return pltpu.make_async_copy(
            zero, out_ref.at[:, b * BLOCK : (b + 1) * BLOCK], zero_sem.at[b]
        )

    idle = []
    for b in range(VF_DEV // BLOCK):
        used = down_ref[0] == b
        for i in range(1, DACT):
            used = used | (down_ref[i] == b)
        idle.append(jnp.logical_not(used))
    loads = [
        pltpu.make_async_copy(virtual_in, virtual, in_sem.at[0]),
        pltpu.make_async_copy(product_in, product, in_sem.at[1]),
    ]
    for copy in loads:
        copy.start()
    more, part = accumulate(1 - lax.axis_index("c"), up_ref, shards, source, held, sems)
    for b in range(VF_DEV // BLOCK):
        pl.when(idle[b])(blank(b).start)
    for copy in loads:
        copy.wait()
    filled = []
    for i in range(DACT):
        at = slice(i * BLOCK, (i + 1) * BLOCK)
        scored[i] = (product[:, at] + part[:, at]) * (virtual[:, at] + more[:, at])
        where = pl.ds(pl.multiple_of(down_ref[i] * BLOCK, BLOCK), BLOCK)
        filled.append(
            pltpu.make_async_copy(scored.at[i], out_ref.at[:, where], out_sem.at[i])
        )
        filled[i].start()
    for b in range(VF_DEV // BLOCK):
        pl.when(idle[b])(blank(b).wait)
    for copy in filled:
        copy.wait()


COLS = DACT * BLOCK
HELD = [
    pltpu.VMEM((2 * NY, KE, UF_DEV), jnp.bfloat16),
    pltpu.VMEM((2 * NY, TE, UF_DEV), jnp.bfloat16),
    pltpu.VMEM((2 * NY, KE, COLS), jnp.bfloat16),
    pltpu.VMEM((2 * NY, TE, COLS), jnp.bfloat16),
    pltpu.SemaphoreType.DMA((2 * NY,)),
    pltpu.SemaphoreType.DMA((2 * NY,)),
    pltpu.SemaphoreType.DMA((2 * NY,)),
    pltpu.SemaphoreType.DMA,
]
COST = pl.CostEstimate(
    flops=UF_DEV * COLS * KD * 2 * NY, bytes_accessed=8 << 20, transcendentals=0
)


def half(up_t, shards, source):
    return pl.pallas_call(
        half_kernel,
        out_shape=(jax.ShapeDtypeStruct((UF_DEV, COLS), jnp.float32),) * 2,
        in_specs=[SMEM] + [ANY] * (2 * NY + 1),
        out_specs=(VMEM, VMEM),
        scratch_shapes=HELD,
        compiler_params=pltpu.CompilerParams(vmem_limit_bytes=60 << 20),
        cost_estimate=COST,
    )(up_t, *shards, source)


def score(up_t, down_blocks, shards, source, sums):
    return pl.pallas_call(
        score_kernel,
        out_shape=jax.ShapeDtypeStruct((UF_DEV, VF_DEV), jnp.float32),
        in_specs=[SMEM, SMEM] + [ANY] * (2 * NY + 3),
        out_specs=ANY,
        scratch_shapes=[
            *HELD,
            pltpu.VMEM((UF_DEV, COLS), jnp.float32),
            pltpu.VMEM((UF_DEV, COLS), jnp.float32),
            pltpu.VMEM((UF_DEV, BLOCK), jnp.float32),
            pltpu.VMEM((DACT, UF_DEV, BLOCK), jnp.float32),
            pltpu.SemaphoreType.DMA((2,)),
            pltpu.SemaphoreType.DMA((VF_DEV // BLOCK,)),
            pltpu.SemaphoreType.DMA((DACT,)),
        ],
        compiler_params=pltpu.CompilerParams(vmem_limit_bytes=60 << 20),
        cost_estimate=COST,
    )(up_t, down_blocks, *shards, source, *sums)


def turn(value, axis, by):
    n = lax.axis_size(axis)
    return lax.ppermute(value, axis, [(i, (i + by) % n) for i in range(n)])


def ring(value):
    right = left = value
    held = [value]
    for _ in range(NY // 2 - 1):
        right, left = turn(right, "y", 1), turn(left, "y", -1)
        held += [right, left]
    return held


def local(deltas, gradients, up_blocks, down_blocks, decoder, encoder):
    d, e = pack(down_blocks, decoder.T, deltas, encoder, gradients)
    own = lax.all_to_all(e, ("z", "xh"), 0, 0, tiled=True)
    near = ring(d)
    across = ring(turn(d, "xl", 1))
    far = turn(near[5], "y", 1)
    beyond = turn(far, "xl", 1)
    near, across = near + [far], across + [beyond]
    own, near[5:], across[5:] = lax.optimization_barrier((own, near[5:], across[5:]))
    shards = [shard for both in zip(near, across) for shard in both]
    swapped = turn(own, "c", 1)
    up_t = up_blocks.T
    return score(up_t, down_blocks, shards, swapped, half(up_t, shards, own))


def solution(mesh):
    torus = Mesh(mesh.devices.reshape(8, 2, 2, 2, 8), ("z", "xh", "c", "xl", "y"))
    return jax.shard_map(
        local,
        mesh=torus,
        in_specs=(P(DOWN, UP), P(UP, DOWN), P(None, UP), P(DOWN), P(UP, DOWN), P(UP, DOWN)),
        out_specs=P(UP, DOWN),
        check_vma=False,
    )
```

time: 103 us -> 98.6 us (0.957)
  waiting for transfers between devices: 23 us -> 14.8 us
  Pallas kernels: 12.9 us -> 16.7 us
  starting transfers between devices: 63.6 us -> 65.2 us
  local copies, waits for them, and re-layouts: 2.33 us -> 0.76 us
    pallas_call x0 -> x1, Pallas kernels: none -> 6.34 us  [half(): pl.pallas_call(half_kernel, out_shape=(jax.ShapeDtypeStruct((UF_DEV, COLS...]
    ppermute x16, waiting for transfers between devices: 18.9 us -> 14.8 us  [turn(): return lax.ppermute(value, axis, [(i, (i + by) % n) for i in range(n)])]
    all_to_all x1, waiting for transfers between devices: 4.11 us -> 0.01 us  [local(): own = lax.all_to_all(e, ('z', 'xh'), 0, 0, tiled=True)]
    pallas_call x1, Pallas kernels: 8.95 us -> 6.42 us  [score(): pl.pallas_call(score_kernel, out_shape=jax.ShapeDtypeStruct((UF_DEV, VF_D...]
    unnamed x32, local copies, waits for them, and re-layouts: 2.33 us -> 0.76 us
    ppermute x16, starting transfers between devices: 50.1 us -> 51.6 us  [turn(): return lax.ppermute(value, axis, [(i, (i + by) % n) for i in range(n)])]
  transfers between devices with their start and end apart: 17 -> 17, of which waited for: 6 -> 4; matrix products, arithmetic and copies ran while one was open for 0% -> 0% of each run, Pallas kernels for 0% -> 6%
where the time goes in v4:
time: 98.6 us; the launch traced here: 97.9 us
  starting transfers between devices  65.2 us (66%)
  Pallas kernels  16.7 us (17%)
  waiting for transfers between devices  14.8 us (15%)
    ppermute x16, starting transfers between devices, turn(): return lax.ppermute(value, axis, [(i, (i + by) % n) for i in range(n)])  51.6 us
    ppermute x16, waiting for transfers between devices, turn(): return lax.ppermute(value, axis, [(i, (i + by) % n) for i in range(n)])  14.8 us
    all_to_all x1, starting transfers between devices, local(): own = lax.all_to_all(e, ('z', 'xh'), 0, 0, tiled=True)  13.6 us
    pallas_call x1, Pallas kernels, score(): pl.pallas_call(score_kernel, out_shape=jax.ShapeDtypeStruct((UF_DEV, VF_D...  6.42 us
    pallas_call x1, Pallas kernels, half(): pl.pallas_call(half_kernel, out_shape=(jax.ShapeDtypeStruct((UF_DEV, COLS...  6.34 us
    pallas_call x1, Pallas kernels, pack(): pl.pallas_call(pack_kernel, out_shape=(jax.ShapeDtypeStruct((RD, UF_DEV),...  3.96 us
  transfers between devices with their start and end apart: 17, of which 4 were waited for; matrix products, arithmetic and copies ran while one was open for 0% of the time, Pallas kernels for 6%

profile of v4, /device:TPU:1, one launch (start us, length us, event | category | flops | bytes accessed | tf_op | source)
XLA Modules:
  0.0 97.9 jit_solution(13180839942314994682)
XLA Ops:
  0.0 4.0 %shard_map.64 = (bf16[304,512]{1,0:T(8,128)(2,1)}, bf16[16,152,512]{2,1,0:T(8,128)(2,1)}) custom-call(s32[4]{0:T(128)} %down_ref.3, bf16[288,512]{1,0:T(8,128)(2,1)} %bitcast.2, bf16[16,512]{1,0:T(8,128)(2,1)} %delta_ref.1, bf16[144,1024]{1,0:T(8,128)(2,1)} %enc_ref.1, bf16[8,1024]{1,0:T(8,128)(2,1)} %grad_ref.1), custom_call_target="tpu_custom_call" | custom-call | tf_op jit(solution)/shard_map/pallas_call | solution.py:53
  4.0 0.0 copy-start.1
  4.0 13.6 %all-to-all-start = ((bf16[16,152,512]{2,1,0:T(8,128)(2,1)}), bf16[16,152,512]{2,1,0:T(8,128)(2,1)S(1)}, u32[]{:S(2)}, u32[]{:S(2)}) async-start(bf16[16,152,512]{2,1,0:T(8,128)(2,1)} %get-tuple-element.17), calls=%async_computation | async-start | bytes 4980736 | tf_op jit(solution)/shard_map/all_to_all | solution.py:236
  17.6 0.0 copy-done.1
  17.6 3.2 %collective-permute-start.1 = (bf16[304,512]{1,0:T(8,128)(2,1)S(1)}, bf16[304,512]{1,0:T(8,128)(2,1)S(1)}, u32[]{:S(2)}, u32[]{:S(2)}) collective-permute-start(bf16[304,512]{1,0:T(8,128)(2,1)S(1)} %copy-done.1), channel_id=1, source_target_pairs={{0,1},{1,2},{2,3},{3,4},{4,5},{5,6},{6,7},{7,0},{8,9},{9,10},{10,1... | collective-permute-start | bytes 933896 | tf_op jit(solution)/shard_map/ppermute | solution.py:222
  20.8 2.2 %collective-permute-start = (bf16[304,512]{1,0:T(8,128)(2,1)S(1)}, bf16[304,512]{1,0:T(8,128)(2,1)S(1)}, u32[]{:S(2)}, u32[]{:S(2)}) collective-permute-start(bf16[304,512]{1,0:T(8,128)(2,1)S(1)} %copy-done.1), channel_id=1, source_target_pairs={{0,8},{8,0},{1,9},{9,1},{2,10},{10,2},{3,11},{11,3},{4,12},{12,4},... | collective-permute-start | bytes 933896 | tf_op jit(solution)/shard_map/ppermute | solution.py:222
  23.0 6.4 %collective-permute-done.1.refs_2_ = bf16[304,512]{1,0:T(8,128)(2,1)S(1)} collective-permute-done((bf16[304,512]{1,0:T(8,128)(2,1)S(1)}, bf16[304,512]{1,0:T(8,128)(2,1)S(1)}, u32[]{:S(2)}, u32[]{:S(2)}) %collective-permute-start.1) | collective-permute-done | bytes 311328 | tf_op jit(solution)/shard_map/ppermute | solution.py:222
  29.4 1.9 %collective-permute-start.5 = (bf16[304,512]{1,0:T(8,128)(2,1)S(1)}, bf16[304,512]{1,0:T(8,128)(2,1)S(1)}, u32[]{:S(2)}, u32[]{:S(2)}) collective-permute-start(bf16[304,512]{1,0:T(8,128)(2,1)S(1)} %collective-permute-done.1.refs_2_), channel_id=1, source_target_pairs={{0,1},{1,2},{2,3},{3,4},{4,5},{5,6},{6,7},{7,0},{8,9},{9,10},{10,1... | collective-permute-start | bytes 933896 | tf_op jit(solution)/shard_map/ppermute | solution.py:222
  31.3 4.6 %collective-permute-start.3 = (bf16[304,512]{1,0:T(8,128)(2,1)S(1)}, bf16[304,512]{1,0:T(8,128)(2,1)S(1)}, u32[]{:S(2)}, u32[]{:S(2)}) collective-permute-start(bf16[304,512]{1,0:T(8,128)(2,1)S(1)} %copy-done.1), channel_id=1, source_target_pairs={{0,7},{1,0},{2,1},{3,2},{4,3},{5,4},{6,5},{7,6},{8,15},{9,8},{10,9... | collective-permute-start | bytes 933896 | tf_op jit(solution)/shard_map/ppermute | solution.py:222
  35.9 0.0 collective-permute-done.refs_1_
  35.9 0.0 copy-start.3
  35.9 1.9 %collective-permute-start.2 = (bf16[304,512]{1,0:T(8,128)(2,1)S(1)}, bf16[304,512]{1,0:T(8,128)(2,1)S(1)}, u32[]{:S(2)}, u32[]{:S(2)}) collective-permute-start(bf16[304,512]{1,0:T(8,128)(2,1)S(1)} %collective-permute-done.refs_1_), channel_id=1, source_target_pairs={{0,1},{1,2},{2,3},{3,4},{4,5},{5,6},{6,7},{7,0},{8,9},{9,10},{10,1... | collective-permute-start | bytes 933896 | tf_op jit(solution)/shard_map/ppermute | solution.py:222
  37.9 4.6 %collective-permute-start.4 = (bf16[304,512]{1,0:T(8,128)(2,1)S(1)}, bf16[304,512]{1,0:T(8,128)(2,1)S(1)}, u32[]{:S(2)}, u32[]{:S(2)}) collective-permute-start(bf16[304,512]{1,0:T(8,128)(2,1)S(1)} %collective-permute-done.refs_1_), channel_id=1, source_target_pairs={{0,7},{1,0},{2,1},{3,2},{4,3},{5,4},{6,5},{7,6},{8,15},{9,8},{10,9... | collective-permute-start | bytes 933896 | tf_op jit(solution)/shard_map/ppermute | solution.py:222
  42.5 0.0 collective-permute-done.5.refs_6_
  42.5 0.0 copy-start.4
  42.5 1.9 %collective-permute-start.9 = (bf16[304,512]{1,0:T(8,128)(2,1)S(1)}, bf16[304,512]{1,0:T(8,128)(2,1)S(1)}, u32[]{:S(2)}, u32[]{:S(2)}) collective-permute-start(bf16[304,512]{1,0:T(8,128)(2,1)S(1)} %collective-permute-done.5.refs_6_), channel_id=1, source_target_pairs={{0,1},{1,2},{2,3},{3,4},{4,5},{5,6},{6,7},{7,0},{8,9},{9,10},{10,1... | collective-permute-start | bytes 933896 | tf_op jit(solution)/shard_map/ppermute | solution.py:222
  44.4 0.0 collective-permute-done.3.refs_4_
  44.4 0.0 copy-start.5
  44.4 4.6 %collective-permute-start.7 = (bf16[304,512]{1,0:T(8,128)(2,1)S(1)}, bf16[304,512]{1,0:T(8,128)(2,1)S(1)}, u32[]{:S(2)}, u32[]{:S(2)}) collective-permute-start(bf16[304,512]{1,0:T(8,128)(2,1)S(1)} %collective-permute-done.3.refs_4_), channel_id=1, source_target_pairs={{0,7},{1,0},{2,1},{3,2},{4,3},{5,4},{6,5},{7,6},{8,15},{9,8},{10,9... | collective-permute-start | bytes 933896 | tf_op jit(solution)/shard_map/ppermute | solution.py:222
  49.0 0.0 collective-permute-done.2.refs_3_
  49.0 0.0 copy-start.6
  49.0 1.9 %collective-permute-start.6 = (bf16[304,512]{1,0:T(8,128)(2,1)S(1)}, bf16[304,512]{1,0:T(8,128)(2,1)S(1)}, u32[]{:S(2)}, u32[]{:S(2)}) collective-permute-start(bf16[304,512]{1,0:T(8,128)(2,1)S(1)} %collective-permute-done.2.refs_3_), channel_id=1, source_target_pairs={{0,1},{1,2},{2,3},{3,4},{4,5},{5,6},{6,7},{7,0},{8,9},{9,10},{10,1... | collective-permute-start | bytes 933896 | tf_op jit(solution)/shard_map/ppermute | solution.py:222
  51.0 0.0 collective-permute-done.4.refs_5_
  51.0 0.0 copy-start.7
  51.0 4.6 %collective-permute-start.8 = (bf16[304,512]{1,0:T(8,128)(2,1)S(1)}, bf16[304,512]{1,0:T(8,128)(2,1)S(1)}, u32[]{:S(2)}, u32[]{:S(2)}) collective-permute-start(bf16[304,512]{1,0:T(8,128)(2,1)S(1)} %collective-permute-done.4.refs_5_), channel_id=1, source_target_pairs={{0,7},{1,0},{2,1},{3,2},{4,3},{5,4},{6,5},{7,6},{8,15},{9,8},{10,9... | collective-permute-start | bytes 933896 | tf_op jit(solution)/shard_map/ppermute | solution.py:222
  55.6 0.0 collective-permute-done.9.refs_10_
  55.6 0.0 copy-start.8
  55.6 1.9 %collective-permute-start.11 = (bf16[304,512]{1,0:T(8,128)(2,1)S(1)}, bf16[304,512]{1,0:T(8,128)(2,1)S(1)}, u32[]{:S(2)}, u32[]{:S(2)}) collective-permute-start(bf16[304,512]{1,0:T(8,128)(2,1)S(1)} %collective-permute-done.9.refs_10_), channel_id=1, source_target_pairs={{0,1},{1,2},{2,3},{3,4},{4,5},{5,6},{6,7},{7,0},{8,9},{9,10},{10,1... | collective-permute-start | bytes 933896 | tf_op jit(solution)/shard_map/ppermute | solution.py:222
  57.5 0.0 collective-permute-done.7.refs_8_
  57.5 0.0 copy-start.9
  57.5 4.6 %collective-permute-start.10 = (bf16[304,512]{1,0:T(8,128)(2,1)S(1)}, bf16[304,512]{1,0:T(8,128)(2,1)S(1)}, u32[]{:S(2)}, u32[]{:S(2)}) collective-permute-start(bf16[304,512]{1,0:T(8,128)(2,1)S(1)} %collective-permute-done.7.refs_8_), channel_id=1, source_target_pairs={{0,7},{1,0},{2,1},{3,2},{4,3},{5,4},{6,5},{7,6},{8,15},{9,8},{10,9... | collective-permute-start | bytes 933896 | tf_op jit(solution)/shard_map/ppermute | solution.py:222
  62.1 0.0 collective-permute-done.6.refs_7_
  62.1 0.0 copy-start.10
  62.1 1.9 %collective-permute-start.12 = (bf16[304,512]{1,0:T(8,128)(2,1)S(1)}, bf16[304,512]{1,0:T(8,128)(2,1)S(1)}, u32[]{:S(2)}, u32[]{:S(2)}) collective-permute-start(bf16[304,512]{1,0:T(8,128)(2,1)S(1)} %collective-permute-done.6.refs_7_), channel_id=1, source_target_pairs={{0,1},{1,2},{2,3},{3,4},{4,5},{5,6},{6,7},{7,0},{8,9},{9,10},{10,1... | collective-permute-start | bytes 933896 | tf_op jit(solution)/shard_map/ppermute | solution.py:222
  64.1 0.0 collective-permute-done.8.refs_9_
  64.1 0.0 copy-start.11
  64.1 4.6 %collective-permute-start.13 = (bf16[304,512]{1,0:T(8,128)(2,1)S(1)}, bf16[304,512]{1,0:T(8,128)(2,1)S(1)}, u32[]{:S(2)}, u32[]{:S(2)}) collective-permute-start(bf16[304,512]{1,0:T(8,128)(2,1)S(1)} %collective-permute-done.8.refs_9_), channel_id=1, source_target_pairs={{0,7},{1,0},{2,1},{3,2},{4,3},{5,4},{6,5},{7,6},{8,15},{9,8},{10,9... | collective-permute-start | bytes 933896 | tf_op jit(solution)/shard_map/ppermute | solution.py:222
  68.7 0.0 collective-permute-done.11.refs_14_
  68.7 0.0 copy-start.12
  68.7 2.2 %collective-permute-start.14 = (bf16[304,512]{1,0:T(8,128)(2,1)S(1)}, bf16[304,512]{1,0:T(8,128)(2,1)}, u32[]{:S(2)}, u32[]{:S(2)}) collective-permute-start(bf16[304,512]{1,0:T(8,128)(2,1)S(1)} %collective-permute-done.11.refs_14_), channel_id=1, source_target_pairs={{0,8},{8,0},{1,9},{9,1},{2,10},{10,2},{3,11},{11,3},{4,12},{12,4},... | collective-permute-start | bytes 933896 | tf_op jit(solution)/shard_map/ppermute | solution.py:222
  70.9 0.0 collective-permute-done.10.refs_12_
  70.9 0.0 copy-start.13
  70.9 1.4 %collective-permute-done.12.refs_11_ = bf16[304,512]{1,0:T(8,128)(2,1)S(1)} collective-permute-done((bf16[304,512]{1,0:T(8,128)(2,1)S(1)}, bf16[304,512]{1,0:T(8,128)(2,1)S(1)}, u32[]{:S(2)}, u32[]{:S(2)}) %collective-permute-start.12) | collective-permute-done | bytes 311328 | tf_op jit(solution)/shard_map/ppermute | solution.py:222
  72.3 1.5 %collective-permute-done.13.refs_13_ = bf16[304,512]{1,0:T(8,128)(2,1)S(1)} collective-permute-done((bf16[304,512]{1,0:T(8,128)(2,1)S(1)}, bf16[304,512]{1,0:T(8,128)(2,1)S(1)}, u32[]{:S(2)}, u32[]{:S(2)}) %collective-permute-start.13) | collective-permute-done | bytes 311328 | tf_op jit(solution)/shard_map/ppermute | solution.py:222
  73.8 0.0 copy-done.4
  73.8 0.0 copy-done.5
  73.8 0.0 copy-done.6
  73.8 0.0 copy-done.7
  73.8 0.0 copy-done.8
  73.8 0.0 copy-done.10
  73.8 0.0 copy-done.11
  73.8 0.0 copy-done.12
  73.8 0.0 copy-done.13
  73.9 0.0 copy-done.14
  73.9 0.0 copy-start.15
  73.9 0.7 copy-done.15
  74.6 5.5 %collective-permute-done.14.refs_15_ = bf16[304,512]{1,0:T(8,128)(2,1)} collective-permute-done((bf16[304,512]{1,0:T(8,128)(2,1)S(1)}, bf16[304,512]{1,0:T(8,128)(2,1)}, u32[]{:S(2)}, u32[]{:S(2)}) %collective-permute-start.14) | collective-permute-done | bytes 311328 | tf_op jit(solution)/shard_map/ppermute | solution.py:222
  80.1 0.0 all-to-all-done.refs_16_
  80.1 5.0 %collective-permute-start.15 = (bf16[16,152,512]{2,1,0:T(8,128)(2,1)S(1)}, bf16[16,152,512]{2,1,0:T(8,128)(2,1)}, u32[]{:S(2)}, u32[]{:S(2)}) collective-permute-start(bf16[16,152,512]{2,1,0:T(8,128)(2,1)S(1)} %all-to-all-done.refs_16_), channel_id=1, source_target_pairs={{0,16},{16,0},{1,17},{17,1},{2,18},{18,2},{3,19},{19,3},{4,20},{20... | collective-permute-start | bytes 7471112 | tf_op jit(solution)/shard_map/ppermute | solution.py:222
  85.1 0.0 copy-done.2
  85.1 0.0 copy-done.3
  85.1 6.3 %shard_map.65 = (f32[512,512]{1,0:T(8,128)}, f32[512,512]{1,0:T(8,128)}) custom-call(s32[2,8]{1,0:T(2,128)} %bitcast.3, bf16[304,512]{1,0:T(8,128)(2,1)} %get-tuple-element.16.refs_0_, bf16[304,512]{1,0:T(8,128)(2,1)} %copy-done.3, bf16[304,512]{1,0:T(8,128)(2,1)} %copy-done.2, bf16[304,512]{1,0:T(8,128)(2,1)} %copy-done.6, bf16[304,512]{1,0:T(8,128)(2,1)} %copy-done.5, ...), custom_call_target="tpu_custom_call" | custom-call | flops 1207959552 | bytes 8388608 | tf_op jit(solution)/shard_map/pallas_call | solution.py:188
  91.5 0.0 collective-permute-done.15.refs_16_
  91.5 6.4 %shard_map.66 = f32[512,1024]{1,0:T(8,128)} custom-call(s32[2,8]{1,0:T(2,128)} %bitcast.4, s32[4]{0:T(128)} %down_ref.3, bf16[304,512]{1,0:T(8,128)(2,1)} %get-tuple-element.16.refs_0_, bf16[304,512]{1,0:T(8,128)(2,1)} %copy-done.3, bf16[304,512]{1,0:T(8,128)(2,1)} %copy-done.2, bf16[304,512]{1,0:T(8,128)(2,1)} %copy-done.6, bf16[304,512]{1,0:T(8,128)(2,1)} %copy-done.5, ...), custom_call_target="tpu_custom_call" | custom-call | flops 1207959552 | bytes 8388608 | tf_op jit(solution)/shard_map/pallas_call | solution.py:200
  (5 shorter events, 0.0 us)
Async XLA Ops:
  4.0 13.6 %copy-start.1 = (bf16[304,512]{1,0:T(8,128)(2,1)S(1)}, bf16[304,512]{1,0:T(8,128)(2,1)}, u32[]{:S(2)}) copy-start(bf16[304,512]{1,0:T(8,128)(2,1)} %get-tuple-element.16.refs_0_) | copy-start | bytes 933892
  4.0 76.1 %all-to-all-start = ((bf16[16,152,512]{2,1,0:T(8,128)(2,1)}), bf16[16,152,512]{2,1,0:T(8,128)(2,1)S(1)}, u32[]{:S(2)}, u32[]{:S(2)}) async-start(bf16[16,152,512]{2,1,0:T(8,128)(2,1)} %get-tuple-element.17), calls=%async_computation | async-start | bytes 4980736 | tf_op jit(solution)/shard_map/all_to_all | solution.py:236
  17.6 11.9 %collective-permute-start.1 = (bf16[304,512]{1,0:T(8,128)(2,1)S(1)}, bf16[304,512]{1,0:T(8,128)(2,1)S(1)}, u32[]{:S(2)}, u32[]{:S(2)}) collective-permute-start(bf16[304,512]{1,0:T(8,128)(2,1)S(1)} %copy-done.1), channel_id=1, source_target_pairs={{0,1},{1,2},{2,3},{3,4},{4,5},{5,6},{6,7},{7,0},{8,9},{9,10},{10,1... | collective-permute-start | bytes 933896 | tf_op jit(solution)/shard_map/ppermute | solution.py:222
  20.8 15.1 %collective-permute-start = (bf16[304,512]{1,0:T(8,128)(2,1)S(1)}, bf16[304,512]{1,0:T(8,128)(2,1)S(1)}, u32[]{:S(2)}, u32[]{:S(2)}) collective-permute-start(bf16[304,512]{1,0:T(8,128)(2,1)S(1)} %copy-done.1), channel_id=1, source_target_pairs={{0,8},{8,0},{1,9},{9,1},{2,10},{10,2},{3,11},{11,3},{4,12},{12,4},... | collective-permute-start | bytes 933896 | tf_op jit(solution)/shard_map/ppermute | solution.py:222
  29.4 55.7 %copy-start.2 = (bf16[304,512]{1,0:T(8,128)(2,1)}, bf16[304,512]{1,0:T(8,128)(2,1)S(1)}, u32[]{:S(2)}) copy-start(bf16[304,512]{1,0:T(8,128)(2,1)S(1)} %collective-permute-done.1.refs_2_) | copy-start | bytes 933892
  29.4 13.0 %collective-permute-start.5 = (bf16[304,512]{1,0:T(8,128)(2,1)S(1)}, bf16[304,512]{1,0:T(8,128)(2,1)S(1)}, u32[]{:S(2)}, u32[]{:S(2)}) collective-permute-start(bf16[304,512]{1,0:T(8,128)(2,1)S(1)} %collective-permute-done.1.refs_2_), channel_id=1, source_target_pairs={{0,1},{1,2},{2,3},{3,4},{4,5},{5,6},{6,7},{7,0},{8,9},{9,10},{10,1... | collective-permute-start | bytes 933896 | tf_op jit(solution)/shard_map/ppermute | solution.py:222
  31.3 13.1 %collective-permute-start.3 = (bf16[304,512]{1,0:T(8,128)(2,1)S(1)}, bf16[304,512]{1,0:T(8,128)(2,1)S(1)}, u32[]{:S(2)}, u32[]{:S(2)}) collective-permute-start(bf16[304,512]{1,0:T(8,128)(2,1)S(1)} %copy-done.1), channel_id=1, source_target_pairs={{0,7},{1,0},{2,1},{3,2},{4,3},{5,4},{6,5},{7,6},{8,15},{9,8},{10,9... | collective-permute-start | bytes 933896 | tf_op jit(solution)/shard_map/ppermute | solution.py:222
  35.9 49.2 %copy-start.3 = (bf16[304,512]{1,0:T(8,128)(2,1)}, bf16[304,512]{1,0:T(8,128)(2,1)S(1)}, u32[]{:S(2)}) copy-start(bf16[304,512]{1,0:T(8,128)(2,1)S(1)} %collective-permute-done.refs_1_) | copy-start | bytes 933892
  35.9 13.1 %collective-permute-start.2 = (bf16[304,512]{1,0:T(8,128)(2,1)S(1)}, bf16[304,512]{1,0:T(8,128)(2,1)S(1)}, u32[]{:S(2)}, u32[]{:S(2)}) collective-permute-start(bf16[304,512]{1,0:T(8,128)(2,1)S(1)} %collective-permute-done.refs_1_), channel_id=1, source_target_pairs={{0,1},{1,2},{2,3},{3,4},{4,5},{5,6},{6,7},{7,0},{8,9},{9,10},{10,1... | collective-permute-start | bytes 933896 | tf_op jit(solution)/shard_map/ppermute | solution.py:222
  37.9 13.1 %collective-permute-start.4 = (bf16[304,512]{1,0:T(8,128)(2,1)S(1)}, bf16[304,512]{1,0:T(8,128)(2,1)S(1)}, u32[]{:S(2)}, u32[]{:S(2)}) collective-permute-start(bf16[304,512]{1,0:T(8,128)(2,1)S(1)} %collective-permute-done.refs_1_), channel_id=1, source_target_pairs={{0,7},{1,0},{2,1},{3,2},{4,3},{5,4},{6,5},{7,6},{8,15},{9,8},{10,9... | collective-permute-start | bytes 933896 | tf_op jit(solution)/shard_map/ppermute | solution.py:222
  42.5 31.3 %copy-start.4 = (bf16[304,512]{1,0:T(8,128)(2,1)}, bf16[304,512]{1,0:T(8,128)(2,1)S(1)}, u32[]{:S(2)}) copy-start(bf16[304,512]{1,0:T(8,128)(2,1)S(1)} %collective-permute-done.5.refs_6_) | copy-start | bytes 933892
  42.5 13.1 %collective-permute-start.9 = (bf16[304,512]{1,0:T(8,128)(2,1)S(1)}, bf16[304,512]{1,0:T(8,128)(2,1)S(1)}, u32[]{:S(2)}, u32[]{:S(2)}) collective-permute-start(bf16[304,512]{1,0:T(8,128)(2,1)S(1)} %collective-permute-done.5.refs_6_), channel_id=1, source_target_pairs={{0,1},{1,2},{2,3},{3,4},{4,5},{5,6},{6,7},{7,0},{8,9},{9,10},{10,1... | collective-permute-start | bytes 933896 | tf_op jit(solution)/shard_map/ppermute | solution.py:222
  44.4 29.4 %copy-start.5 = (bf16[304,512]{1,0:T(8,128)(2,1)}, bf16[304,512]{1,0:T(8,128)(2,1)S(1)}, u32[]{:S(2)}) copy-start(bf16[304,512]{1,0:T(8,128)(2,1)S(1)} %collective-permute-done.3.refs_4_) | copy-start | bytes 933892
  44.4 13.1 %collective-permute-start.7 = (bf16[304,512]{1,0:T(8,128)(2,1)S(1)}, bf16[304,512]{1,0:T(8,128)(2,1)S(1)}, u32[]{:S(2)}, u32[]{:S(2)}) collective-permute-start(bf16[304,512]{1,0:T(8,128)(2,1)S(1)} %collective-permute-done.3.refs_4_), channel_id=1, source_target_pairs={{0,7},{1,0},{2,1},{3,2},{4,3},{5,4},{6,5},{7,6},{8,15},{9,8},{10,9... | collective-permute-start | bytes 933896 | tf_op jit(solution)/shard_map/ppermute | solution.py:222
  49.0 24.8 %copy-start.6 = (bf16[304,512]{1,0:T(8,128)(2,1)}, bf16[304,512]{1,0:T(8,128)(2,1)S(1)}, u32[]{:S(2)}) copy-start(bf16[304,512]{1,0:T(8,128)(2,1)S(1)} %collective-permute-done.2.refs_3_) | copy-start | bytes 933892
  49.0 13.1 %collective-permute-start.6 = (bf16[304,512]{1,0:T(8,128)(2,1)S(1)}, bf16[304,512]{1,0:T(8,128)(2,1)S(1)}, u32[]{:S(2)}, u32[]{:S(2)}) collective-permute-start(bf16[304,512]{1,0:T(8,128)(2,1)S(1)} %collective-permute-done.2.refs_3_), channel_id=1, source_target_pairs={{0,1},{1,2},{2,3},{3,4},{4,5},{5,6},{6,7},{7,0},{8,9},{9,10},{10,1... | collective-permute-start | bytes 933896 | tf_op jit(solution)/shard_map/ppermute | solution.py:222
  51.0 22.8 %copy-start.7 = (bf16[304,512]{1,0:T(8,128)(2,1)}, bf16[304,512]{1,0:T(8,128)(2,1)S(1)}, u32[]{:S(2)}) copy-start(bf16[304,512]{1,0:T(8,128)(2,1)S(1)} %collective-permute-done.4.refs_5_) | copy-start | bytes 933892
  51.0 13.1 %collective-permute-start.8 = (bf16[304,512]{1,0:T(8,128)(2,1)S(1)}, bf16[304,512]{1,0:T(8,128)(2,1)S(1)}, u32[]{:S(2)}, u32[]{:S(2)}) collective-permute-start(bf16[304,512]{1,0:T(8,128)(2,1)S(1)} %collective-permute-done.4.refs_5_), channel_id=1, source_target_pairs={{0,7},{1,0},{2,1},{3,2},{4,3},{5,4},{6,5},{7,6},{8,15},{9,8},{10,9... | collective-permute-start | bytes 933896 | tf_op jit(solution)/shard_map/ppermute | solution.py:222
  55.6 18.2 %copy-start.8 = (bf16[304,512]{1,0:T(8,128)(2,1)}, bf16[304,512]{1,0:T(8,128)(2,1)S(1)}, u32[]{:S(2)}) copy-start(bf16[304,512]{1,0:T(8,128)(2,1)S(1)} %collective-permute-done.9.refs_10_) | copy-start | bytes 933892
  55.6 13.1 %collective-permute-start.11 = (bf16[304,512]{1,0:T(8,128)(2,1)S(1)}, bf16[304,512]{1,0:T(8,128)(2,1)S(1)}, u32[]{:S(2)}, u32[]{:S(2)}) collective-permute-start(bf16[304,512]{1,0:T(8,128)(2,1)S(1)} %collective-permute-done.9.refs_10_), channel_id=1, source_target_pairs={{0,1},{1,2},{2,3},{3,4},{4,5},{5,6},{6,7},{7,0},{8,9},{9,10},{10,1... | collective-permute-start | bytes 933896 | tf_op jit(solution)/shard_map/ppermute | solution.py:222
  57.5 27.6 %copy-start.9 = (bf16[304,512]{1,0:T(8,128)(2,1)}, bf16[304,512]{1,0:T(8,128)(2,1)S(1)}, u32[]{:S(2)}) copy-start(bf16[304,512]{1,0:T(8,128)(2,1)S(1)} %collective-permute-done.7.refs_8_) | copy-start | bytes 933892
  57.5 13.4 %collective-permute-start.10 = (bf16[304,512]{1,0:T(8,128)(2,1)S(1)}, bf16[304,512]{1,0:T(8,128)(2,1)S(1)}, u32[]{:S(2)}, u32[]{:S(2)}) collective-permute-start(bf16[304,512]{1,0:T(8,128)(2,1)S(1)} %collective-permute-done.7.refs_8_), channel_id=1, source_target_pairs={{0,7},{1,0},{2,1},{3,2},{4,3},{5,4},{6,5},{7,6},{8,15},{9,8},{10,9... | collective-permute-start | bytes 933896 | tf_op jit(solution)/shard_map/ppermute | solution.py:222
  62.1 11.7 %copy-start.10 = (bf16[304,512]{1,0:T(8,128)(2,1)}, bf16[304,512]{1,0:T(8,128)(2,1)S(1)}, u32[]{:S(2)}) copy-start(bf16[304,512]{1,0:T(8,128)(2,1)S(1)} %collective-permute-done.6.refs_7_) | copy-start | bytes 933892
  62.1 10.2 %collective-permute-start.12 = (bf16[304,512]{1,0:T(8,128)(2,1)S(1)}, bf16[304,512]{1,0:T(8,128)(2,1)S(1)}, u32[]{:S(2)}, u32[]{:S(2)}) collective-permute-start(bf16[304,512]{1,0:T(8,128)(2,1)S(1)} %collective-permute-done.6.refs_7_), channel_id=1, source_target_pairs={{0,1},{1,2},{2,3},{3,4},{4,5},{5,6},{6,7},{7,0},{8,9},{9,10},{10,1... | collective-permute-start | bytes 933896 | tf_op jit(solution)/shard_map/ppermute | solution.py:222
  64.1 9.8 %copy-start.11 = (bf16[304,512]{1,0:T(8,128)(2,1)}, bf16[304,512]{1,0:T(8,128)(2,1)S(1)}, u32[]{:S(2)}) copy-start(bf16[304,512]{1,0:T(8,128)(2,1)S(1)} %collective-permute-done.8.refs_9_) | copy-start | bytes 933892
  64.1 9.7 %collective-permute-start.13 = (bf16[304,512]{1,0:T(8,128)(2,1)S(1)}, bf16[304,512]{1,0:T(8,128)(2,1)S(1)}, u32[]{:S(2)}, u32[]{:S(2)}) collective-permute-start(bf16[304,512]{1,0:T(8,128)(2,1)S(1)} %collective-permute-done.8.refs_9_), channel_id=1, source_target_pairs={{0,7},{1,0},{2,1},{3,2},{4,3},{5,4},{6,5},{7,6},{8,15},{9,8},{10,9... | collective-permute-start | bytes 933896 | tf_op jit(solution)/shard_map/ppermute | solution.py:222
  68.7 5.2 %copy-start.12 = (bf16[304,512]{1,0:T(8,128)(2,1)}, bf16[304,512]{1,0:T(8,128)(2,1)S(1)}, u32[]{:S(2)}) copy-start(bf16[304,512]{1,0:T(8,128)(2,1)S(1)} %collective-permute-done.11.refs_14_) | copy-start | bytes 933892
  68.7 11.4 %collective-permute-start.14 = (bf16[304,512]{1,0:T(8,128)(2,1)S(1)}, bf16[304,512]{1,0:T(8,128)(2,1)}, u32[]{:S(2)}, u32[]{:S(2)}) collective-permute-start(bf16[304,512]{1,0:T(8,128)(2,1)S(1)} %collective-permute-done.11.refs_14_), channel_id=1, source_target_pairs={{0,8},{8,0},{1,9},{9,1},{2,10},{10,2},{3,11},{11,3},{4,12},{12,4},... | collective-permute-start | bytes 933896 | tf_op jit(solution)/shard_map/ppermute | solution.py:222
  70.9 2.9 %copy-start.13 = (bf16[304,512]{1,0:T(8,128)(2,1)}, bf16[304,512]{1,0:T(8,128)(2,1)S(1)}, u32[]{:S(2)}) copy-start(bf16[304,512]{1,0:T(8,128)(2,1)S(1)} %collective-permute-done.10.refs_12_) | copy-start | bytes 933892
  72.3 1.5 %copy-start.14 = (bf16[304,512]{1,0:T(8,128)(2,1)}, bf16[304,512]{1,0:T(8,128)(2,1)S(1)}, u32[]{:S(2)}) copy-start(bf16[304,512]{1,0:T(8,128)(2,1)S(1)} %collective-permute-done.12.refs_11_) | copy-start | bytes 933892
  73.9 0.7 copy-start.15
  80.1 5.0 %copy-start = (bf16[16,152,512]{2,1,0:T(8,128)(2,1)}, bf16[16,152,512]{2,1,0:T(8,128)(2,1)S(1)}, u32[]{:S(2)}) copy-start(bf16[16,152,512]{2,1,0:T(8,128)(2,1)S(1)} %all-to-all-done.refs_16_) | copy-start | bytes 7471108
  80.1 11.4 %collective-permute-start.15 = (bf16[16,152,512]{2,1,0:T(8,128)(2,1)S(1)}, bf16[16,152,512]{2,1,0:T(8,128)(2,1)}, u32[]{:S(2)}, u32[]{:S(2)}) collective-permute-start(bf16[16,152,512]{2,1,0:T(8,128)(2,1)S(1)} %all-to-all-done.refs_16_), channel_id=1, source_target_pairs={{0,16},{16,0},{1,17},{17,1},{2,18},{18,2},{3,19},{19,3},{4,20},{20... | collective-permute-start | bytes 7471112 | tf_op jit(solution)/shard_map/ppermute | solution.py:222

commit v5 on v4

v5 whole, which is shorter than its diff:
```python
import jax
import jax.numpy as jnp
from jax import lax
from jax.experimental import pallas as pl
from jax.experimental.pallas import tpu as pltpu
from jax.sharding import Mesh
from jax.sharding import PartitionSpec as P

UF_DEV = 512
VF_DEV = 1024
BLOCK = 128
DACT = 4
UACT = 2
KD = 288
KE = 144
TD = 16
TE = 8
RD = KD + TD
RE = KE + TE
DOWN = ("xl", "y")
UP = ("z", "xh", "c")
NY = 8
TURNS = (0, -1, 1, -2, 2, -3, 3, 4)
STEP = 4
VMEM = pl.BlockSpec(memory_space=pltpu.VMEM)
SMEM = pl.BlockSpec(memory_space=pltpu.SMEM)
ANY = pl.BlockSpec(memory_space=pl.ANY)


def pack_kernel(down_ref, dec_ref, delta_ref, enc_ref, grad_ref, d_ref, e_ref, active, sems):
    copies = []

    def move(source, target):
        copies.append(pltpu.make_async_copy(source, target, sems.at[len(copies)]))
        copies[-1].start()

    for i in range(DACT):
        cols = pl.ds(pl.multiple_of(down_ref[i] * BLOCK, BLOCK), BLOCK)
        move(enc_ref.at[:, cols], active.at[:KE, i * BLOCK : (i + 1) * BLOCK])
        move(grad_ref.at[:, cols], active.at[KE:, i * BLOCK : (i + 1) * BLOCK])
    loads = len(copies)
    move(dec_ref, d_ref.at[:KD])
    move(delta_ref, d_ref.at[KD:])
    for copy in copies[:loads]:
        copy.wait()
    for n in range(2 * NY):
        move(active, e_ref.at[n])
    for copy in copies[loads:]:
        copy.wait()


def pack(down_blocks, dec_t, deltas, encoder, gradients):
    return pl.pallas_call(
        pack_kernel,
        out_shape=(
            jax.ShapeDtypeStruct((RD, UF_DEV), jnp.bfloat16),
            jax.ShapeDtypeStruct((2 * NY, RE, DACT * BLOCK), jnp.bfloat16),
        ),
        in_specs=[SMEM, ANY, ANY, ANY, ANY],
        out_specs=(VMEM, ANY),
        scratch_shapes=[
            pltpu.VMEM((RE, DACT * BLOCK), jnp.bfloat16),
            pltpu.SemaphoreType.DMA((2 * DACT + 2 + 2 * NY,)),
        ],
        compiler_params=pltpu.CompilerParams(vmem_limit_bytes=60 << 20),
    )(down_blocks, dec_t, deltas, encoder, gradients)


def accumulate(items, up_ref, dec, enc, dec_sem, enc_sem):
    chunks = [range(low, min(low + STEP, len(items))) for low in range(0, len(items), STEP)]
    if len(chunks[-1]) == 1:
        chunks[-2:] = [range(chunks[-2].start, len(items))]
    for n, chunk in enumerate(chunks):
        for slot in chunk:
            shard, k, part, source = items[slot]
            rows = pl.ds(pl.multiple_of(part * KE, 16), KE)
            tokens = pl.ds(pl.multiple_of(KD + part * TE, TE), TE)
            here = dec.at[slot]
            pltpu.make_async_copy(source.at[k], enc.at[slot], enc_sem.at[n]).start()
            pltpu.make_async_copy(shard.at[rows], here.at[:KE], dec_sem.at[n]).start()
            pltpu.make_async_copy(shard.at[tokens], here.at[KE:], dec_sem.at[n]).start()
    dims = (((0,), (0,)), ((), ()))
    cols = DACT * BLOCK
    virtual = None
    for n, chunk in enumerate(chunks):
        at = slice(chunk.start, chunk.stop)
        pltpu.make_async_copy(dec.at[at], dec.at[at], dec_sem.at[n]).wait()
        pltpu.make_async_copy(enc.at[at], enc.at[at], enc_sem.at[n]).wait()
        term = lax.dot_general(
            dec[at, :KE].reshape(len(chunk) * KE, UF_DEV),
            enc[at, :KE].reshape(len(chunk) * KE, cols),
            dims,
            preferred_element_type=jnp.float32,
        )
        virtual = term if virtual is None else virtual + term
    lane_block = lax.broadcasted_iota(jnp.int32, (TE, UF_DEV), 1) // BLOCK
    masked, kept = [], []
    for slot, (_, k, _, _) in enumerate(items):
        w = k // 2
        on = (lane_block == up_ref[0, w]) | (lane_block == up_ref[1, w])
        masked.append(jnp.where(on, dec[slot, KE:].astype(jnp.float32), 0.0))
        kept.append(enc[slot, KE:].astype(jnp.float32))
    masked, kept = (jnp.concatenate(v, 0).astype(jnp.bfloat16) for v in (masked, kept))
    product = lax.dot_general(masked, kept, dims, preferred_element_type=jnp.float32)
    return virtual, product


def places():
    y, xl = lax.axis_index("y"), lax.axis_index("xl")
    return [
        (xl if slot % 2 == 0 else 1 - xl) * NY + lax.rem(y + TURNS[slot // 2] + NY, NY)
        for slot in range(2 * NY)
    ]


def half_kernel(up_ref, *refs):
    shards, refs = refs[: 2 * NY - 1], refs[2 * NY - 1 :]
    source, virtual_ref, product_ref, dec, enc, dec_sem, enc_sem = refs
    core = lax.axis_index("c")
    items = [(shard, k, core, source) for shard, k in zip(shards, places())]
    virtual_ref[...], product_ref[...] = accumulate(
        items, up_ref, dec, enc, dec_sem, enc_sem
    )


def score_kernel(up_ref, down_ref, *refs):
    shards, refs = refs[: 2 * NY], refs[2 * NY :]
    own, swapped, virtual_in, product_in, out_ref = refs[:5]
    dec, enc, dec_sem, enc_sem, virtual, product, zero, scored = refs[5:13]
    in_sem, zero_sem, out_sem = refs[13:]
    zero[...] = jnp.zeros_like(zero)

    def blank(b):
        return pltpu.make_async_copy(
            zero, out_ref.at[:, b * BLOCK : (b + 1) * BLOCK], zero_sem.at[b]
        )

    idle = []
    for b in range(VF_DEV // BLOCK):
        used = down_ref[0] == b
        for i in range(1, DACT):
            used = used | (down_ref[i] == b)
        idle.append(jnp.logical_not(used))
    loads = [
        pltpu.make_async_copy(virtual_in, virtual, in_sem.at[0]),
        pltpu.make_async_copy(product_in, product, in_sem.at[1]),
    ]
    for copy in loads:
        copy.start()
    core, ks = lax.axis_index("c"), places()
    items = [(shard, k, 1 - core, swapped) for shard, k in zip(shards, ks)]
    items.append((shards[-1], ks[-1], core, own))
    more, part = accumulate(items, up_ref, dec, enc, dec_sem, enc_sem)
    for b in range(VF_DEV // BLOCK):
        pl.when(idle[b])(blank(b).start)
    for copy in loads:
        copy.wait()
    filled = []
    for i in range(DACT):
        at = slice(i * BLOCK, (i + 1) * BLOCK)
        scored[i] = (product[:, at] + part[:, at]) * (virtual[:, at] + more[:, at])
        where = pl.ds(pl.multiple_of(down_ref[i] * BLOCK, BLOCK), BLOCK)
        filled.append(
            pltpu.make_async_copy(scored.at[i], out_ref.at[:, where], out_sem.at[i])
        )
        filled[i].start()
    for b in range(VF_DEV // BLOCK):
        pl.when(idle[b])(blank(b).wait)
    for copy in filled:
        copy.wait()


COLS = DACT * BLOCK


def held(count):
    return [
        pltpu.VMEM((count, RE, UF_DEV), jnp.bfloat16),
        pltpu.VMEM((count, RE, COLS), jnp.bfloat16),
        pltpu.SemaphoreType.DMA((-(-count // STEP),)),
        pltpu.SemaphoreType.DMA((-(-count // STEP),)),
    ]


COST = pl.CostEstimate(
    flops=UF_DEV * COLS * KD * 2 * NY, bytes_accessed=8 << 20, transcendentals=0
)


def half(up_t, shards, source):
    return pl.pallas_call(
        half_kernel,
        out_shape=(jax.ShapeDtypeStruct((UF_DEV, COLS), jnp.float32),) * 2,
        in_specs=[SMEM] + [ANY] * (2 * NY),
        out_specs=(VMEM, VMEM),
        scratch_shapes=held(2 * NY - 1),
        compiler_params=pltpu.CompilerParams(vmem_limit_bytes=60 << 20),
        cost_estimate=COST,
    )(up_t, *shards, source)


def score(up_t, down_blocks, shards, own, swapped, sums):
    return pl.pallas_call(
        score_kernel,
        out_shape=jax.ShapeDtypeStruct((UF_DEV, VF_DEV), jnp.float32),
        in_specs=[SMEM, SMEM] + [ANY] * (2 * NY + 4),
        out_specs=ANY,
        scratch_shapes=[
            *held(2 * NY + 1),
            pltpu.VMEM((UF_DEV, COLS), jnp.float32),
            pltpu.VMEM((UF_DEV, COLS), jnp.float32),
            pltpu.VMEM((UF_DEV, BLOCK), jnp.float32),
            pltpu.VMEM((DACT, UF_DEV, BLOCK), jnp.float32),
            pltpu.SemaphoreType.DMA((2,)),
            pltpu.SemaphoreType.DMA((VF_DEV // BLOCK,)),
            pltpu.SemaphoreType.DMA((DACT,)),
        ],
        compiler_params=pltpu.CompilerParams(vmem_limit_bytes=60 << 20),
        cost_estimate=COST,
    )(up_t, down_blocks, *shards, own, swapped, *sums)


def turn(value, axis, by):
    n = lax.axis_size(axis)
    return lax.ppermute(value, axis, [(i, (i + by) % n) for i in range(n)])


def step(right, left):
    return turn(right, "y", 1), turn(left, "y", -1)


def local(deltas, gradients, up_blocks, down_blocks, decoder, encoder):
    d, e = pack(down_blocks, decoder.T, deltas, encoder, gradients)
    own = lax.all_to_all(e, ("z", "xh"), 0, 0, tiled=True)
    a1 = step(d, d)
    b0 = turn(d, "xl", 1)
    a2 = step(*a1)
    a3 = step(*a2)
    b1 = step(b0, b0)
    b2 = step(*b1)
    b3 = step(*b2)
    a4 = turn(a3[0], "y", 1)
    b4 = turn(a4, "xl", 1)
    own, a3, a4, b3, b4 = lax.optimization_barrier((own, a3, a4, b3, b4))
    near, across = [d, *a1, *a2, *a3, a4], [b0, *b1, *b2, *b3, b4]
    shards = [shard for both in zip(near, across) for shard in both]
    swapped = turn(own, "c", 1)
    up_t = up_blocks.T
    sums = half(up_t, shards[:-1], own)
    return score(up_t, down_blocks, shards, own, swapped, sums)


def solution(mesh):
    torus = Mesh(mesh.devices.reshape(8, 2, 2, 2, 8), ("z", "xh", "c", "xl", "y"))
    return jax.shard_map(
        local,
        mesh=torus,
        in_specs=(P(DOWN, UP), P(UP, DOWN), P(None, UP), P(DOWN), P(UP, DOWN), P(UP, DOWN)),
        out_specs=P(UP, DOWN),
        check_vma=False,
    )
```

time: 98.6 us -> 97.9 us (level)
  starting transfers between devices: 65.2 us -> 63.3 us
  waiting for transfers between devices: 14.8 us -> 16.7 us
    ppermute x16, starting transfers between devices: 51.6 us -> 49.7 us  [turn(): return lax.ppermute(value, axis, [(i, (i + by) % n) for i in range(n)])]
    ppermute x16, waiting for transfers between devices: 14.8 us -> 16.7 us  [turn(): return lax.ppermute(value, axis, [(i, (i + by) % n) for i in range(n)])]
where the time goes in v5:
time: 97.9 us; the launch traced here: 97.2 us
  starting transfers between devices  63.3 us (65%)
  waiting for transfers between devices  16.7 us (17%)
  Pallas kernels  16 us (16%)
    ppermute x16, starting transfers between devices, turn(): return lax.ppermute(value, axis, [(i, (i + by) % n) for i in range(n)])  49.7 us
    ppermute x16, waiting for transfers between devices, turn(): return lax.ppermute(value, axis, [(i, (i + by) % n) for i in range(n)])  16.7 us
    all_to_all x1, starting transfers between devices, local(): own = lax.all_to_all(e, ('z', 'xh'), 0, 0, tiled=True)  13.6 us
    pallas_call x1, Pallas kernels, score(): pl.pallas_call(score_kernel, out_shape=jax.ShapeDtypeStruct((UF_DEV, VF_D...  6.1 us
    pallas_call x1, Pallas kernels, half(): pl.pallas_call(half_kernel, out_shape=(jax.ShapeDtypeStruct((UF_DEV, COLS...  5.94 us
    pallas_call x1, Pallas kernels, pack(): pl.pallas_call(pack_kernel, out_shape=(jax.ShapeDtypeStruct((RD, UF_DEV),...  3.97 us
  transfers between devices with their start and end apart: 17, of which 4 were waited for; matrix products, arithmetic and copies ran while one was open for 0% of the time, Pallas kernels for 6%

profile of v5, /device:TPU:1, one launch (start us, length us, event | category | flops | bytes accessed | tf_op | source)
XLA Modules:
  0.0 97.2 jit_solution(3456663034901914418)
XLA Ops:
  0.0 4.0 %shard_map.64 = (bf16[304,512]{1,0:T(8,128)(2,1)}, bf16[16,152,512]{2,1,0:T(8,128)(2,1)}) custom-call(s32[4]{0:T(128)} %down_ref.3, bf16[288,512]{1,0:T(8,128)(2,1)} %bitcast.2, bf16[16,512]{1,0:T(8,128)(2,1)} %delta_ref.1, bf16[144,1024]{1,0:T(8,128)(2,1)} %enc_ref.1, bf16[8,1024]{1,0:T(8,128)(2,1)} %grad_ref.1), custom_call_target="tpu_custom_call" | custom-call | tf_op jit(solution)/shard_map/pallas_call | solution.py:53
  4.0 0.0 copy-start.1
  4.0 13.6 %all-to-all-start = ((bf16[16,152,512]{2,1,0:T(8,128)(2,1)}), bf16[16,152,512]{2,1,0:T(8,128)(2,1)S(1)}, u32[]{:S(2)}, u32[]{:S(2)}) async-start(bf16[16,152,512]{2,1,0:T(8,128)(2,1)} %get-tuple-element.17), calls=%async_computation | async-start | bytes 4980736 | tf_op jit(solution)/shard_map/all_to_all | solution.py:234
  17.6 0.0 copy-done.1
  17.6 3.2 %collective-permute-start.1 = (bf16[304,512]{1,0:T(8,128)(2,1)S(1)}, bf16[304,512]{1,0:T(8,128)(2,1)S(1)}, u32[]{:S(2)}, u32[]{:S(2)}) collective-permute-start(bf16[304,512]{1,0:T(8,128)(2,1)S(1)} %copy-done.1), channel_id=1, source_target_pairs={{0,1},{1,2},{2,3},{3,4},{4,5},{5,6},{6,7},{7,0},{8,9},{9,10},{10,1... | collective-permute-start | bytes 933896 | tf_op jit(solution)/shard_map/ppermute | solution.py:225
  20.8 2.2 %collective-permute-start = (bf16[304,512]{1,0:T(8,128)(2,1)S(1)}, bf16[304,512]{1,0:T(8,128)(2,1)S(1)}, u32[]{:S(2)}, u32[]{:S(2)}) collective-permute-start(bf16[304,512]{1,0:T(8,128)(2,1)S(1)} %copy-done.1), channel_id=1, source_target_pairs={{0,8},{8,0},{1,9},{9,1},{2,10},{10,2},{3,11},{11,3},{4,12},{12,4},... | collective-permute-start | bytes 933896 | tf_op jit(solution)/shard_map/ppermute | solution.py:225
  23.0 6.4 %collective-permute-done.1.refs_2_ = bf16[304,512]{1,0:T(8,128)(2,1)S(1)} collective-permute-done((bf16[304,512]{1,0:T(8,128)(2,1)S(1)}, bf16[304,512]{1,0:T(8,128)(2,1)S(1)}, u32[]{:S(2)}, u32[]{:S(2)}) %collective-permute-start.1) | collective-permute-done | bytes 311328 | tf_op jit(solution)/shard_map/ppermute | solution.py:225
  29.4 1.9 %collective-permute-start.5 = (bf16[304,512]{1,0:T(8,128)(2,1)S(1)}, bf16[304,512]{1,0:T(8,128)(2,1)S(1)}, u32[]{:S(2)}, u32[]{:S(2)}) collective-permute-start(bf16[304,512]{1,0:T(8,128)(2,1)S(1)} %collective-permute-done.1.refs_2_), channel_id=1, source_target_pairs={{0,1},{1,2},{2,3},{3,4},{4,5},{5,6},{6,7},{7,0},{8,9},{9,10},{10,1... | collective-permute-start | bytes 933896 | tf_op jit(solution)/shard_map/ppermute | solution.py:225
  31.3 4.6 %collective-permute-start.3 = (bf16[304,512]{1,0:T(8,128)(2,1)S(1)}, bf16[304,512]{1,0:T(8,128)(2,1)S(1)}, u32[]{:S(2)}, u32[]{:S(2)}) collective-permute-start(bf16[304,512]{1,0:T(8,128)(2,1)S(1)} %copy-done.1), channel_id=1, source_target_pairs={{0,7},{1,0},{2,1},{3,2},{4,3},{5,4},{6,5},{7,6},{8,15},{9,8},{10,9... | collective-permute-start | bytes 933896 | tf_op jit(solution)/shard_map/ppermute | solution.py:225
  35.9 0.0 collective-permute-done.refs_1_
  35.9 0.0 copy-start.3
  35.9 1.9 %collective-permute-start.4 = (bf16[304,512]{1,0:T(8,128)(2,1)S(1)}, bf16[304,512]{1,0:T(8,128)(2,1)S(1)}, u32[]{:S(2)}, u32[]{:S(2)}) collective-permute-start(bf16[304,512]{1,0:T(8,128)(2,1)S(1)} %collective-permute-done.refs_1_), channel_id=1, source_target_pairs={{0,7},{1,0},{2,1},{3,2},{4,3},{5,4},{6,5},{7,6},{8,15},{9,8},{10,9... | collective-permute-start | bytes 933896 | tf_op jit(solution)/shard_map/ppermute | solution.py:225
  37.9 3.4 %collective-permute-start.2 = (bf16[304,512]{1,0:T(8,128)(2,1)S(1)}, bf16[304,512]{1,0:T(8,128)(2,1)S(1)}, u32[]{:S(2)}, u32[]{:S(2)}) collective-permute-start(bf16[304,512]{1,0:T(8,128)(2,1)S(1)} %collective-permute-done.refs_1_), channel_id=1, source_target_pairs={{0,1},{1,2},{2,3},{3,4},{4,5},{5,6},{6,7},{7,0},{8,9},{9,10},{10,1... | collective-permute-start | bytes 933896 | tf_op jit(solution)/shard_map/ppermute | solution.py:225
  41.2 0.0 collective-permute-done.5.refs_6_
  41.3 0.0 copy-start.4
  41.3 1.9 %collective-permute-start.9 = (bf16[304,512]{1,0:T(8,128)(2,1)S(1)}, bf16[304,512]{1,0:T(8,128)(2,1)S(1)}, u32[]{:S(2)}, u32[]{:S(2)}) collective-permute-start(bf16[304,512]{1,0:T(8,128)(2,1)S(1)} %collective-permute-done.5.refs_6_), channel_id=1, source_target_pairs={{0,1},{1,2},{2,3},{3,4},{4,5},{5,6},{6,7},{7,0},{8,9},{9,10},{10,1... | collective-permute-start | bytes 933896 | tf_op jit(solution)/shard_map/ppermute | solution.py:225
  43.2 0.0 collective-permute-done.3.refs_4_
  43.2 0.0 copy-start.5
  43.2 4.6 %collective-permute-start.7 = (bf16[304,512]{1,0:T(8,128)(2,1)S(1)}, bf16[304,512]{1,0:T(8,128)(2,1)S(1)}, u32[]{:S(2)}, u32[]{:S(2)}) collective-permute-start(bf16[304,512]{1,0:T(8,128)(2,1)S(1)} %collective-permute-done.3.refs_4_), channel_id=1, source_target_pairs={{0,7},{1,0},{2,1},{3,2},{4,3},{5,4},{6,5},{7,6},{8,15},{9,8},{10,9... | collective-permute-start | bytes 933896 | tf_op jit(solution)/shard_map/ppermute | solution.py:225
  47.8 0.0 collective-permute-done.4.refs_5_
  47.8 0.0 copy-start.6
  47.8 4.9 %collective-permute-start.8 = (bf16[304,512]{1,0:T(8,128)(2,1)S(1)}, bf16[304,512]{1,0:T(8,128)(2,1)S(1)}, u32[]{:S(2)}, u32[]{:S(2)}) collective-permute-start(bf16[304,512]{1,0:T(8,128)(2,1)S(1)} %collective-permute-done.4.refs_5_), channel_id=1, source_target_pairs={{0,7},{1,0},{2,1},{3,2},{4,3},{5,4},{6,5},{7,6},{8,15},{9,8},{10,9... | collective-permute-start | bytes 933896 | tf_op jit(solution)/shard_map/ppermute | solution.py:225
  52.7 0.0 collective-permute-done.2.refs_3_
  52.7 0.0 copy-start.7
  52.7 1.9 %collective-permute-start.6 = (bf16[304,512]{1,0:T(8,128)(2,1)S(1)}, bf16[304,512]{1,0:T(8,128)(2,1)S(1)}, u32[]{:S(2)}, u32[]{:S(2)}) collective-permute-start(bf16[304,512]{1,0:T(8,128)(2,1)S(1)} %collective-permute-done.2.refs_3_), channel_id=1, source_target_pairs={{0,1},{1,2},{2,3},{3,4},{4,5},{5,6},{6,7},{7,0},{8,9},{9,10},{10,1... | collective-permute-start | bytes 933896 | tf_op jit(solution)/shard_map/ppermute | solution.py:225
  54.7 0.0 collective-permute-done.9.refs_10_
  54.7 0.0 copy-start.8
  54.7 2.1 %collective-permute-start.11 = (bf16[304,512]{1,0:T(8,128)(2,1)S(1)}, bf16[304,512]{1,0:T(8,128)(2,1)S(1)}, u32[]{:S(2)}, u32[]{:S(2)}) collective-permute-start(bf16[304,512]{1,0:T(8,128)(2,1)S(1)} %collective-permute-done.9.refs_10_), channel_id=1, source_target_pairs={{0,1},{1,2},{2,3},{3,4},{4,5},{5,6},{6,7},{7,0},{8,9},{9,10},{10,1... | collective-permute-start | bytes 933896 | tf_op jit(solution)/shard_map/ppermute | solution.py:225
  56.8 0.0 collective-permute-done.7.refs_8_
  56.8 0.0 copy-start.9
  56.8 4.4 %collective-permute-start.10 = (bf16[304,512]{1,0:T(8,128)(2,1)S(1)}, bf16[304,512]{1,0:T(8,128)(2,1)S(1)}, u32[]{:S(2)}, u32[]{:S(2)}) collective-permute-start(bf16[304,512]{1,0:T(8,128)(2,1)S(1)} %collective-permute-done.7.refs_8_), channel_id=1, source_target_pairs={{0,7},{1,0},{2,1},{3,2},{4,3},{5,4},{6,5},{7,6},{8,15},{9,8},{10,9... | collective-permute-start | bytes 933896 | tf_op jit(solution)/shard_map/ppermute | solution.py:225
  61.2 0.0 collective-permute-done.8.refs_9_
  61.2 0.0 copy-start.10
  61.2 4.8 %collective-permute-start.13 = (bf16[304,512]{1,0:T(8,128)(2,1)S(1)}, bf16[304,512]{1,0:T(8,128)(2,1)S(1)}, u32[]{:S(2)}, u32[]{:S(2)}) collective-permute-start(bf16[304,512]{1,0:T(8,128)(2,1)S(1)} %collective-permute-done.8.refs_9_), channel_id=1, source_target_pairs={{0,7},{1,0},{2,1},{3,2},{4,3},{5,4},{6,5},{7,6},{8,15},{9,8},{10,9... | collective-permute-start | bytes 933896 | tf_op jit(solution)/shard_map/ppermute | solution.py:225
  66.0 0.0 collective-permute-done.6.refs_7_
  66.0 0.0 copy-start.11
  66.0 1.9 %collective-permute-start.12 = (bf16[304,512]{1,0:T(8,128)(2,1)S(1)}, bf16[304,512]{1,0:T(8,128)(2,1)S(1)}, u32[]{:S(2)}, u32[]{:S(2)}) collective-permute-start(bf16[304,512]{1,0:T(8,128)(2,1)S(1)} %collective-permute-done.6.refs_7_), channel_id=1, source_target_pairs={{0,1},{1,2},{2,3},{3,4},{4,5},{5,6},{6,7},{7,0},{8,9},{9,10},{10,1... | collective-permute-start | bytes 933896 | tf_op jit(solution)/shard_map/ppermute | solution.py:225
  68.0 0.0 collective-permute-done.11.refs_14_
  68.0 0.0 copy-start.12
  68.0 2.2 %collective-permute-start.14 = (bf16[304,512]{1,0:T(8,128)(2,1)S(1)}, bf16[304,512]{1,0:T(8,128)(2,1)}, u32[]{:S(2)}, u32[]{:S(2)}) collective-permute-start(bf16[304,512]{1,0:T(8,128)(2,1)S(1)} %collective-permute-done.11.refs_14_), channel_id=1, source_target_pairs={{0,8},{8,0},{1,9},{9,1},{2,10},{10,2},{3,11},{11,3},{4,12},{12,4},... | collective-permute-start | bytes 933896 | tf_op jit(solution)/shard_map/ppermute | solution.py:225
  70.2 0.0 collective-permute-done.10.refs_12_
  70.2 0.0 copy-start.13
  70.2 2.6 %collective-permute-done.13.refs_13_ = bf16[304,512]{1,0:T(8,128)(2,1)S(1)} collective-permute-done((bf16[304,512]{1,0:T(8,128)(2,1)S(1)}, bf16[304,512]{1,0:T(8,128)(2,1)S(1)}, u32[]{:S(2)}, u32[]{:S(2)}) %collective-permute-start.13) | collective-permute-done | bytes 311328 | tf_op jit(solution)/shard_map/ppermute | solution.py:225
  72.9 2.4 %collective-permute-done.12.refs_11_ = bf16[304,512]{1,0:T(8,128)(2,1)S(1)} collective-permute-done((bf16[304,512]{1,0:T(8,128)(2,1)S(1)}, bf16[304,512]{1,0:T(8,128)(2,1)S(1)}, u32[]{:S(2)}, u32[]{:S(2)}) %collective-permute-start.12) | collective-permute-done | bytes 311328 | tf_op jit(solution)/shard_map/ppermute | solution.py:225
  75.2 0.0 copy-done.4
  75.2 0.0 copy-done.5
  75.2 0.0 copy-done.6
  75.2 0.0 copy-done.7
  75.3 0.0 copy-done.8
  75.3 0.0 copy-done.10
  75.3 0.0 copy-done.11
  75.3 0.0 copy-done.12
  75.3 0.0 copy-done.13
  75.3 0.0 copy-done.14
  75.3 0.0 copy-start.15
  75.3 0.7 copy-done.15
  76.0 5.2 %collective-permute-done.14.refs_15_ = bf16[304,512]{1,0:T(8,128)(2,1)} collective-permute-done((bf16[304,512]{1,0:T(8,128)(2,1)S(1)}, bf16[304,512]{1,0:T(8,128)(2,1)}, u32[]{:S(2)}, u32[]{:S(2)}) %collective-permute-start.14) | collective-permute-done | bytes 311328 | tf_op jit(solution)/shard_map/ppermute | solution.py:225
  81.3 0.0 all-to-all-done.refs_15_.refs_16_
  81.3 3.8 %collective-permute-start.15 = (bf16[16,152,512]{2,1,0:T(8,128)(2,1)S(1)}, bf16[16,152,512]{2,1,0:T(8,128)(2,1)}, u32[]{:S(2)}, u32[]{:S(2)}) collective-permute-start(bf16[16,152,512]{2,1,0:T(8,128)(2,1)S(1)} %all-to-all-done.refs_15_.refs_16_), channel_id=1, source_target_pairs={{0,16},{16,0},{1,17},{17,1},{2,18},{18,2},{3,19},{19,3},{4,20},{20... | collective-permute-start | bytes 7471112 | tf_op jit(solution)/shard_map/ppermute | solution.py:225
  85.1 0.0 copy-done.2
  85.1 0.0 copy-done.3
  85.1 5.9 %shard_map.65 = (f32[512,512]{1,0:T(8,128)}, f32[512,512]{1,0:T(8,128)}) custom-call(s32[2,8]{1,0:T(2,128)} %bitcast.3, bf16[304,512]{1,0:T(8,128)(2,1)} %get-tuple-element.16.refs_0_, bf16[304,512]{1,0:T(8,128)(2,1)} %copy-done.3, bf16[304,512]{1,0:T(8,128)(2,1)} %copy-done.2, bf16[304,512]{1,0:T(8,128)(2,1)} %copy-done.7, bf16[304,512]{1,0:T(8,128)(2,1)} %copy-done.5, ...), custom_call_target="tpu_custom_call" | custom-call | flops 1207959552 | bytes 8388608 | tf_op jit(solution)/shard_map/pallas_call | solution.py:191
  91.1 0.0 collective-permute-done.15.refs_17_
  91.1 6.1 %shard_map.66 = f32[512,1024]{1,0:T(8,128)} custom-call(s32[2,8]{1,0:T(2,128)} %bitcast.4, s32[4]{0:T(128)} %down_ref.3, bf16[304,512]{1,0:T(8,128)(2,1)} %get-tuple-element.16.refs_0_, bf16[304,512]{1,0:T(8,128)(2,1)} %copy-done.3, bf16[304,512]{1,0:T(8,128)(2,1)} %copy-done.2, bf16[304,512]{1,0:T(8,128)(2,1)} %copy-done.7, bf16[304,512]{1,0:T(8,128)(2,1)} %copy-done.5, ...), custom_call_target="tpu_custom_call" | custom-call | flops 1207959552 | bytes 8388608 | tf_op jit(solution)/shard_map/pallas_call | solution.py:203
  (5 shorter events, 0.0 us)
Async XLA Ops:
  4.0 13.6 %copy-start.1 = (bf16[304,512]{1,0:T(8,128)(2,1)S(1)}, bf16[304,512]{1,0:T(8,128)(2,1)}, u32[]{:S(2)}) copy-start(bf16[304,512]{1,0:T(8,128)(2,1)} %get-tuple-element.16.refs_0_) | copy-start | bytes 933892
  4.0 77.3 %all-to-all-start = ((bf16[16,152,512]{2,1,0:T(8,128)(2,1)}), bf16[16,152,512]{2,1,0:T(8,128)(2,1)S(1)}, u32[]{:S(2)}, u32[]{:S(2)}) async-start(bf16[16,152,512]{2,1,0:T(8,128)(2,1)} %get-tuple-element.17), calls=%async_computation | async-start | bytes 4980736 | tf_op jit(solution)/shard_map/all_to_all | solution.py:234
  17.6 11.8 %collective-permute-start.1 = (bf16[304,512]{1,0:T(8,128)(2,1)S(1)}, bf16[304,512]{1,0:T(8,128)(2,1)S(1)}, u32[]{:S(2)}, u32[]{:S(2)}) collective-permute-start(bf16[304,512]{1,0:T(8,128)(2,1)S(1)} %copy-done.1), channel_id=1, source_target_pairs={{0,1},{1,2},{2,3},{3,4},{4,5},{5,6},{6,7},{7,0},{8,9},{9,10},{10,1... | collective-permute-start | bytes 933896 | tf_op jit(solution)/shard_map/ppermute | solution.py:225
  20.8 15.1 %collective-permute-start = (bf16[304,512]{1,0:T(8,128)(2,1)S(1)}, bf16[304,512]{1,0:T(8,128)(2,1)S(1)}, u32[]{:S(2)}, u32[]{:S(2)}) collective-permute-start(bf16[304,512]{1,0:T(8,128)(2,1)S(1)} %copy-done.1), channel_id=1, source_target_pairs={{0,8},{8,0},{1,9},{9,1},{2,10},{10,2},{3,11},{11,3},{4,12},{12,4},... | collective-permute-start | bytes 933896 | tf_op jit(solution)/shard_map/ppermute | solution.py:225
  29.4 55.7 %copy-start.2 = (bf16[304,512]{1,0:T(8,128)(2,1)}, bf16[304,512]{1,0:T(8,128)(2,1)S(1)}, u32[]{:S(2)}) copy-start(bf16[304,512]{1,0:T(8,128)(2,1)S(1)} %collective-permute-done.1.refs_2_) | copy-start | bytes 933892
  29.4 11.8 %collective-permute-start.5 = (bf16[304,512]{1,0:T(8,128)(2,1)S(1)}, bf16[304,512]{1,0:T(8,128)(2,1)S(1)}, u32[]{:S(2)}, u32[]{:S(2)}) collective-permute-start(bf16[304,512]{1,0:T(8,128)(2,1)S(1)} %collective-permute-done.1.refs_2_), channel_id=1, source_target_pairs={{0,1},{1,2},{2,3},{3,4},{4,5},{5,6},{6,7},{7,0},{8,9},{9,10},{10,1... | collective-permute-start | bytes 933896 | tf_op jit(solution)/shard_map/ppermute | solution.py:225
  31.3 11.9 %collective-permute-start.3 = (bf16[304,512]{1,0:T(8,128)(2,1)S(1)}, bf16[304,512]{1,0:T(8,128)(2,1)S(1)}, u32[]{:S(2)}, u32[]{:S(2)}) collective-permute-start(bf16[304,512]{1,0:T(8,128)(2,1)S(1)} %copy-done.1), channel_id=1, source_target_pairs={{0,7},{1,0},{2,1},{3,2},{4,3},{5,4},{6,5},{7,6},{8,15},{9,8},{10,9... | collective-permute-start | bytes 933896 | tf_op jit(solution)/shard_map/ppermute | solution.py:225
  35.9 49.2 %copy-start.3 = (bf16[304,512]{1,0:T(8,128)(2,1)}, bf16[304,512]{1,0:T(8,128)(2,1)S(1)}, u32[]{:S(2)}) copy-start(bf16[304,512]{1,0:T(8,128)(2,1)S(1)} %collective-permute-done.refs_1_) | copy-start | bytes 933892
  35.9 11.9 %collective-permute-start.4 = (bf16[304,512]{1,0:T(8,128)(2,1)S(1)}, bf16[304,512]{1,0:T(8,128)(2,1)S(1)}, u32[]{:S(2)}, u32[]{:S(2)}) collective-permute-start(bf16[304,512]{1,0:T(8,128)(2,1)S(1)} %collective-permute-done.refs_1_), channel_id=1, source_target_pairs={{0,7},{1,0},{2,1},{3,2},{4,3},{5,4},{6,5},{7,6},{8,15},{9,8},{10,9... | collective-permute-start | bytes 933896 | tf_op jit(solution)/shard_map/ppermute | solution.py:225
  37.9 14.8 %collective-permute-start.2 = (bf16[304,512]{1,0:T(8,128)(2,1)S(1)}, bf16[304,512]{1,0:T(8,128)(2,1)S(1)}, u32[]{:S(2)}, u32[]{:S(2)}) collective-permute-start(bf16[304,512]{1,0:T(8,128)(2,1)S(1)} %collective-permute-done.refs_1_), channel_id=1, source_target_pairs={{0,1},{1,2},{2,3},{3,4},{4,5},{5,6},{6,7},{7,0},{8,9},{9,10},{10,1... | collective-permute-start | bytes 933896 | tf_op jit(solution)/shard_map/ppermute | solution.py:225
  41.3 34.0 %copy-start.4 = (bf16[304,512]{1,0:T(8,128)(2,1)}, bf16[304,512]{1,0:T(8,128)(2,1)S(1)}, u32[]{:S(2)}) copy-start(bf16[304,512]{1,0:T(8,128)(2,1)S(1)} %collective-permute-done.5.refs_6_) | copy-start | bytes 933892
  41.3 13.4 %collective-permute-start.9 = (bf16[304,512]{1,0:T(8,128)(2,1)S(1)}, bf16[304,512]{1,0:T(8,128)(2,1)S(1)}, u32[]{:S(2)}, u32[]{:S(2)}) collective-permute-start(bf16[304,512]{1,0:T(8,128)(2,1)S(1)} %collective-permute-done.5.refs_6_), channel_id=1, source_target_pairs={{0,1},{1,2},{2,3},{3,4},{4,5},{5,6},{6,7},{7,0},{8,9},{9,10},{10,1... | collective-permute-start | bytes 933896 | tf_op jit(solution)/shard_map/ppermute | solution.py:225
  43.2 32.0 %copy-start.5 = (bf16[304,512]{1,0:T(8,128)(2,1)}, bf16[304,512]{1,0:T(8,128)(2,1)S(1)}, u32[]{:S(2)}) copy-start(bf16[304,512]{1,0:T(8,128)(2,1)S(1)} %collective-permute-done.3.refs_4_) | copy-start | bytes 933892
  43.2 13.6 %collective-permute-start.7 = (bf16[304,512]{1,0:T(8,128)(2,1)S(1)}, bf16[304,512]{1,0:T(8,128)(2,1)S(1)}, u32[]{:S(2)}, u32[]{:S(2)}) collective-permute-start(bf16[304,512]{1,0:T(8,128)(2,1)S(1)} %collective-permute-done.3.refs_4_), channel_id=1, source_target_pairs={{0,7},{1,0},{2,1},{3,2},{4,3},{5,4},{6,5},{7,6},{8,15},{9,8},{10,9... | collective-permute-start | bytes 933896 | tf_op jit(solution)/shard_map/ppermute | solution.py:225
  47.8 27.4 %copy-start.6 = (bf16[304,512]{1,0:T(8,128)(2,1)}, bf16[304,512]{1,0:T(8,128)(2,1)S(1)}, u32[]{:S(2)}) copy-start(bf16[304,512]{1,0:T(8,128)(2,1)S(1)} %collective-permute-done.4.refs_5_) | copy-start | bytes 933892
  47.8 13.4 %collective-permute-start.8 = (bf16[304,512]{1,0:T(8,128)(2,1)S(1)}, bf16[304,512]{1,0:T(8,128)(2,1)S(1)}, u32[]{:S(2)}, u32[]{:S(2)}) collective-permute-start(bf16[304,512]{1,0:T(8,128)(2,1)S(1)} %collective-permute-done.4.refs_5_), channel_id=1, source_target_pairs={{0,7},{1,0},{2,1},{3,2},{4,3},{5,4},{6,5},{7,6},{8,15},{9,8},{10,9... | collective-permute-start | bytes 933896 | tf_op jit(solution)/shard_map/ppermute | solution.py:225
  52.7 22.5 %copy-start.7 = (bf16[304,512]{1,0:T(8,128)(2,1)}, bf16[304,512]{1,0:T(8,128)(2,1)S(1)}, u32[]{:S(2)}) copy-start(bf16[304,512]{1,0:T(8,128)(2,1)S(1)} %collective-permute-done.2.refs_3_) | copy-start | bytes 933892
  52.7 13.3 %collective-permute-start.6 = (bf16[304,512]{1,0:T(8,128)(2,1)S(1)}, bf16[304,512]{1,0:T(8,128)(2,1)S(1)}, u32[]{:S(2)}, u32[]{:S(2)}) collective-permute-start(bf16[304,512]{1,0:T(8,128)(2,1)S(1)} %collective-permute-done.2.refs_3_), channel_id=1, source_target_pairs={{0,1},{1,2},{2,3},{3,4},{4,5},{5,6},{6,7},{7,0},{8,9},{9,10},{10,1... | collective-permute-start | bytes 933896 | tf_op jit(solution)/shard_map/ppermute | solution.py:225
  54.7 20.6 %copy-start.8 = (bf16[304,512]{1,0:T(8,128)(2,1)}, bf16[304,512]{1,0:T(8,128)(2,1)S(1)}, u32[]{:S(2)}) copy-start(bf16[304,512]{1,0:T(8,128)(2,1)S(1)} %collective-permute-done.9.refs_10_) | copy-start | bytes 933892
  54.7 13.3 %collective-permute-start.11 = (bf16[304,512]{1,0:T(8,128)(2,1)S(1)}, bf16[304,512]{1,0:T(8,128)(2,1)S(1)}, u32[]{:S(2)}, u32[]{:S(2)}) collective-permute-start(bf16[304,512]{1,0:T(8,128)(2,1)S(1)} %collective-permute-done.9.refs_10_), channel_id=1, source_target_pairs={{0,1},{1,2},{2,3},{3,4},{4,5},{5,6},{6,7},{7,0},{8,9},{9,10},{10,1... | collective-permute-start | bytes 933896 | tf_op jit(solution)/shard_map/ppermute | solution.py:225
  56.8 28.3 %copy-start.9 = (bf16[304,512]{1,0:T(8,128)(2,1)}, bf16[304,512]{1,0:T(8,128)(2,1)S(1)}, u32[]{:S(2)}) copy-start(bf16[304,512]{1,0:T(8,128)(2,1)S(1)} %collective-permute-done.7.refs_8_) | copy-start | bytes 933892
  56.8 13.4 %collective-permute-start.10 = (bf16[304,512]{1,0:T(8,128)(2,1)S(1)}, bf16[304,512]{1,0:T(8,128)(2,1)S(1)}, u32[]{:S(2)}, u32[]{:S(2)}) collective-permute-start(bf16[304,512]{1,0:T(8,128)(2,1)S(1)} %collective-permute-done.7.refs_8_), channel_id=1, source_target_pairs={{0,7},{1,0},{2,1},{3,2},{4,3},{5,4},{6,5},{7,6},{8,15},{9,8},{10,9... | collective-permute-start | bytes 933896 | tf_op jit(solution)/shard_map/ppermute | solution.py:225
  61.2 14.0 %copy-start.10 = (bf16[304,512]{1,0:T(8,128)(2,1)}, bf16[304,512]{1,0:T(8,128)(2,1)S(1)}, u32[]{:S(2)}) copy-start(bf16[304,512]{1,0:T(8,128)(2,1)S(1)} %collective-permute-done.8.refs_9_) | copy-start | bytes 933892
  61.2 11.6 %collective-permute-start.13 = (bf16[304,512]{1,0:T(8,128)(2,1)S(1)}, bf16[304,512]{1,0:T(8,128)(2,1)S(1)}, u32[]{:S(2)}, u32[]{:S(2)}) collective-permute-start(bf16[304,512]{1,0:T(8,128)(2,1)S(1)} %collective-permute-done.8.refs_9_), channel_id=1, source_target_pairs={{0,7},{1,0},{2,1},{3,2},{4,3},{5,4},{6,5},{7,6},{8,15},{9,8},{10,9... | collective-permute-start | bytes 933896 | tf_op jit(solution)/shard_map/ppermute | solution.py:225
  66.0 9.3 %copy-start.11 = (bf16[304,512]{1,0:T(8,128)(2,1)}, bf16[304,512]{1,0:T(8,128)(2,1)S(1)}, u32[]{:S(2)}) copy-start(bf16[304,512]{1,0:T(8,128)(2,1)S(1)} %collective-permute-done.6.refs_7_) | copy-start | bytes 933892
  66.0 9.2 %collective-permute-start.12 = (bf16[304,512]{1,0:T(8,128)(2,1)S(1)}, bf16[304,512]{1,0:T(8,128)(2,1)S(1)}, u32[]{:S(2)}, u32[]{:S(2)}) collective-permute-start(bf16[304,512]{1,0:T(8,128)(2,1)S(1)} %collective-permute-done.6.refs_7_), channel_id=1, source_target_pairs={{0,1},{1,2},{2,3},{3,4},{4,5},{5,6},{6,7},{7,0},{8,9},{9,10},{10,1... | collective-permute-start | bytes 933896 | tf_op jit(solution)/shard_map/ppermute | solution.py:225
  68.0 7.3 %copy-start.12 = (bf16[304,512]{1,0:T(8,128)(2,1)}, bf16[304,512]{1,0:T(8,128)(2,1)S(1)}, u32[]{:S(2)}) copy-start(bf16[304,512]{1,0:T(8,128)(2,1)S(1)} %collective-permute-done.11.refs_14_) | copy-start | bytes 933892
  68.0 13.3 %collective-permute-start.14 = (bf16[304,512]{1,0:T(8,128)(2,1)S(1)}, bf16[304,512]{1,0:T(8,128)(2,1)}, u32[]{:S(2)}, u32[]{:S(2)}) collective-permute-start(bf16[304,512]{1,0:T(8,128)(2,1)S(1)} %collective-permute-done.11.refs_14_), channel_id=1, source_target_pairs={{0,8},{8,0},{1,9},{9,1},{2,10},{10,2},{3,11},{11,3},{4,12},{12,4},... | collective-permute-start | bytes 933896 | tf_op jit(solution)/shard_map/ppermute | solution.py:225
  70.2 5.1 %copy-start.13 = (bf16[304,512]{1,0:T(8,128)(2,1)}, bf16[304,512]{1,0:T(8,128)(2,1)S(1)}, u32[]{:S(2)}) copy-start(bf16[304,512]{1,0:T(8,128)(2,1)S(1)} %collective-permute-done.10.refs_12_) | copy-start | bytes 933892
  72.9 2.4 %copy-start.14 = (bf16[304,512]{1,0:T(8,128)(2,1)}, bf16[304,512]{1,0:T(8,128)(2,1)S(1)}, u32[]{:S(2)}) copy-start(bf16[304,512]{1,0:T(8,128)(2,1)S(1)} %collective-permute-done.13.refs_13_) | copy-start | bytes 933892
  75.3 0.7 copy-start.15
  81.3 3.8 %copy-start = (bf16[16,152,512]{2,1,0:T(8,128)(2,1)}, bf16[16,152,512]{2,1,0:T(8,128)(2,1)S(1)}, u32[]{:S(2)}) copy-start(bf16[16,152,512]{2,1,0:T(8,128)(2,1)S(1)} %all-to-all-done.refs_15_.refs_16_) | copy-start | bytes 7471108
  81.3 9.8 %collective-permute-start.15 = (bf16[16,152,512]{2,1,0:T(8,128)(2,1)S(1)}, bf16[16,152,512]{2,1,0:T(8,128)(2,1)}, u32[]{:S(2)}, u32[]{:S(2)}) collective-permute-start(bf16[16,152,512]{2,1,0:T(8,128)(2,1)S(1)} %all-to-all-done.refs_15_.refs_16_), channel_id=1, source_target_pairs={{0,16},{16,0},{1,17},{17,1},{2,18},{18,2},{3,19},{19,3},{4,20},{20... | collective-permute-start | bytes 7471112 | tf_op jit(solution)/shard_map/ppermute | solution.py:225

commit v6 on v5

--- a/solution.py
+++ b/solution.py
@@ -22,6 +22,7 @@
 NY = 8
 TURNS = (0, -1, 1, -2, 2, -3, 3, 4)
 STEP = 4
+DIMS = (((0,), (0,)), ((), ()))
 VMEM = pl.BlockSpec(memory_space=pltpu.VMEM)
 SMEM = pl.BlockSpec(memory_space=pltpu.SMEM)
 ANY = pl.BlockSpec(memory_space=pl.ANY)
@@ -66,7 +67,7 @@
     )(down_blocks, dec_t, deltas, encoder, gradients)
 
 
-def accumulate(items, up_ref, dec, enc, dec_sem, enc_sem):
+def accumulate(items, tokens, dec, enc, dec_sem, enc_sem):
     chunks = [range(low, min(low + STEP, len(items))) for low in range(0, len(items), STEP)]
     if len(chunks[-1]) == 1:
         chunks[-2:] = [range(chunks[-2].start, len(items))]
@@ -74,13 +75,13 @@
         for slot in chunk:
             shard, k, part, source = items[slot]
             rows = pl.ds(pl.multiple_of(part * KE, 16), KE)
-            tokens = pl.ds(pl.multiple_of(KD + part * TE, TE), TE)
             here = dec.at[slot]
-            pltpu.make_async_copy(source.at[k], enc.at[slot], enc_sem.at[n]).start()
+            pltpu.make_async_copy(
+                source.at[k, : enc.shape[1]], enc.at[slot], enc_sem.at[n]
+            ).start()
             pltpu.make_async_copy(shard.at[rows], here.at[:KE], dec_sem.at[n]).start()
-            pltpu.make_async_copy(shard.at[tokens], here.at[KE:], dec_sem.at[n]).start()
-    dims = (((0,), (0,)), ((), ()))
-    cols = DACT * BLOCK
+            if tokens:
+                pltpu.make_async_copy(shard.at[KD:], here.at[KE:], dec_sem.at[n]).start()
     virtual = None
     for n, chunk in enumerate(chunks):
         at = slice(chunk.start, chunk.stop)
@@ -88,21 +89,12 @@
         pltpu.make_async_copy(enc.at[at], enc.at[at], enc_sem.at[n]).wait()
         term = lax.dot_general(
             dec[at, :KE].reshape(len(chunk) * KE, UF_DEV),
-            enc[at, :KE].reshape(len(chunk) * KE, cols),
-            dims,
+            enc[at, :KE].reshape(len(chunk) * KE, DACT * BLOCK),
+            DIMS,
             preferred_element_type=jnp.float32,
         )
         virtual = term if virtual is None else virtual + term
-    lane_block = lax.broadcasted_iota(jnp.int32, (TE, UF_DEV), 1) // BLOCK
-    masked, kept = [], []
-    for slot, (_, k, _, _) in enumerate(items):
-        w = k // 2
-        on = (lane_block == up_ref[0, w]) | (lane_block == up_ref[1, w])
-        masked.append(jnp.where(on, dec[slot, KE:].astype(jnp.float32), 0.0))
-        kept.append(enc[slot, KE:].astype(jnp.float32))
-    masked, kept = (jnp.concatenate(v, 0).astype(jnp.bfloat16) for v in (masked, kept))
-    product = lax.dot_general(masked, kept, dims, preferred_element_type=jnp.float32)
-    return virtual, product
+    return virtual
 
 
 def places():
@@ -113,21 +105,19 @@
     ]
 
 
-def half_kernel(up_ref, *refs):
+def half_kernel(*refs):
     shards, refs = refs[: 2 * NY - 1], refs[2 * NY - 1 :]
-    source, virtual_ref, product_ref, dec, enc, dec_sem, enc_sem = refs
+    source, virtual_ref, dec, enc, dec_sem, enc_sem = refs
     core = lax.axis_index("c")
     items = [(shard, k, core, source) for shard, k in zip(shards, places())]
-    virtual_ref[...], product_ref[...] = accumulate(
-        items, up_ref, dec, enc, dec_sem, enc_sem
-    )
+    virtual_ref[...] = accumulate(items, False, dec, enc, dec_sem, enc_sem)
 
 
 def score_kernel(up_ref, down_ref, *refs):
     shards, refs = refs[: 2 * NY], refs[2 * NY :]
-    own, swapped, virtual_in, product_in, out_ref = refs[:5]
-    dec, enc, dec_sem, enc_sem, virtual, product, zero, scored = refs[5:13]
-    in_sem, zero_sem, out_sem = refs[13:]
+    own, swapped, virtual_in, out_ref = refs[:4]
+    dec, enc, dec_sem, enc_sem, virtual, grad, zero, scored = refs[4:12]
+    in_sem, zero_sem, out_sem = refs[12:]
     zero[...] = jnp.zeros_like(zero)
 
     def blank(b):
@@ -143,22 +133,31 @@
         idle.append(jnp.logical_not(used))
     loads = [
         pltpu.make_async_copy(virtual_in, virtual, in_sem.at[0]),
-        pltpu.make_async_copy(product_in, product, in_sem.at[1]),
+        pltpu.make_async_copy(own.at[:, KE:], grad, in_sem.at[1]),
     ]
     for copy in loads:
         copy.start()
     core, ks = lax.axis_index("c"), places()
     items = [(shard, k, 1 - core, swapped) for shard, k in zip(shards, ks)]
     items.append((shards[-1], ks[-1], core, own))
-    more, part = accumulate(items, up_ref, dec, enc, dec_sem, enc_sem)
+    more = accumulate(items, True, dec, enc, dec_sem, enc_sem)
     for b in range(VF_DEV // BLOCK):
         pl.when(idle[b])(blank(b).start)
     for copy in loads:
         copy.wait()
+    lane_block = lax.broadcasted_iota(jnp.int32, (TD, UF_DEV), 1) // BLOCK
+    masked, kept = [], []
+    for slot, k in enumerate(ks):
+        on = (lane_block == up_ref[0, k // 2]) | (lane_block == up_ref[1, k // 2])
+        masked.append(jnp.where(on, dec[slot, KE:].astype(jnp.float32), 0.0))
+        mine, theirs = grad[k].astype(jnp.float32), enc[slot, KE:].astype(jnp.float32)
+        kept += [jnp.where(core == 0, mine, theirs), jnp.where(core == 0, theirs, mine)]
+    masked, kept = (jnp.concatenate(v, 0).astype(jnp.bfloat16) for v in (masked, kept))
+    product = lax.dot_general(masked, kept, DIMS, preferred_element_type=jnp.float32)
     filled = []
     for i in range(DACT):
         at = slice(i * BLOCK, (i + 1) * BLOCK)
-        scored[i] = (product[:, at] + part[:, at]) * (virtual[:, at] + more[:, at])
+        scored[i] = product[:, at] * (virtual[:, at] + more[:, at])
         where = pl.ds(pl.multiple_of(down_ref[i] * BLOCK, BLOCK), BLOCK)
         filled.append(
             pltpu.make_async_copy(scored.at[i], out_ref.at[:, where], out_sem.at[i])
@@ -173,10 +172,10 @@
 COLS = DACT * BLOCK
 
 
-def held(count):
+def held(count, tokens, grads):
     return [
-        pltpu.VMEM((count, RE, UF_DEV), jnp.bfloat16),
-        pltpu.VMEM((count, RE, COLS), jnp.bfloat16),
+        pltpu.VMEM((count, KE + tokens, UF_DEV), jnp.bfloat16),
+        pltpu.VMEM((count, KE + grads, COLS), jnp.bfloat16),
         pltpu.SemaphoreType.DMA((-(-count // STEP),)),
         pltpu.SemaphoreType.DMA((-(-count // STEP),)),
     ]
@@ -187,28 +186,28 @@
 )
 
 
-def half(up_t, shards, source):
+def half(shards, source):
     return pl.pallas_call(
         half_kernel,
-        out_shape=(jax.ShapeDtypeStruct((UF_DEV, COLS), jnp.float32),) * 2,
-        in_specs=[SMEM] + [ANY] * (2 * NY),
-        out_specs=(VMEM, VMEM),
-        scratch_shapes=held(2 * NY - 1),
+        out_shape=jax.ShapeDtypeStruct((UF_DEV, COLS), jnp.float32),
+        in_specs=[ANY] * (2 * NY),
+        out_specs=VMEM,
+        scratch_shapes=held(2 * NY - 1, 0, 0),
         compiler_params=pltpu.CompilerParams(vmem_limit_bytes=60 << 20),
         cost_estimate=COST,
-    )(up_t, *shards, source)
-
-
-def score(up_t, down_blocks, shards, own, swapped, sums):
+    )(*shards, source)
+
+
+def score(up_t, down_blocks, shards, own, swapped, total):
     return pl.pallas_call(
         score_kernel,
         out_shape=jax.ShapeDtypeStruct((UF_DEV, VF_DEV), jnp.float32),
-        in_specs=[SMEM, SMEM] + [ANY] * (2 * NY + 4),
+        in_specs=[SMEM, SMEM] + [ANY] * (2 * NY + 3),
         out_specs=ANY,
         scratch_shapes=[
-            *held(2 * NY + 1),
+            *held(2 * NY + 1, TD, TE),
             pltpu.VMEM((UF_DEV, COLS), jnp.float32),
-            pltpu.VMEM((UF_DEV, COLS), jnp.float32),
+            pltpu.VMEM((2 * NY, TE, COLS), jnp.bfloat16),
             pltpu.VMEM((UF_DEV, BLOCK), jnp.float32),
             pltpu.VMEM((DACT, UF_DEV, BLOCK), jnp.float32),
             pltpu.SemaphoreType.DMA((2,)),
@@ -217,7 +216,7 @@
         ],
         compiler_params=pltpu.CompilerParams(vmem_limit_bytes=60 << 20),
         cost_estimate=COST,
-    )(up_t, down_blocks, *shards, own, swapped, *sums)
+    )(up_t, down_blocks, *shards, own, swapped, total)
 
 
 def turn(value, axis, by):
@@ -246,8 +245,8 @@
     shards = [shard for both in zip(near, across) for shard in both]
     swapped = turn(own, "c", 1)
     up_t = up_blocks.T
-    sums = half(up_t, shards[:-1], own)
-    return score(up_t, down_blocks, shards, own, swapped, sums)
+    total = half(shards[:-1], own)
+    return score(up_t, down_blocks, shards, own, swapped, total)
 
 
 def solution(mesh):

time: 97.9 us -> 96.9 us (0.990)
  Pallas kernels: 16 us -> 15 us
    pallas_call x1, Pallas kernels: 5.94 us -> 4.65 us  [half(): pl.pallas_call(half_kernel, out_shape=jax.ShapeDtypeStruct((UF_DEV, COLS)...]
  transfers between devices with their start and end apart: 17 -> 17, of which waited for: 4 -> 4; matrix products, arithmetic and copies ran while one was open for 0% -> 0% of each run, Pallas kernels for 6% -> 5%
where the time goes in v6:
time: 96.9 us; the launch traced here: 96.2 us
  starting transfers between devices  63.3 us (65%)
  waiting for transfers between devices  16.7 us (17%)
  Pallas kernels  15 us (15%)
    ppermute x16, starting transfers between devices, turn(): return lax.ppermute(value, axis, [(i, (i + by) % n) for i in range(n)])  49.7 us
    ppermute x16, waiting for transfers between devices, turn(): return lax.ppermute(value, axis, [(i, (i + by) % n) for i in range(n)])  16.7 us
    all_to_all x1, starting transfers between devices, local(): own = lax.all_to_all(e, ('z', 'xh'), 0, 0, tiled=True)  13.6 us
    pallas_call x1, Pallas kernels, score(): pl.pallas_call(score_kernel, out_shape=jax.ShapeDtypeStruct((UF_DEV, VF_D...  6.37 us
    pallas_call x1, Pallas kernels, half(): pl.pallas_call(half_kernel, out_shape=jax.ShapeDtypeStruct((UF_DEV, COLS)...  4.65 us
    pallas_call x1, Pallas kernels, pack(): pl.pallas_call(pack_kernel, out_shape=(jax.ShapeDtypeStruct((RD, UF_DEV),...  3.96 us
  transfers between devices with their start and end apart: 17, of which 4 were waited for; matrix products, arithmetic and copies ran while one was open for 0% of the time, Pallas kernels for 5%

profile of v6, /device:TPU:1, one launch (start us, length us, event | category | flops | bytes accessed | tf_op | source)
XLA Modules:
  0.0 96.2 jit_solution(3847616579948393931)
XLA Ops:
  0.0 4.0 %shard_map.64 = (bf16[304,512]{1,0:T(8,128)(2,1)}, bf16[16,152,512]{2,1,0:T(8,128)(2,1)}) custom-call(s32[4]{0:T(128)} %down_ref.3, bf16[288,512]{1,0:T(8,128)(2,1)} %bitcast.2, bf16[16,512]{1,0:T(8,128)(2,1)} %delta_ref.1, bf16[144,1024]{1,0:T(8,128)(2,1)} %enc_ref.1, bf16[8,1024]{1,0:T(8,128)(2,1)} %grad_ref.1), custom_call_target="tpu_custom_call" | custom-call | tf_op jit(solution)/shard_map/pallas_call | solution.py:54
  4.0 0.0 copy-start.1
  4.0 13.6 %all-to-all-start = ((bf16[16,152,512]{2,1,0:T(8,128)(2,1)}), bf16[16,152,512]{2,1,0:T(8,128)(2,1)S(1)}, u32[]{:S(2)}, u32[]{:S(2)}) async-start(bf16[16,152,512]{2,1,0:T(8,128)(2,1)} %get-tuple-element.15), calls=%async_computation | async-start | bytes 4980736 | tf_op jit(solution)/shard_map/all_to_all | solution.py:233
  17.6 0.0 copy-done.1
  17.6 3.2 %collective-permute-start.1 = (bf16[304,512]{1,0:T(8,128)(2,1)S(1)}, bf16[304,512]{1,0:T(8,128)(2,1)S(1)}, u32[]{:S(2)}, u32[]{:S(2)}) collective-permute-start(bf16[304,512]{1,0:T(8,128)(2,1)S(1)} %copy-done.1), channel_id=1, source_target_pairs={{0,1},{1,2},{2,3},{3,4},{4,5},{5,6},{6,7},{7,0},{8,9},{9,10},{10,1... | collective-permute-start | bytes 933896 | tf_op jit(solution)/shard_map/ppermute | solution.py:224
  20.8 2.2 %collective-permute-start = (bf16[304,512]{1,0:T(8,128)(2,1)S(1)}, bf16[304,512]{1,0:T(8,128)(2,1)S(1)}, u32[]{:S(2)}, u32[]{:S(2)}) collective-permute-start(bf16[304,512]{1,0:T(8,128)(2,1)S(1)} %copy-done.1), channel_id=1, source_target_pairs={{0,8},{8,0},{1,9},{9,1},{2,10},{10,2},{3,11},{11,3},{4,12},{12,4},... | collective-permute-start | bytes 933896 | tf_op jit(solution)/shard_map/ppermute | solution.py:224
  23.0 6.4 %collective-permute-done.1.refs_2_ = bf16[304,512]{1,0:T(8,128)(2,1)S(1)} collective-permute-done((bf16[304,512]{1,0:T(8,128)(2,1)S(1)}, bf16[304,512]{1,0:T(8,128)(2,1)S(1)}, u32[]{:S(2)}, u32[]{:S(2)}) %collective-permute-start.1) | collective-permute-done | bytes 311328 | tf_op jit(solution)/shard_map/ppermute | solution.py:224
  29.4 1.9 %collective-permute-start.5 = (bf16[304,512]{1,0:T(8,128)(2,1)S(1)}, bf16[304,512]{1,0:T(8,128)(2,1)S(1)}, u32[]{:S(2)}, u32[]{:S(2)}) collective-permute-start(bf16[304,512]{1,0:T(8,128)(2,1)S(1)} %collective-permute-done.1.refs_2_), channel_id=1, source_target_pairs={{0,1},{1,2},{2,3},{3,4},{4,5},{5,6},{6,7},{7,0},{8,9},{9,10},{10,1... | collective-permute-start | bytes 933896 | tf_op jit(solution)/shard_map/ppermute | solution.py:224
  31.3 4.6 %collective-permute-start.3 = (bf16[304,512]{1,0:T(8,128)(2,1)S(1)}, bf16[304,512]{1,0:T(8,128)(2,1)S(1)}, u32[]{:S(2)}, u32[]{:S(2)}) collective-permute-start(bf16[304,512]{1,0:T(8,128)(2,1)S(1)} %copy-done.1), channel_id=1, source_target_pairs={{0,7},{1,0},{2,1},{3,2},{4,3},{5,4},{6,5},{7,6},{8,15},{9,8},{10,9... | collective-permute-start | bytes 933896 | tf_op jit(solution)/shard_map/ppermute | solution.py:224
  35.9 0.0 collective-permute-done.refs_1_
  35.9 0.0 copy-start.3
  35.9 1.9 %collective-permute-start.4 = (bf16[304,512]{1,0:T(8,128)(2,1)S(1)}, bf16[304,512]{1,0:T(8,128)(2,1)S(1)}, u32[]{:S(2)}, u32[]{:S(2)}) collective-permute-start(bf16[304,512]{1,0:T(8,128)(2,1)S(1)} %collective-permute-done.refs_1_), channel_id=1, source_target_pairs={{0,7},{1,0},{2,1},{3,2},{4,3},{5,4},{6,5},{7,6},{8,15},{9,8},{10,9... | collective-permute-start | bytes 933896 | tf_op jit(solution)/shard_map/ppermute | solution.py:224
  37.9 3.4 %collective-permute-start.2 = (bf16[304,512]{1,0:T(8,128)(2,1)S(1)}, bf16[304,512]{1,0:T(8,128)(2,1)S(1)}, u32[]{:S(2)}, u32[]{:S(2)}) collective-permute-start(bf16[304,512]{1,0:T(8,128)(2,1)S(1)} %collective-permute-done.refs_1_), channel_id=1, source_target_pairs={{0,1},{1,2},{2,3},{3,4},{4,5},{5,6},{6,7},{7,0},{8,9},{9,10},{10,1... | collective-permute-start | bytes 933896 | tf_op jit(solution)/shard_map/ppermute | solution.py:224
  41.2 0.0 collective-permute-done.5.refs_6_
  41.3 0.0 copy-start.4
  41.3 1.9 %collective-permute-start.9 = (bf16[304,512]{1,0:T(8,128)(2,1)S(1)}, bf16[304,512]{1,0:T(8,128)(2,1)S(1)}, u32[]{:S(2)}, u32[]{:S(2)}) collective-permute-start(bf16[304,512]{1,0:T(8,128)(2,1)S(1)} %collective-permute-done.5.refs_6_), channel_id=1, source_target_pairs={{0,1},{1,2},{2,3},{3,4},{4,5},{5,6},{6,7},{7,0},{8,9},{9,10},{10,1... | collective-permute-start | bytes 933896 | tf_op jit(solution)/shard_map/ppermute | solution.py:224
  43.2 0.0 collective-permute-done.3.refs_4_
  43.2 0.0 copy-start.5
  43.2 4.6 %collective-permute-start.7 = (bf16[304,512]{1,0:T(8,128)(2,1)S(1)}, bf16[304,512]{1,0:T(8,128)(2,1)S(1)}, u32[]{:S(2)}, u32[]{:S(2)}) collective-permute-start(bf16[304,512]{1,0:T(8,128)(2,1)S(1)} %collective-permute-done.3.refs_4_), channel_id=1, source_target_pairs={{0,7},{1,0},{2,1},{3,2},{4,3},{5,4},{6,5},{7,6},{8,15},{9,8},{10,9... | collective-permute-start | bytes 933896 | tf_op jit(solution)/shard_map/ppermute | solution.py:224
  47.8 0.0 collective-permute-done.4.refs_5_
  47.8 0.0 copy-start.6
  47.8 4.9 %collective-permute-start.8 = (bf16[304,512]{1,0:T(8,128)(2,1)S(1)}, bf16[304,512]{1,0:T(8,128)(2,1)S(1)}, u32[]{:S(2)}, u32[]{:S(2)}) collective-permute-start(bf16[304,512]{1,0:T(8,128)(2,1)S(1)} %collective-permute-done.4.refs_5_), channel_id=1, source_target_pairs={{0,7},{1,0},{2,1},{3,2},{4,3},{5,4},{6,5},{7,6},{8,15},{9,8},{10,9... | collective-permute-start | bytes 933896 | tf_op jit(solution)/shard_map/ppermute | solution.py:224
  52.7 0.0 collective-permute-done.2.refs_3_
  52.7 0.0 copy-start.7
  52.7 1.9 %collective-permute-start.6 = (bf16[304,512]{1,0:T(8,128)(2,1)S(1)}, bf16[304,512]{1,0:T(8,128)(2,1)S(1)}, u32[]{:S(2)}, u32[]{:S(2)}) collective-permute-start(bf16[304,512]{1,0:T(8,128)(2,1)S(1)} %collective-permute-done.2.refs_3_), channel_id=1, source_target_pairs={{0,1},{1,2},{2,3},{3,4},{4,5},{5,6},{6,7},{7,0},{8,9},{9,10},{10,1... | collective-permute-start | bytes 933896 | tf_op jit(solution)/shard_map/ppermute | solution.py:224
  54.7 0.0 collective-permute-done.9.refs_10_
  54.7 0.0 copy-start.8
  54.7 2.1 %collective-permute-start.11 = (bf16[304,512]{1,0:T(8,128)(2,1)S(1)}, bf16[304,512]{1,0:T(8,128)(2,1)S(1)}, u32[]{:S(2)}, u32[]{:S(2)}) collective-permute-start(bf16[304,512]{1,0:T(8,128)(2,1)S(1)} %collective-permute-done.9.refs_10_), channel_id=1, source_target_pairs={{0,1},{1,2},{2,3},{3,4},{4,5},{5,6},{6,7},{7,0},{8,9},{9,10},{10,1... | collective-permute-start | bytes 933896 | tf_op jit(solution)/shard_map/ppermute | solution.py:224
  56.8 0.0 collective-permute-done.7.refs_8_
  56.8 0.0 copy-start.9
  56.8 4.4 %collective-permute-start.10 = (bf16[304,512]{1,0:T(8,128)(2,1)S(1)}, bf16[304,512]{1,0:T(8,128)(2,1)S(1)}, u32[]{:S(2)}, u32[]{:S(2)}) collective-permute-start(bf16[304,512]{1,0:T(8,128)(2,1)S(1)} %collective-permute-done.7.refs_8_), channel_id=1, source_target_pairs={{0,7},{1,0},{2,1},{3,2},{4,3},{5,4},{6,5},{7,6},{8,15},{9,8},{10,9... | collective-permute-start | bytes 933896 | tf_op jit(solution)/shard_map/ppermute | solution.py:224
  61.2 0.0 collective-permute-done.8.refs_9_
  61.2 0.0 copy-start.10
  61.2 4.8 %collective-permute-start.13 = (bf16[304,512]{1,0:T(8,128)(2,1)S(1)}, bf16[304,512]{1,0:T(8,128)(2,1)S(1)}, u32[]{:S(2)}, u32[]{:S(2)}) collective-permute-start(bf16[304,512]{1,0:T(8,128)(2,1)S(1)} %collective-permute-done.8.refs_9_), channel_id=1, source_target_pairs={{0,7},{1,0},{2,1},{3,2},{4,3},{5,4},{6,5},{7,6},{8,15},{9,8},{10,9... | collective-permute-start | bytes 933896 | tf_op jit(solution)/shard_map/ppermute | solution.py:224
  66.0 0.0 collective-permute-done.6.refs_7_
  66.0 0.0 copy-start.11
  66.0 1.9 %collective-permute-start.12 = (bf16[304,512]{1,0:T(8,128)(2,1)S(1)}, bf16[304,512]{1,0:T(8,128)(2,1)S(1)}, u32[]{:S(2)}, u32[]{:S(2)}) collective-permute-start(bf16[304,512]{1,0:T(8,128)(2,1)S(1)} %collective-permute-done.6.refs_7_), channel_id=1, source_target_pairs={{0,1},{1,2},{2,3},{3,4},{4,5},{5,6},{6,7},{7,0},{8,9},{9,10},{10,1... | collective-permute-start | bytes 933896 | tf_op jit(solution)/shard_map/ppermute | solution.py:224
  68.0 0.0 collective-permute-done.11.refs_14_
  68.0 0.0 copy-start.12
  68.0 2.2 %collective-permute-start.14 = (bf16[304,512]{1,0:T(8,128)(2,1)S(1)}, bf16[304,512]{1,0:T(8,128)(2,1)}, u32[]{:S(2)}, u32[]{:S(2)}) collective-permute-start(bf16[304,512]{1,0:T(8,128)(2,1)S(1)} %collective-permute-done.11.refs_14_), channel_id=1, source_target_pairs={{0,8},{8,0},{1,9},{9,1},{2,10},{10,2},{3,11},{11,3},{4,12},{12,4},... | collective-permute-start | bytes 933896 | tf_op jit(solution)/shard_map/ppermute | solution.py:224
  70.2 0.0 collective-permute-done.10.refs_12_
  70.2 0.0 copy-start.13
  70.2 2.6 %collective-permute-done.13.refs_13_ = bf16[304,512]{1,0:T(8,128)(2,1)S(1)} collective-permute-done((bf16[304,512]{1,0:T(8,128)(2,1)S(1)}, bf16[304,512]{1,0:T(8,128)(2,1)S(1)}, u32[]{:S(2)}, u32[]{:S(2)}) %collective-permute-start.13) | collective-permute-done | bytes 311328 | tf_op jit(solution)/shard_map/ppermute | solution.py:224
  72.9 2.4 %collective-permute-done.12.refs_11_ = bf16[304,512]{1,0:T(8,128)(2,1)S(1)} collective-permute-done((bf16[304,512]{1,0:T(8,128)(2,1)S(1)}, bf16[304,512]{1,0:T(8,128)(2,1)S(1)}, u32[]{:S(2)}, u32[]{:S(2)}) %collective-permute-start.12) | collective-permute-done | bytes 311328 | tf_op jit(solution)/shard_map/ppermute | solution.py:224
  75.2 0.0 copy-done.4
  75.2 0.0 copy-done.5
  75.2 0.0 copy-done.6
  75.2 0.0 copy-done.7
  75.2 0.0 copy-done.8
  75.3 0.0 copy-done.10
  75.3 0.0 copy-done.11
  75.3 0.0 copy-done.12
  75.3 0.0 copy-done.13
  75.3 0.7 copy-done.15
  76.0 5.2 %collective-permute-done.14.refs_15_ = bf16[304,512]{1,0:T(8,128)(2,1)} collective-permute-done((bf16[304,512]{1,0:T(8,128)(2,1)S(1)}, bf16[304,512]{1,0:T(8,128)(2,1)}, u32[]{:S(2)}, u32[]{:S(2)}) %collective-permute-start.14) | collective-permute-done | bytes 311328 | tf_op jit(solution)/shard_map/ppermute | solution.py:224
  81.3 0.0 all-to-all-done.refs_15_.refs_16_
  81.3 3.8 %collective-permute-start.15 = (bf16[16,152,512]{2,1,0:T(8,128)(2,1)S(1)}, bf16[16,152,512]{2,1,0:T(8,128)(2,1)}, u32[]{:S(2)}, u32[]{:S(2)}) collective-permute-start(bf16[16,152,512]{2,1,0:T(8,128)(2,1)S(1)} %all-to-all-done.refs_15_.refs_16_), channel_id=1, source_target_pairs={{0,16},{16,0},{1,17},{17,1},{2,18},{18,2},{3,19},{19,3},{4,20},{20... | collective-permute-start | bytes 7471112 | tf_op jit(solution)/shard_map/ppermute | solution.py:224
  85.1 0.0 copy-done.2
  85.1 0.0 copy-done.3
  85.1 0.0 copy-done.9
  85.1 0.0 copy-done
  85.1 4.6 %shard_map.65.refs_18_ = f32[512,512]{1,0:T(8,128)} custom-call(bf16[304,512]{1,0:T(8,128)(2,1)} %get-tuple-element.14.refs_0_, bf16[304,512]{1,0:T(8,128)(2,1)} %copy-done.3, bf16[304,512]{1,0:T(8,128)(2,1)} %copy-done.2, bf16[304,512]{1,0:T(8,128)(2,1)} %copy-done.7, bf16[304,512]{1,0:T(8,128)(2,1)} %copy-done.5, bf16[304,512]{1,0:T(8,128)(2,1)} %copy-done.6, ...), custom_call_target="tpu_custom_call" | custom-call | flops 1207959552 | bytes 8388608 | tf_op jit(solution)/shard_map/pallas_call | solution.py:190
  89.8 0.0 collective-permute-done.15.refs_17_
  89.8 6.4 %shard_map.66 = f32[512,1024]{1,0:T(8,128)} custom-call(s32[2,8]{1,0:T(2,128)} %bitcast.3, s32[4]{0:T(128)} %down_ref.3, bf16[304,512]{1,0:T(8,128)(2,1)} %get-tuple-element.14.refs_0_, bf16[304,512]{1,0:T(8,128)(2,1)} %copy-done.3, bf16[304,512]{1,0:T(8,128)(2,1)} %copy-done.2, bf16[304,512]{1,0:T(8,128)(2,1)} %copy-done.7, bf16[304,512]{1,0:T(8,128)(2,1)} %copy-done.5, ...), custom_call_target="tpu_custom_call" | custom-call | flops 1207959552 | bytes 8388608 | tf_op jit(solution)/shard_map/pallas_call | solution.py:202
  (5 shorter events, 0.0 us)
Async XLA Ops:
  4.0 13.6 %copy-start.1 = (bf16[304,512]{1,0:T(8,128)(2,1)S(1)}, bf16[304,512]{1,0:T(8,128)(2,1)}, u32[]{:S(2)}) copy-start(bf16[304,512]{1,0:T(8,128)(2,1)} %get-tuple-element.14.refs_0_) | copy-start | bytes 933892
  4.0 77.3 %all-to-all-start = ((bf16[16,152,512]{2,1,0:T(8,128)(2,1)}), bf16[16,152,512]{2,1,0:T(8,128)(2,1)S(1)}, u32[]{:S(2)}, u32[]{:S(2)}) async-start(bf16[16,152,512]{2,1,0:T(8,128)(2,1)} %get-tuple-element.15), calls=%async_computation | async-start | bytes 4980736 | tf_op jit(solution)/shard_map/all_to_all | solution.py:233
  17.6 11.9 %collective-permute-start.1 = (bf16[304,512]{1,0:T(8,128)(2,1)S(1)}, bf16[304,512]{1,0:T(8,128)(2,1)S(1)}, u32[]{:S(2)}, u32[]{:S(2)}) collective-permute-start(bf16[304,512]{1,0:T(8,128)(2,1)S(1)} %copy-done.1), channel_id=1, source_target_pairs={{0,1},{1,2},{2,3},{3,4},{4,5},{5,6},{6,7},{7,0},{8,9},{9,10},{10,1... | collective-permute-start | bytes 933896 | tf_op jit(solution)/shard_map/ppermute | solution.py:224
  20.8 15.1 %collective-permute-start = (bf16[304,512]{1,0:T(8,128)(2,1)S(1)}, bf16[304,512]{1,0:T(8,128)(2,1)S(1)}, u32[]{:S(2)}, u32[]{:S(2)}) collective-permute-start(bf16[304,512]{1,0:T(8,128)(2,1)S(1)} %copy-done.1), channel_id=1, source_target_pairs={{0,8},{8,0},{1,9},{9,1},{2,10},{10,2},{3,11},{11,3},{4,12},{12,4},... | collective-permute-start | bytes 933896 | tf_op jit(solution)/shard_map/ppermute | solution.py:224
  29.4 55.7 %copy-start.2 = (bf16[304,512]{1,0:T(8,128)(2,1)}, bf16[304,512]{1,0:T(8,128)(2,1)S(1)}, u32[]{:S(2)}) copy-start(bf16[304,512]{1,0:T(8,128)(2,1)S(1)} %collective-permute-done.1.refs_2_) | copy-start | bytes 933892
  29.4 11.8 %collective-permute-start.5 = (bf16[304,512]{1,0:T(8,128)(2,1)S(1)}, bf16[304,512]{1,0:T(8,128)(2,1)S(1)}, u32[]{:S(2)}, u32[]{:S(2)}) collective-permute-start(bf16[304,512]{1,0:T(8,128)(2,1)S(1)} %collective-permute-done.1.refs_2_), channel_id=1, source_target_pairs={{0,1},{1,2},{2,3},{3,4},{4,5},{5,6},{6,7},{7,0},{8,9},{9,10},{10,1... | collective-permute-start | bytes 933896 | tf_op jit(solution)/shard_map/ppermute | solution.py:224
  31.3 11.9 %collective-permute-start.3 = (bf16[304,512]{1,0:T(8,128)(2,1)S(1)}, bf16[304,512]{1,0:T(8,128)(2,1)S(1)}, u32[]{:S(2)}, u32[]{:S(2)}) collective-permute-start(bf16[304,512]{1,0:T(8,128)(2,1)S(1)} %copy-done.1), channel_id=1, source_target_pairs={{0,7},{1,0},{2,1},{3,2},{4,3},{5,4},{6,5},{7,6},{8,15},{9,8},{10,9... | collective-permute-start | bytes 933896 | tf_op jit(solution)/shard_map/ppermute | solution.py:224
  35.9 49.2 %copy-start.3 = (bf16[304,512]{1,0:T(8,128)(2,1)}, bf16[304,512]{1,0:T(8,128)(2,1)S(1)}, u32[]{:S(2)}) copy-start(bf16[304,512]{1,0:T(8,128)(2,1)S(1)} %collective-permute-done.refs_1_) | copy-start | bytes 933892
  35.9 11.9 %collective-permute-start.4 = (bf16[304,512]{1,0:T(8,128)(2,1)S(1)}, bf16[304,512]{1,0:T(8,128)(2,1)S(1)}, u32[]{:S(2)}, u32[]{:S(2)}) collective-permute-start(bf16[304,512]{1,0:T(8,128)(2,1)S(1)} %collective-permute-done.refs_1_), channel_id=1, source_target_pairs={{0,7},{1,0},{2,1},{3,2},{4,3},{5,4},{6,5},{7,6},{8,15},{9,8},{10,9... | collective-permute-start | bytes 933896 | tf_op jit(solution)/shard_map/ppermute | solution.py:224
  37.9 14.8 %collective-permute-start.2 = (bf16[304,512]{1,0:T(8,128)(2,1)S(1)}, bf16[304,512]{1,0:T(8,128)(2,1)S(1)}, u32[]{:S(2)}, u32[]{:S(2)}) collective-permute-start(bf16[304,512]{1,0:T(8,128)(2,1)S(1)} %collective-permute-done.refs_1_), channel_id=1, source_target_pairs={{0,1},{1,2},{2,3},{3,4},{4,5},{5,6},{6,7},{7,0},{8,9},{9,10},{10,1... | collective-permute-start | bytes 933896 | tf_op jit(solution)/shard_map/ppermute | solution.py:224
  41.3 34.0 %copy-start.4 = (bf16[304,512]{1,0:T(8,128)(2,1)}, bf16[304,512]{1,0:T(8,128)(2,1)S(1)}, u32[]{:S(2)}) copy-start(bf16[304,512]{1,0:T(8,128)(2,1)S(1)} %collective-permute-done.5.refs_6_) | copy-start | bytes 933892
  41.3 13.4 %collective-permute-start.9 = (bf16[304,512]{1,0:T(8,128)(2,1)S(1)}, bf16[304,512]{1,0:T(8,128)(2,1)S(1)}, u32[]{:S(2)}, u32[]{:S(2)}) collective-permute-start(bf16[304,512]{1,0:T(8,128)(2,1)S(1)} %collective-permute-done.5.refs_6_), channel_id=1, source_target_pairs={{0,1},{1,2},{2,3},{3,4},{4,5},{5,6},{6,7},{7,0},{8,9},{9,10},{10,1... | collective-permute-start | bytes 933896 | tf_op jit(solution)/shard_map/ppermute | solution.py:224
  43.2 32.0 %copy-start.5 = (bf16[304,512]{1,0:T(8,128)(2,1)}, bf16[304,512]{1,0:T(8,128)(2,1)S(1)}, u32[]{:S(2)}) copy-start(bf16[304,512]{1,0:T(8,128)(2,1)S(1)} %collective-permute-done.3.refs_4_) | copy-start | bytes 933892
  43.2 13.6 %collective-permute-start.7 = (bf16[304,512]{1,0:T(8,128)(2,1)S(1)}, bf16[304,512]{1,0:T(8,128)(2,1)S(1)}, u32[]{:S(2)}, u32[]{:S(2)}) collective-permute-start(bf16[304,512]{1,0:T(8,128)(2,1)S(1)} %collective-permute-done.3.refs_4_), channel_id=1, source_target_pairs={{0,7},{1,0},{2,1},{3,2},{4,3},{5,4},{6,5},{7,6},{8,15},{9,8},{10,9... | collective-permute-start | bytes 933896 | tf_op jit(solution)/shard_map/ppermute | solution.py:224
  47.8 27.4 %copy-start.6 = (bf16[304,512]{1,0:T(8,128)(2,1)}, bf16[304,512]{1,0:T(8,128)(2,1)S(1)}, u32[]{:S(2)}) copy-start(bf16[304,512]{1,0:T(8,128)(2,1)S(1)} %collective-permute-done.4.refs_5_) | copy-start | bytes 933892
  47.8 13.4 %collective-permute-start.8 = (bf16[304,512]{1,0:T(8,128)(2,1)S(1)}, bf16[304,512]{1,0:T(8,128)(2,1)S(1)}, u32[]{:S(2)}, u32[]{:S(2)}) collective-permute-start(bf16[304,512]{1,0:T(8,128)(2,1)S(1)} %collective-permute-done.4.refs_5_), channel_id=1, source_target_pairs={{0,7},{1,0},{2,1},{3,2},{4,3},{5,4},{6,5},{7,6},{8,15},{9,8},{10,9... | collective-permute-start | bytes 933896 | tf_op jit(solution)/shard_map/ppermute | solution.py:224
  52.7 22.5 %copy-start.7 = (bf16[304,512]{1,0:T(8,128)(2,1)}, bf16[304,512]{1,0:T(8,128)(2,1)S(1)}, u32[]{:S(2)}) copy-start(bf16[304,512]{1,0:T(8,128)(2,1)S(1)} %collective-permute-done.2.refs_3_) | copy-start | bytes 933892
  52.7 13.3 %collective-permute-start.6 = (bf16[304,512]{1,0:T(8,128)(2,1)S(1)}, bf16[304,512]{1,0:T(8,128)(2,1)S(1)}, u32[]{:S(2)}, u32[]{:S(2)}) collective-permute-start(bf16[304,512]{1,0:T(8,128)(2,1)S(1)} %collective-permute-done.2.refs_3_), channel_id=1, source_target_pairs={{0,1},{1,2},{2,3},{3,4},{4,5},{5,6},{6,7},{7,0},{8,9},{9,10},{10,1... | collective-permute-start | bytes 933896 | tf_op jit(solution)/shard_map/ppermute | solution.py:224
  54.7 20.6 %copy-start.8 = (bf16[304,512]{1,0:T(8,128)(2,1)}, bf16[304,512]{1,0:T(8,128)(2,1)S(1)}, u32[]{:S(2)}) copy-start(bf16[304,512]{1,0:T(8,128)(2,1)S(1)} %collective-permute-done.9.refs_10_) | copy-start | bytes 933892
  54.7 13.3 %collective-permute-start.11 = (bf16[304,512]{1,0:T(8,128)(2,1)S(1)}, bf16[304,512]{1,0:T(8,128)(2,1)S(1)}, u32[]{:S(2)}, u32[]{:S(2)}) collective-permute-start(bf16[304,512]{1,0:T(8,128)(2,1)S(1)} %collective-permute-done.9.refs_10_), channel_id=1, source_target_pairs={{0,1},{1,2},{2,3},{3,4},{4,5},{5,6},{6,7},{7,0},{8,9},{9,10},{10,1... | collective-permute-start | bytes 933896 | tf_op jit(solution)/shard_map/ppermute | solution.py:224
  56.8 28.3 %copy-start.9 = (bf16[304,512]{1,0:T(8,128)(2,1)}, bf16[304,512]{1,0:T(8,128)(2,1)S(1)}, u32[]{:S(2)}) copy-start(bf16[304,512]{1,0:T(8,128)(2,1)S(1)} %collective-permute-done.7.refs_8_) | copy-start | bytes 933892
  56.8 13.4 %collective-permute-start.10 = (bf16[304,512]{1,0:T(8,128)(2,1)S(1)}, bf16[304,512]{1,0:T(8,128)(2,1)S(1)}, u32[]{:S(2)}, u32[]{:S(2)}) collective-permute-start(bf16[304,512]{1,0:T(8,128)(2,1)S(1)} %collective-permute-done.7.refs_8_), channel_id=1, source_target_pairs={{0,7},{1,0},{2,1},{3,2},{4,3},{5,4},{6,5},{7,6},{8,15},{9,8},{10,9... | collective-permute-start | bytes 933896 | tf_op jit(solution)/shard_map/ppermute | solution.py:224
  61.2 14.0 %copy-start.10 = (bf16[304,512]{1,0:T(8,128)(2,1)}, bf16[304,512]{1,0:T(8,128)(2,1)S(1)}, u32[]{:S(2)}) copy-start(bf16[304,512]{1,0:T(8,128)(2,1)S(1)} %collective-permute-done.8.refs_9_) | copy-start | bytes 933892
  61.2 11.6 %collective-permute-start.13 = (bf16[304,512]{1,0:T(8,128)(2,1)S(1)}, bf16[304,512]{1,0:T(8,128)(2,1)S(1)}, u32[]{:S(2)}, u32[]{:S(2)}) collective-permute-start(bf16[304,512]{1,0:T(8,128)(2,1)S(1)} %collective-permute-done.8.refs_9_), channel_id=1, source_target_pairs={{0,7},{1,0},{2,1},{3,2},{4,3},{5,4},{6,5},{7,6},{8,15},{9,8},{10,9... | collective-permute-start | bytes 933896 | tf_op jit(solution)/shard_map/ppermute | solution.py:224
  66.0 9.3 %copy-start.11 = (bf16[304,512]{1,0:T(8,128)(2,1)}, bf16[304,512]{1,0:T(8,128)(2,1)S(1)}, u32[]{:S(2)}) copy-start(bf16[304,512]{1,0:T(8,128)(2,1)S(1)} %collective-permute-done.6.refs_7_) | copy-start | bytes 933892
  66.0 9.2 %collective-permute-start.12 = (bf16[304,512]{1,0:T(8,128)(2,1)S(1)}, bf16[304,512]{1,0:T(8,128)(2,1)S(1)}, u32[]{:S(2)}, u32[]{:S(2)}) collective-permute-start(bf16[304,512]{1,0:T(8,128)(2,1)S(1)} %collective-permute-done.6.refs_7_), channel_id=1, source_target_pairs={{0,1},{1,2},{2,3},{3,4},{4,5},{5,6},{6,7},{7,0},{8,9},{9,10},{10,1... | collective-permute-start | bytes 933896 | tf_op jit(solution)/shard_map/ppermute | solution.py:224
  68.0 7.3 %copy-start.12 = (bf16[304,512]{1,0:T(8,128)(2,1)}, bf16[304,512]{1,0:T(8,128)(2,1)S(1)}, u32[]{:S(2)}) copy-start(bf16[304,512]{1,0:T(8,128)(2,1)S(1)} %collective-permute-done.11.refs_14_) | copy-start | bytes 933892
  68.0 13.3 %collective-permute-start.14 = (bf16[304,512]{1,0:T(8,128)(2,1)S(1)}, bf16[304,512]{1,0:T(8,128)(2,1)}, u32[]{:S(2)}, u32[]{:S(2)}) collective-permute-start(bf16[304,512]{1,0:T(8,128)(2,1)S(1)} %collective-permute-done.11.refs_14_), channel_id=1, source_target_pairs={{0,8},{8,0},{1,9},{9,1},{2,10},{10,2},{3,11},{11,3},{4,12},{12,4},... | collective-permute-start | bytes 933896 | tf_op jit(solution)/shard_map/ppermute | solution.py:224
  70.2 5.1 %copy-start.13 = (bf16[304,512]{1,0:T(8,128)(2,1)}, bf16[304,512]{1,0:T(8,128)(2,1)S(1)}, u32[]{:S(2)}) copy-start(bf16[304,512]{1,0:T(8,128)(2,1)S(1)} %collective-permute-done.10.refs_12_) | copy-start | bytes 933892
  72.9 2.4 %copy-start.14 = (bf16[304,512]{1,0:T(8,128)(2,1)}, bf16[304,512]{1,0:T(8,128)(2,1)S(1)}, u32[]{:S(2)}) copy-start(bf16[304,512]{1,0:T(8,128)(2,1)S(1)} %collective-permute-done.13.refs_13_) | copy-start | bytes 933892
  75.3 0.7 copy-start.15
  81.3 3.8 %copy-start = (bf16[16,152,512]{2,1,0:T(8,128)(2,1)}, bf16[16,152,512]{2,1,0:T(8,128)(2,1)S(1)}, u32[]{:S(2)}) copy-start(bf16[16,152,512]{2,1,0:T(8,128)(2,1)S(1)} %all-to-all-done.refs_15_.refs_16_) | copy-start | bytes 7471108
  81.3 8.5 %collective-permute-start.15 = (bf16[16,152,512]{2,1,0:T(8,128)(2,1)S(1)}, bf16[16,152,512]{2,1,0:T(8,128)(2,1)}, u32[]{:S(2)}, u32[]{:S(2)}) collective-permute-start(bf16[16,152,512]{2,1,0:T(8,128)(2,1)S(1)} %all-to-all-done.refs_15_.refs_16_), channel_id=1, source_target_pairs={{0,16},{16,0},{1,17},{17,1},{2,18},{18,2},{3,19},{19,3},{4,20},{20... | collective-permute-start | bytes 7471112 | tf_op jit(solution)/shard_map/ppermute | solution.py:224

commit v7 on v6

--- a/solution.py
+++ b/solution.py
@@ -67,7 +67,7 @@
     )(down_blocks, dec_t, deltas, encoder, gradients)
 
 
-def accumulate(items, tokens, dec, enc, dec_sem, enc_sem):
+def accumulate(items, tokens, dec, enc, dec_sem, enc_sem, meanwhile=None):
     chunks = [range(low, min(low + STEP, len(items))) for low in range(0, len(items), STEP)]
     if len(chunks[-1]) == 1:
         chunks[-2:] = [range(chunks[-2].start, len(items))]
@@ -82,6 +82,8 @@
             pltpu.make_async_copy(shard.at[rows], here.at[:KE], dec_sem.at[n]).start()
             if tokens:
                 pltpu.make_async_copy(shard.at[KD:], here.at[KE:], dec_sem.at[n]).start()
+    if meanwhile is not None:
+        meanwhile()
     virtual = None
     for n, chunk in enumerate(chunks):
         at = slice(chunk.start, chunk.stop)
@@ -140,9 +142,12 @@
     core, ks = lax.axis_index("c"), places()
     items = [(shard, k, 1 - core, swapped) for shard, k in zip(shards, ks)]
     items.append((shards[-1], ks[-1], core, own))
-    more = accumulate(items, True, dec, enc, dec_sem, enc_sem)
-    for b in range(VF_DEV // BLOCK):
-        pl.when(idle[b])(blank(b).start)
+
+    def blanks():
+        for b in range(VF_DEV // BLOCK):
+            pl.when(idle[b])(blank(b).start)
+
+    more = accumulate(items, True, dec, enc, dec_sem, enc_sem, blanks)
     for copy in loads:
         copy.wait()
     lane_block = lax.broadcasted_iota(jnp.int32, (TD, UF_DEV), 1) // BLOCK

time: 96.9 us -> 97.2 us (level)
  no operation moved by 1% of the time
where the time goes in v7:
time: 97.2 us; the launch traced here: 96.5 us
  starting transfers between devices  63.3 us (65%)
  waiting for transfers between devices  16.7 us (17%)
  Pallas kernels  15.3 us (16%)
    ppermute x16, starting transfers between devices, turn(): return lax.ppermute(value, axis, [(i, (i + by) % n) for i in range(n)])  49.7 us
    ppermute x16, waiting for transfers between devices, turn(): return lax.ppermute(value, axis, [(i, (i + by) % n) for i in range(n)])  16.7 us
    all_to_all x1, starting transfers between devices, local(): own = lax.all_to_all(e, ('z', 'xh'), 0, 0, tiled=True)  13.6 us
    pallas_call x1, Pallas kernels, score(): pl.pallas_call(score_kernel, out_shape=jax.ShapeDtypeStruct((UF_DEV, VF_D...  6.74 us
    pallas_call x1, Pallas kernels, half(): pl.pallas_call(half_kernel, out_shape=jax.ShapeDtypeStruct((UF_DEV, COLS)...  4.65 us
    pallas_call x1, Pallas kernels, pack(): pl.pallas_call(pack_kernel, out_shape=(jax.ShapeDtypeStruct((RD, UF_DEV),...  3.96 us
  transfers between devices with their start and end apart: 17, of which 4 were waited for; matrix products, arithmetic and copies ran while one was open for 0% of the time, Pallas kernels for 5%

profile of v7, /device:TPU:1, one launch (start us, length us, event | category | flops | bytes accessed | tf_op | source)
XLA Modules:
  0.0 96.5 jit_solution(5536044300767974162)
XLA Ops:
  0.0 4.0 %shard_map.64 = (bf16[304,512]{1,0:T(8,128)(2,1)}, bf16[16,152,512]{2,1,0:T(8,128)(2,1)}) custom-call(s32[4]{0:T(128)} %down_ref.3, bf16[288,512]{1,0:T(8,128)(2,1)} %bitcast.2, bf16[16,512]{1,0:T(8,128)(2,1)} %delta_ref.1, bf16[144,1024]{1,0:T(8,128)(2,1)} %enc_ref.1, bf16[8,1024]{1,0:T(8,128)(2,1)} %grad_ref.1), custom_call_target="tpu_custom_call" | custom-call | tf_op jit(solution)/shard_map/pallas_call | solution.py:54
  4.0 0.0 copy-start.1
  4.0 13.6 %all-to-all-start = ((bf16[16,152,512]{2,1,0:T(8,128)(2,1)}), bf16[16,152,512]{2,1,0:T(8,128)(2,1)S(1)}, u32[]{:S(2)}, u32[]{:S(2)}) async-start(bf16[16,152,512]{2,1,0:T(8,128)(2,1)} %get-tuple-element.15), calls=%async_computation | async-start | bytes 4980736 | tf_op jit(solution)/shard_map/all_to_all | solution.py:238
  17.6 0.0 copy-done.1
  17.6 3.2 %collective-permute-start.1 = (bf16[304,512]{1,0:T(8,128)(2,1)S(1)}, bf16[304,512]{1,0:T(8,128)(2,1)S(1)}, u32[]{:S(2)}, u32[]{:S(2)}) collective-permute-start(bf16[304,512]{1,0:T(8,128)(2,1)S(1)} %copy-done.1), channel_id=1, source_target_pairs={{0,1},{1,2},{2,3},{3,4},{4,5},{5,6},{6,7},{7,0},{8,9},{9,10},{10,1... | collective-permute-start | bytes 933896 | tf_op jit(solution)/shard_map/ppermute | solution.py:229
  20.8 2.2 %collective-permute-start = (bf16[304,512]{1,0:T(8,128)(2,1)S(1)}, bf16[304,512]{1,0:T(8,128)(2,1)S(1)}, u32[]{:S(2)}, u32[]{:S(2)}) collective-permute-start(bf16[304,512]{1,0:T(8,128)(2,1)S(1)} %copy-done.1), channel_id=1, source_target_pairs={{0,8},{8,0},{1,9},{9,1},{2,10},{10,2},{3,11},{11,3},{4,12},{12,4},... | collective-permute-start | bytes 933896 | tf_op jit(solution)/shard_map/ppermute | solution.py:229
  23.0 6.4 %collective-permute-done.1.refs_2_ = bf16[304,512]{1,0:T(8,128)(2,1)S(1)} collective-permute-done((bf16[304,512]{1,0:T(8,128)(2,1)S(1)}, bf16[304,512]{1,0:T(8,128)(2,1)S(1)}, u32[]{:S(2)}, u32[]{:S(2)}) %collective-permute-start.1) | collective-permute-done | bytes 311328 | tf_op jit(solution)/shard_map/ppermute | solution.py:229
  29.4 1.9 %collective-permute-start.5 = (bf16[304,512]{1,0:T(8,128)(2,1)S(1)}, bf16[304,512]{1,0:T(8,128)(2,1)S(1)}, u32[]{:S(2)}, u32[]{:S(2)}) collective-permute-start(bf16[304,512]{1,0:T(8,128)(2,1)S(1)} %collective-permute-done.1.refs_2_), channel_id=1, source_target_pairs={{0,1},{1,2},{2,3},{3,4},{4,5},{5,6},{6,7},{7,0},{8,9},{9,10},{10,1... | collective-permute-start | bytes 933896 | tf_op jit(solution)/shard_map/ppermute | solution.py:229
  31.3 4.6 %collective-permute-start.3 = (bf16[304,512]{1,0:T(8,128)(2,1)S(1)}, bf16[304,512]{1,0:T(8,128)(2,1)S(1)}, u32[]{:S(2)}, u32[]{:S(2)}) collective-permute-start(bf16[304,512]{1,0:T(8,128)(2,1)S(1)} %copy-done.1), channel_id=1, source_target_pairs={{0,7},{1,0},{2,1},{3,2},{4,3},{5,4},{6,5},{7,6},{8,15},{9,8},{10,9... | collective-permute-start | bytes 933896 | tf_op jit(solution)/shard_map/ppermute | solution.py:229
  35.9 0.0 collective-permute-done.refs_1_
  35.9 0.0 copy-start.3
  35.9 1.9 %collective-permute-start.4 = (bf16[304,512]{1,0:T(8,128)(2,1)S(1)}, bf16[304,512]{1,0:T(8,128)(2,1)S(1)}, u32[]{:S(2)}, u32[]{:S(2)}) collective-permute-start(bf16[304,512]{1,0:T(8,128)(2,1)S(1)} %collective-permute-done.refs_1_), channel_id=1, source_target_pairs={{0,7},{1,0},{2,1},{3,2},{4,3},{5,4},{6,5},{7,6},{8,15},{9,8},{10,9... | collective-permute-start | bytes 933896 | tf_op jit(solution)/shard_map/ppermute | solution.py:229
  37.9 3.4 %collective-permute-start.2 = (bf16[304,512]{1,0:T(8,128)(2,1)S(1)}, bf16[304,512]{1,0:T(8,128)(2,1)S(1)}, u32[]{:S(2)}, u32[]{:S(2)}) collective-permute-start(bf16[304,512]{1,0:T(8,128)(2,1)S(1)} %collective-permute-done.refs_1_), channel_id=1, source_target_pairs={{0,1},{1,2},{2,3},{3,4},{4,5},{5,6},{6,7},{7,0},{8,9},{9,10},{10,1... | collective-permute-start | bytes 933896 | tf_op jit(solution)/shard_map/ppermute | solution.py:229
  41.2 0.0 collective-permute-done.5.refs_6_
  41.3 0.0 copy-start.4
  41.3 1.9 %collective-permute-start.9 = (bf16[304,512]{1,0:T(8,128)(2,1)S(1)}, bf16[304,512]{1,0:T(8,128)(2,1)S(1)}, u32[]{:S(2)}, u32[]{:S(2)}) collective-permute-start(bf16[304,512]{1,0:T(8,128)(2,1)S(1)} %collective-permute-done.5.refs_6_), channel_id=1, source_target_pairs={{0,1},{1,2},{2,3},{3,4},{4,5},{5,6},{6,7},{7,0},{8,9},{9,10},{10,1... | collective-permute-start | bytes 933896 | tf_op jit(solution)/shard_map/ppermute | solution.py:229
  43.2 0.0 collective-permute-done.3.refs_4_
  43.2 0.0 copy-start.5
  43.2 4.6 %collective-permute-start.7 = (bf16[304,512]{1,0:T(8,128)(2,1)S(1)}, bf16[304,512]{1,0:T(8,128)(2,1)S(1)}, u32[]{:S(2)}, u32[]{:S(2)}) collective-permute-start(bf16[304,512]{1,0:T(8,128)(2,1)S(1)} %collective-permute-done.3.refs_4_), channel_id=1, source_target_pairs={{0,7},{1,0},{2,1},{3,2},{4,3},{5,4},{6,5},{7,6},{8,15},{9,8},{10,9... | collective-permute-start | bytes 933896 | tf_op jit(solution)/shard_map/ppermute | solution.py:229
  47.8 0.0 collective-permute-done.4.refs_5_
  47.8 0.0 copy-start.6
  47.8 4.9 %collective-permute-start.8 = (bf16[304,512]{1,0:T(8,128)(2,1)S(1)}, bf16[304,512]{1,0:T(8,128)(2,1)S(1)}, u32[]{:S(2)}, u32[]{:S(2)}) collective-permute-start(bf16[304,512]{1,0:T(8,128)(2,1)S(1)} %collective-permute-done.4.refs_5_), channel_id=1, source_target_pairs={{0,7},{1,0},{2,1},{3,2},{4,3},{5,4},{6,5},{7,6},{8,15},{9,8},{10,9... | collective-permute-start | bytes 933896 | tf_op jit(solution)/shard_map/ppermute | solution.py:229
  52.7 0.0 collective-permute-done.2.refs_3_
  52.7 0.0 copy-start.7
  52.7 1.9 %collective-permute-start.6 = (bf16[304,512]{1,0:T(8,128)(2,1)S(1)}, bf16[304,512]{1,0:T(8,128)(2,1)S(1)}, u32[]{:S(2)}, u32[]{:S(2)}) collective-permute-start(bf16[304,512]{1,0:T(8,128)(2,1)S(1)} %collective-permute-done.2.refs_3_), channel_id=1, source_target_pairs={{0,1},{1,2},{2,3},{3,4},{4,5},{5,6},{6,7},{7,0},{8,9},{9,10},{10,1... | collective-permute-start | bytes 933896 | tf_op jit(solution)/shard_map/ppermute | solution.py:229
  54.7 0.0 collective-permute-done.9.refs_10_
  54.7 0.0 copy-start.8
  54.7 2.1 %collective-permute-start.11 = (bf16[304,512]{1,0:T(8,128)(2,1)S(1)}, bf16[304,512]{1,0:T(8,128)(2,1)S(1)}, u32[]{:S(2)}, u32[]{:S(2)}) collective-permute-start(bf16[304,512]{1,0:T(8,128)(2,1)S(1)} %collective-permute-done.9.refs_10_), channel_id=1, source_target_pairs={{0,1},{1,2},{2,3},{3,4},{4,5},{5,6},{6,7},{7,0},{8,9},{9,10},{10,1... | collective-permute-start | bytes 933896 | tf_op jit(solution)/shard_map/ppermute | solution.py:229
  56.8 0.0 collective-permute-done.7.refs_8_
  56.8 0.0 copy-start.9
  56.8 4.4 %collective-permute-start.10 = (bf16[304,512]{1,0:T(8,128)(2,1)S(1)}, bf16[304,512]{1,0:T(8,128)(2,1)S(1)}, u32[]{:S(2)}, u32[]{:S(2)}) collective-permute-start(bf16[304,512]{1,0:T(8,128)(2,1)S(1)} %collective-permute-done.7.refs_8_), channel_id=1, source_target_pairs={{0,7},{1,0},{2,1},{3,2},{4,3},{5,4},{6,5},{7,6},{8,15},{9,8},{10,9... | collective-permute-start | bytes 933896 | tf_op jit(solution)/shard_map/ppermute | solution.py:229
  61.2 0.0 collective-permute-done.8.refs_9_
  61.2 0.0 copy-start.10
  61.2 4.8 %collective-permute-start.13 = (bf16[304,512]{1,0:T(8,128)(2,1)S(1)}, bf16[304,512]{1,0:T(8,128)(2,1)S(1)}, u32[]{:S(2)}, u32[]{:S(2)}) collective-permute-start(bf16[304,512]{1,0:T(8,128)(2,1)S(1)} %collective-permute-done.8.refs_9_), channel_id=1, source_target_pairs={{0,7},{1,0},{2,1},{3,2},{4,3},{5,4},{6,5},{7,6},{8,15},{9,8},{10,9... | collective-permute-start | bytes 933896 | tf_op jit(solution)/shard_map/ppermute | solution.py:229
  66.0 0.0 collective-permute-done.6.refs_7_
  66.0 0.0 copy-start.11
  66.0 1.9 %collective-permute-start.12 = (bf16[304,512]{1,0:T(8,128)(2,1)S(1)}, bf16[304,512]{1,0:T(8,128)(2,1)S(1)}, u32[]{:S(2)}, u32[]{:S(2)}) collective-permute-start(bf16[304,512]{1,0:T(8,128)(2,1)S(1)} %collective-permute-done.6.refs_7_), channel_id=1, source_target_pairs={{0,1},{1,2},{2,3},{3,4},{4,5},{5,6},{6,7},{7,0},{8,9},{9,10},{10,1... | collective-permute-start | bytes 933896 | tf_op jit(solution)/shard_map/ppermute | solution.py:229
  68.0 0.0 collective-permute-done.11.refs_14_
  68.0 0.0 copy-start.12
  68.0 2.2 %collective-permute-start.14 = (bf16[304,512]{1,0:T(8,128)(2,1)S(1)}, bf16[304,512]{1,0:T(8,128)(2,1)}, u32[]{:S(2)}, u32[]{:S(2)}) collective-permute-start(bf16[304,512]{1,0:T(8,128)(2,1)S(1)} %collective-permute-done.11.refs_14_), channel_id=1, source_target_pairs={{0,8},{8,0},{1,9},{9,1},{2,10},{10,2},{3,11},{11,3},{4,12},{12,4},... | collective-permute-start | bytes 933896 | tf_op jit(solution)/shard_map/ppermute | solution.py:229
  70.2 0.0 collective-permute-done.10.refs_12_
  70.2 0.0 copy-start.13
  70.2 2.6 %collective-permute-done.13.refs_13_ = bf16[304,512]{1,0:T(8,128)(2,1)S(1)} collective-permute-done((bf16[304,512]{1,0:T(8,128)(2,1)S(1)}, bf16[304,512]{1,0:T(8,128)(2,1)S(1)}, u32[]{:S(2)}, u32[]{:S(2)}) %collective-permute-start.13) | collective-permute-done | bytes 311328 | tf_op jit(solution)/shard_map/ppermute | solution.py:229
  72.9 2.4 %collective-permute-done.12.refs_11_ = bf16[304,512]{1,0:T(8,128)(2,1)S(1)} collective-permute-done((bf16[304,512]{1,0:T(8,128)(2,1)S(1)}, bf16[304,512]{1,0:T(8,128)(2,1)S(1)}, u32[]{:S(2)}, u32[]{:S(2)}) %collective-permute-start.12) | collective-permute-done | bytes 311328 | tf_op jit(solution)/shard_map/ppermute | solution.py:229
  75.2 0.0 copy-done.4
  75.2 0.0 copy-done.5
  75.2 0.0 copy-done.6
  75.2 0.0 copy-done.7
  75.2 0.0 copy-done.8
  75.3 0.0 copy-done.10
  75.3 0.0 copy-done.11
  75.3 0.0 copy-done.12
  75.3 0.0 copy-done.13
  75.3 0.7 copy-done.15
  76.0 5.2 %collective-permute-done.14.refs_15_ = bf16[304,512]{1,0:T(8,128)(2,1)} collective-permute-done((bf16[304,512]{1,0:T(8,128)(2,1)S(1)}, bf16[304,512]{1,0:T(8,128)(2,1)}, u32[]{:S(2)}, u32[]{:S(2)}) %collective-permute-start.14) | collective-permute-done | bytes 311328 | tf_op jit(solution)/shard_map/ppermute | solution.py:229
  81.3 0.0 all-to-all-done.refs_15_.refs_16_
  81.3 3.8 %collective-permute-start.15 = (bf16[16,152,512]{2,1,0:T(8,128)(2,1)S(1)}, bf16[16,152,512]{2,1,0:T(8,128)(2,1)}, u32[]{:S(2)}, u32[]{:S(2)}) collective-permute-start(bf16[16,152,512]{2,1,0:T(8,128)(2,1)S(1)} %all-to-all-done.refs_15_.refs_16_), channel_id=1, source_target_pairs={{0,16},{16,0},{1,17},{17,1},{2,18},{18,2},{3,19},{19,3},{4,20},{20... | collective-permute-start | bytes 7471112 | tf_op jit(solution)/shard_map/ppermute | solution.py:229
  85.1 0.0 copy-done.2
  85.1 0.0 copy-done.3
  85.1 0.0 copy-done.9
  85.1 0.0 copy-done
  85.1 4.6 %shard_map.65.refs_18_ = f32[512,512]{1,0:T(8,128)} custom-call(bf16[304,512]{1,0:T(8,128)(2,1)} %get-tuple-element.14.refs_0_, bf16[304,512]{1,0:T(8,128)(2,1)} %copy-done.3, bf16[304,512]{1,0:T(8,128)(2,1)} %copy-done.2, bf16[304,512]{1,0:T(8,128)(2,1)} %copy-done.7, bf16[304,512]{1,0:T(8,128)(2,1)} %copy-done.5, bf16[304,512]{1,0:T(8,128)(2,1)} %copy-done.6, ...), custom_call_target="tpu_custom_call" | custom-call | flops 1207959552 | bytes 8388608 | tf_op jit(solution)/shard_map/pallas_call | solution.py:195
  89.8 0.0 collective-permute-done.15.refs_17_
  89.8 6.7 %shard_map.66 = f32[512,1024]{1,0:T(8,128)} custom-call(s32[2,8]{1,0:T(2,128)} %bitcast.3, s32[4]{0:T(128)} %down_ref.3, bf16[304,512]{1,0:T(8,128)(2,1)} %get-tuple-element.14.refs_0_, bf16[304,512]{1,0:T(8,128)(2,1)} %copy-done.3, bf16[304,512]{1,0:T(8,128)(2,1)} %copy-done.2, bf16[304,512]{1,0:T(8,128)(2,1)} %copy-done.7, bf16[304,512]{1,0:T(8,128)(2,1)} %copy-done.5, ...), custom_call_target="tpu_custom_call" | custom-call | flops 1207959552 | bytes 8388608 | tf_op jit(solution)/shard_map/pallas_call | solution.py:207
  (5 shorter events, 0.0 us)
Async XLA Ops:
  4.0 13.6 %copy-start.1 = (bf16[304,512]{1,0:T(8,128)(2,1)S(1)}, bf16[304,512]{1,0:T(8,128)(2,1)}, u32[]{:S(2)}) copy-start(bf16[304,512]{1,0:T(8,128)(2,1)} %get-tuple-element.14.refs_0_) | copy-start | bytes 933892
  4.0 77.3 %all-to-all-start = ((bf16[16,152,512]{2,1,0:T(8,128)(2,1)}), bf16[16,152,512]{2,1,0:T(8,128)(2,1)S(1)}, u32[]{:S(2)}, u32[]{:S(2)}) async-start(bf16[16,152,512]{2,1,0:T(8,128)(2,1)} %get-tuple-element.15), calls=%async_computation | async-start | bytes 4980736 | tf_op jit(solution)/shard_map/all_to_all | solution.py:238
  17.6 11.9 %collective-permute-start.1 = (bf16[304,512]{1,0:T(8,128)(2,1)S(1)}, bf16[304,512]{1,0:T(8,128)(2,1)S(1)}, u32[]{:S(2)}, u32[]{:S(2)}) collective-permute-start(bf16[304,512]{1,0:T(8,128)(2,1)S(1)} %copy-done.1), channel_id=1, source_target_pairs={{0,1},{1,2},{2,3},{3,4},{4,5},{5,6},{6,7},{7,0},{8,9},{9,10},{10,1... | collective-permute-start | bytes 933896 | tf_op jit(solution)/shard_map/ppermute | solution.py:229
  20.8 15.1 %collective-permute-start = (bf16[304,512]{1,0:T(8,128)(2,1)S(1)}, bf16[304,512]{1,0:T(8,128)(2,1)S(1)}, u32[]{:S(2)}, u32[]{:S(2)}) collective-permute-start(bf16[304,512]{1,0:T(8,128)(2,1)S(1)} %copy-done.1), channel_id=1, source_target_pairs={{0,8},{8,0},{1,9},{9,1},{2,10},{10,2},{3,11},{11,3},{4,12},{12,4},... | collective-permute-start | bytes 933896 | tf_op jit(solution)/shard_map/ppermute | solution.py:229
  29.4 55.7 %copy-start.2 = (bf16[304,512]{1,0:T(8,128)(2,1)}, bf16[304,512]{1,0:T(8,128)(2,1)S(1)}, u32[]{:S(2)}) copy-start(bf16[304,512]{1,0:T(8,128)(2,1)S(1)} %collective-permute-done.1.refs_2_) | copy-start | bytes 933892
  29.4 11.8 %collective-permute-start.5 = (bf16[304,512]{1,0:T(8,128)(2,1)S(1)}, bf16[304,512]{1,0:T(8,128)(2,1)S(1)}, u32[]{:S(2)}, u32[]{:S(2)}) collective-permute-start(bf16[304,512]{1,0:T(8,128)(2,1)S(1)} %collective-permute-done.1.refs_2_), channel_id=1, source_target_pairs={{0,1},{1,2},{2,3},{3,4},{4,5},{5,6},{6,7},{7,0},{8,9},{9,10},{10,1... | collective-permute-start | bytes 933896 | tf_op jit(solution)/shard_map/ppermute | solution.py:229
  31.3 11.9 %collective-permute-start.3 = (bf16[304,512]{1,0:T(8,128)(2,1)S(1)}, bf16[304,512]{1,0:T(8,128)(2,1)S(1)}, u32[]{:S(2)}, u32[]{:S(2)}) collective-permute-start(bf16[304,512]{1,0:T(8,128)(2,1)S(1)} %copy-done.1), channel_id=1, source_target_pairs={{0,7},{1,0},{2,1},{3,2},{4,3},{5,4},{6,5},{7,6},{8,15},{9,8},{10,9... | collective-permute-start | bytes 933896 | tf_op jit(solution)/shard_map/ppermute | solution.py:229
  35.9 49.2 %copy-start.3 = (bf16[304,512]{1,0:T(8,128)(2,1)}, bf16[304,512]{1,0:T(8,128)(2,1)S(1)}, u32[]{:S(2)}) copy-start(bf16[304,512]{1,0:T(8,128)(2,1)S(1)} %collective-permute-done.refs_1_) | copy-start | bytes 933892
  35.9 11.9 %collective-permute-start.4 = (bf16[304,512]{1,0:T(8,128)(2,1)S(1)}, bf16[304,512]{1,0:T(8,128)(2,1)S(1)}, u32[]{:S(2)}, u32[]{:S(2)}) collective-permute-start(bf16[304,512]{1,0:T(8,128)(2,1)S(1)} %collective-permute-done.refs_1_), channel_id=1, source_target_pairs={{0,7},{1,0},{2,1},{3,2},{4,3},{5,4},{6,5},{7,6},{8,15},{9,8},{10,9... | collective-permute-start | bytes 933896 | tf_op jit(solution)/shard_map/ppermute | solution.py:229
  37.9 14.8 %collective-permute-start.2 = (bf16[304,512]{1,0:T(8,128)(2,1)S(1)}, bf16[304,512]{1,0:T(8,128)(2,1)S(1)}, u32[]{:S(2)}, u32[]{:S(2)}) collective-permute-start(bf16[304,512]{1,0:T(8,128)(2,1)S(1)} %collective-permute-done.refs_1_), channel_id=1, source_target_pairs={{0,1},{1,2},{2,3},{3,4},{4,5},{5,6},{6,7},{7,0},{8,9},{9,10},{10,1... | collective-permute-start | bytes 933896 | tf_op jit(solution)/shard_map/ppermute | solution.py:229
  41.3 34.0 %copy-start.4 = (bf16[304,512]{1,0:T(8,128)(2,1)}, bf16[304,512]{1,0:T(8,128)(2,1)S(1)}, u32[]{:S(2)}) copy-start(bf16[304,512]{1,0:T(8,128)(2,1)S(1)} %collective-permute-done.5.refs_6_) | copy-start | bytes 933892
  41.3 13.4 %collective-permute-start.9 = (bf16[304,512]{1,0:T(8,128)(2,1)S(1)}, bf16[304,512]{1,0:T(8,128)(2,1)S(1)}, u32[]{:S(2)}, u32[]{:S(2)}) collective-permute-start(bf16[304,512]{1,0:T(8,128)(2,1)S(1)} %collective-permute-done.5.refs_6_), channel_id=1, source_target_pairs={{0,1},{1,2},{2,3},{3,4},{4,5},{5,6},{6,7},{7,0},{8,9},{9,10},{10,1... | collective-permute-start | bytes 933896 | tf_op jit(solution)/shard_map/ppermute | solution.py:229
  43.2 32.0 %copy-start.5 = (bf16[304,512]{1,0:T(8,128)(2,1)}, bf16[304,512]{1,0:T(8,128)(2,1)S(1)}, u32[]{:S(2)}) copy-start(bf16[304,512]{1,0:T(8,128)(2,1)S(1)} %collective-permute-done.3.refs_4_) | copy-start | bytes 933892
  43.2 13.6 %collective-permute-start.7 = (bf16[304,512]{1,0:T(8,128)(2,1)S(1)}, bf16[304,512]{1,0:T(8,128)(2,1)S(1)}, u32[]{:S(2)}, u32[]{:S(2)}) collective-permute-start(bf16[304,512]{1,0:T(8,128)(2,1)S(1)} %collective-permute-done.3.refs_4_), channel_id=1, source_target_pairs={{0,7},{1,0},{2,1},{3,2},{4,3},{5,4},{6,5},{7,6},{8,15},{9,8},{10,9... | collective-permute-start | bytes 933896 | tf_op jit(solution)/shard_map/ppermute | solution.py:229
  47.8 27.4 %copy-start.6 = (bf16[304,512]{1,0:T(8,128)(2,1)}, bf16[304,512]{1,0:T(8,128)(2,1)S(1)}, u32[]{:S(2)}) copy-start(bf16[304,512]{1,0:T(8,128)(2,1)S(1)} %collective-permute-done.4.refs_5_) | copy-start | bytes 933892
  47.8 13.4 %collective-permute-start.8 = (bf16[304,512]{1,0:T(8,128)(2,1)S(1)}, bf16[304,512]{1,0:T(8,128)(2,1)S(1)}, u32[]{:S(2)}, u32[]{:S(2)}) collective-permute-start(bf16[304,512]{1,0:T(8,128)(2,1)S(1)} %collective-permute-done.4.refs_5_), channel_id=1, source_target_pairs={{0,7},{1,0},{2,1},{3,2},{4,3},{5,4},{6,5},{7,6},{8,15},{9,8},{10,9... | collective-permute-start | bytes 933896 | tf_op jit(solution)/shard_map/ppermute | solution.py:229
  52.7 22.5 %copy-start.7 = (bf16[304,512]{1,0:T(8,128)(2,1)}, bf16[304,512]{1,0:T(8,128)(2,1)S(1)}, u32[]{:S(2)}) copy-start(bf16[304,512]{1,0:T(8,128)(2,1)S(1)} %collective-permute-done.2.refs_3_) | copy-start | bytes 933892
  52.7 13.3 %collective-permute-start.6 = (bf16[304,512]{1,0:T(8,128)(2,1)S(1)}, bf16[304,512]{1,0:T(8,128)(2,1)S(1)}, u32[]{:S(2)}, u32[]{:S(2)}) collective-permute-start(bf16[304,512]{1,0:T(8,128)(2,1)S(1)} %collective-permute-done.2.refs_3_), channel_id=1, source_target_pairs={{0,1},{1,2},{2,3},{3,4},{4,5},{5,6},{6,7},{7,0},{8,9},{9,10},{10,1... | collective-permute-start | bytes 933896 | tf_op jit(solution)/shard_map/ppermute | solution.py:229
  54.7 20.6 %copy-start.8 = (bf16[304,512]{1,0:T(8,128)(2,1)}, bf16[304,512]{1,0:T(8,128)(2,1)S(1)}, u32[]{:S(2)}) copy-start(bf16[304,512]{1,0:T(8,128)(2,1)S(1)} %collective-permute-done.9.refs_10_) | copy-start | bytes 933892
  54.7 13.3 %collective-permute-start.11 = (bf16[304,512]{1,0:T(8,128)(2,1)S(1)}, bf16[304,512]{1,0:T(8,128)(2,1)S(1)}, u32[]{:S(2)}, u32[]{:S(2)}) collective-permute-start(bf16[304,512]{1,0:T(8,128)(2,1)S(1)} %collective-permute-done.9.refs_10_), channel_id=1, source_target_pairs={{0,1},{1,2},{2,3},{3,4},{4,5},{5,6},{6,7},{7,0},{8,9},{9,10},{10,1... | collective-permute-start | bytes 933896 | tf_op jit(solution)/shard_map/ppermute | solution.py:229
  56.8 28.3 %copy-start.9 = (bf16[304,512]{1,0:T(8,128)(2,1)}, bf16[304,512]{1,0:T(8,128)(2,1)S(1)}, u32[]{:S(2)}) copy-start(bf16[304,512]{1,0:T(8,128)(2,1)S(1)} %collective-permute-done.7.refs_8_) | copy-start | bytes 933892
  56.8 13.4 %collective-permute-start.10 = (bf16[304,512]{1,0:T(8,128)(2,1)S(1)}, bf16[304,512]{1,0:T(8,128)(2,1)S(1)}, u32[]{:S(2)}, u32[]{:S(2)}) collective-permute-start(bf16[304,512]{1,0:T(8,128)(2,1)S(1)} %collective-permute-done.7.refs_8_), channel_id=1, source_target_pairs={{0,7},{1,0},{2,1},{3,2},{4,3},{5,4},{6,5},{7,6},{8,15},{9,8},{10,9... | collective-permute-start | bytes 933896 | tf_op jit(solution)/shard_map/ppermute | solution.py:229
  61.2 14.0 %copy-start.10 = (bf16[304,512]{1,0:T(8,128)(2,1)}, bf16[304,512]{1,0:T(8,128)(2,1)S(1)}, u32[]{:S(2)}) copy-start(bf16[304,512]{1,0:T(8,128)(2,1)S(1)} %collective-permute-done.8.refs_9_) | copy-start | bytes 933892
  61.2 11.6 %collective-permute-start.13 = (bf16[304,512]{1,0:T(8,128)(2,1)S(1)}, bf16[304,512]{1,0:T(8,128)(2,1)S(1)}, u32[]{:S(2)}, u32[]{:S(2)}) collective-permute-start(bf16[304,512]{1,0:T(8,128)(2,1)S(1)} %collective-permute-done.8.refs_9_), channel_id=1, source_target_pairs={{0,7},{1,0},{2,1},{3,2},{4,3},{5,4},{6,5},{7,6},{8,15},{9,8},{10,9... | collective-permute-start | bytes 933896 | tf_op jit(solution)/shard_map/ppermute | solution.py:229
  66.0 9.3 %copy-start.11 = (bf16[304,512]{1,0:T(8,128)(2,1)}, bf16[304,512]{1,0:T(8,128)(2,1)S(1)}, u32[]{:S(2)}) copy-start(bf16[304,512]{1,0:T(8,128)(2,1)S(1)} %collective-permute-done.6.refs_7_) | copy-start | bytes 933892
  66.0 9.2 %collective-permute-start.12 = (bf16[304,512]{1,0:T(8,128)(2,1)S(1)}, bf16[304,512]{1,0:T(8,128)(2,1)S(1)}, u32[]{:S(2)}, u32[]{:S(2)}) collective-permute-start(bf16[304,512]{1,0:T(8,128)(2,1)S(1)} %collective-permute-done.6.refs_7_), channel_id=1, source_target_pairs={{0,1},{1,2},{2,3},{3,4},{4,5},{5,6},{6,7},{7,0},{8,9},{9,10},{10,1... | collective-permute-start | bytes 933896 | tf_op jit(solution)/shard_map/ppermute | solution.py:229
  68.0 7.3 %copy-start.12 = (bf16[304,512]{1,0:T(8,128)(2,1)}, bf16[304,512]{1,0:T(8,128)(2,1)S(1)}, u32[]{:S(2)}) copy-start(bf16[304,512]{1,0:T(8,128)(2,1)S(1)} %collective-permute-done.11.refs_14_) | copy-start | bytes 933892
  68.0 13.3 %collective-permute-start.14 = (bf16[304,512]{1,0:T(8,128)(2,1)S(1)}, bf16[304,512]{1,0:T(8,128)(2,1)}, u32[]{:S(2)}, u32[]{:S(2)}) collective-permute-start(bf16[304,512]{1,0:T(8,128)(2,1)S(1)} %collective-permute-done.11.refs_14_), channel_id=1, source_target_pairs={{0,8},{8,0},{1,9},{9,1},{2,10},{10,2},{3,11},{11,3},{4,12},{12,4},... | collective-permute-start | bytes 933896 | tf_op jit(solution)/shard_map/ppermute | solution.py:229
  70.2 5.1 %copy-start.13 = (bf16[304,512]{1,0:T(8,128)(2,1)}, bf16[304,512]{1,0:T(8,128)(2,1)S(1)}, u32[]{:S(2)}) copy-start(bf16[304,512]{1,0:T(8,128)(2,1)S(1)} %collective-permute-done.10.refs_12_) | copy-start | bytes 933892
  72.9 2.4 %copy-start.14 = (bf16[304,512]{1,0:T(8,128)(2,1)}, bf16[304,512]{1,0:T(8,128)(2,1)S(1)}, u32[]{:S(2)}) copy-start(bf16[304,512]{1,0:T(8,128)(2,1)S(1)} %collective-permute-done.13.refs_13_) | copy-start | bytes 933892
  75.3 0.7 copy-start.15
  81.3 3.8 %copy-start = (bf16[16,152,512]{2,1,0:T(8,128)(2,1)}, bf16[16,152,512]{2,1,0:T(8,128)(2,1)S(1)}, u32[]{:S(2)}) copy-start(bf16[16,152,512]{2,1,0:T(8,128)(2,1)S(1)} %all-to-all-done.refs_15_.refs_16_) | copy-start | bytes 7471108
  81.3 8.5 %collective-permute-start.15 = (bf16[16,152,512]{2,1,0:T(8,128)(2,1)S(1)}, bf16[16,152,512]{2,1,0:T(8,128)(2,1)}, u32[]{:S(2)}, u32[]{:S(2)}) collective-permute-start(bf16[16,152,512]{2,1,0:T(8,128)(2,1)S(1)} %all-to-all-done.refs_15_.refs_16_), channel_id=1, source_target_pairs={{0,16},{16,0},{1,17},{17,1},{2,18},{18,2},{3,19},{19,3},{4,20},{20... | collective-permute-start | bytes 7471112 | tf_op jit(solution)/shard_map/ppermute | solution.py:229

commit v8 on v6

--- a/solution.py
+++ b/solution.py
@@ -21,7 +21,7 @@
 UP = ("z", "xh", "c")
 NY = 8
 TURNS = (0, -1, 1, -2, 2, -3, 3, 4)
-STEP = 4
+STEP = 5
 DIMS = (((0,), (0,)), ((), ()))
 VMEM = pl.BlockSpec(memory_space=pltpu.VMEM)
 SMEM = pl.BlockSpec(memory_space=pltpu.SMEM)

time: 96.9 us -> 96.7 us (level)
  no operation moved by 1% of the time
where the time goes in v8:
time: 96.7 us; the launch traced here: 96 us
  starting transfers between devices  63.3 us (65%)
  waiting for transfers between devices  16.7 us (17%)
  Pallas kernels  14.8 us (15%)
    ppermute x16, starting transfers between devices, turn(): return lax.ppermute(value, axis, [(i, (i + by) % n) for i in range(n)])  49.7 us
    ppermute x16, waiting for transfers between devices, turn(): return lax.ppermute(value, axis, [(i, (i + by) % n) for i in range(n)])  16.7 us
    all_to_all x1, starting transfers between devices, local(): own = lax.all_to_all(e, ('z', 'xh'), 0, 0, tiled=True)  13.6 us
    pallas_call x1, Pallas kernels, score(): pl.pallas_call(score_kernel, out_shape=jax.ShapeDtypeStruct((UF_DEV, VF_D...  6.36 us
    pallas_call x1, Pallas kernels, half(): pl.pallas_call(half_kernel, out_shape=jax.ShapeDtypeStruct((UF_DEV, COLS)...  4.46 us
    pallas_call x1, Pallas kernels, pack(): pl.pallas_call(pack_kernel, out_shape=(jax.ShapeDtypeStruct((RD, UF_DEV),...  3.96 us
  transfers between devices with their start and end apart: 17, of which 4 were waited for; matrix products, arithmetic and copies ran while one was open for 0% of the time, Pallas kernels for 5%

profile of v8, /device:TPU:1, one launch (start us, length us, event | category | flops | bytes accessed | tf_op | source)
XLA Modules:
  0.0 96.0 jit_solution(8564863132134351805)
XLA Ops:
  0.0 4.0 %shard_map.64 = (bf16[304,512]{1,0:T(8,128)(2,1)}, bf16[16,152,512]{2,1,0:T(8,128)(2,1)}) custom-call(s32[4]{0:T(128)} %down_ref.3, bf16[288,512]{1,0:T(8,128)(2,1)} %bitcast.2, bf16[16,512]{1,0:T(8,128)(2,1)} %delta_ref.1, bf16[144,1024]{1,0:T(8,128)(2,1)} %enc_ref.1, bf16[8,1024]{1,0:T(8,128)(2,1)} %grad_ref.1), custom_call_target="tpu_custom_call" | custom-call | tf_op jit(solution)/shard_map/pallas_call | solution.py:54
  4.0 0.0 copy-start.1
  4.0 13.6 %all-to-all-start = ((bf16[16,152,512]{2,1,0:T(8,128)(2,1)}), bf16[16,152,512]{2,1,0:T(8,128)(2,1)S(1)}, u32[]{:S(2)}, u32[]{:S(2)}) async-start(bf16[16,152,512]{2,1,0:T(8,128)(2,1)} %get-tuple-element.15), calls=%async_computation | async-start | bytes 4980736 | tf_op jit(solution)/shard_map/all_to_all | solution.py:233
  17.6 0.0 copy-done.1
  17.6 3.2 %collective-permute-start.1 = (bf16[304,512]{1,0:T(8,128)(2,1)S(1)}, bf16[304,512]{1,0:T(8,128)(2,1)S(1)}, u32[]{:S(2)}, u32[]{:S(2)}) collective-permute-start(bf16[304,512]{1,0:T(8,128)(2,1)S(1)} %copy-done.1), channel_id=1, source_target_pairs={{0,1},{1,2},{2,3},{3,4},{4,5},{5,6},{6,7},{7,0},{8,9},{9,10},{10,1... | collective-permute-start | bytes 933896 | tf_op jit(solution)/shard_map/ppermute | solution.py:224
  20.8 2.2 %collective-permute-start = (bf16[304,512]{1,0:T(8,128)(2,1)S(1)}, bf16[304,512]{1,0:T(8,128)(2,1)S(1)}, u32[]{:S(2)}, u32[]{:S(2)}) collective-permute-start(bf16[304,512]{1,0:T(8,128)(2,1)S(1)} %copy-done.1), channel_id=1, source_target_pairs={{0,8},{8,0},{1,9},{9,1},{2,10},{10,2},{3,11},{11,3},{4,12},{12,4},... | collective-permute-start | bytes 933896 | tf_op jit(solution)/shard_map/ppermute | solution.py:224
  23.0 6.4 %collective-permute-done.1.refs_2_ = bf16[304,512]{1,0:T(8,128)(2,1)S(1)} collective-permute-done((bf16[304,512]{1,0:T(8,128)(2,1)S(1)}, bf16[304,512]{1,0:T(8,128)(2,1)S(1)}, u32[]{:S(2)}, u32[]{:S(2)}) %collective-permute-start.1) | collective-permute-done | bytes 311328 | tf_op jit(solution)/shard_map/ppermute | solution.py:224
  29.4 1.9 %collective-permute-start.5 = (bf16[304,512]{1,0:T(8,128)(2,1)S(1)}, bf16[304,512]{1,0:T(8,128)(2,1)S(1)}, u32[]{:S(2)}, u32[]{:S(2)}) collective-permute-start(bf16[304,512]{1,0:T(8,128)(2,1)S(1)} %collective-permute-done.1.refs_2_), channel_id=1, source_target_pairs={{0,1},{1,2},{2,3},{3,4},{4,5},{5,6},{6,7},{7,0},{8,9},{9,10},{10,1... | collective-permute-start | bytes 933896 | tf_op jit(solution)/shard_map/ppermute | solution.py:224
  31.3 4.6 %collective-permute-start.3 = (bf16[304,512]{1,0:T(8,128)(2,1)S(1)}, bf16[304,512]{1,0:T(8,128)(2,1)S(1)}, u32[]{:S(2)}, u32[]{:S(2)}) collective-permute-start(bf16[304,512]{1,0:T(8,128)(2,1)S(1)} %copy-done.1), channel_id=1, source_target_pairs={{0,7},{1,0},{2,1},{3,2},{4,3},{5,4},{6,5},{7,6},{8,15},{9,8},{10,9... | collective-permute-start | bytes 933896 | tf_op jit(solution)/shard_map/ppermute | solution.py:224
  35.9 0.0 collective-permute-done.refs_1_
  35.9 0.0 copy-start.3
  35.9 1.9 %collective-permute-start.4 = (bf16[304,512]{1,0:T(8,128)(2,1)S(1)}, bf16[304,512]{1,0:T(8,128)(2,1)S(1)}, u32[]{:S(2)}, u32[]{:S(2)}) collective-permute-start(bf16[304,512]{1,0:T(8,128)(2,1)S(1)} %collective-permute-done.refs_1_), channel_id=1, source_target_pairs={{0,7},{1,0},{2,1},{3,2},{4,3},{5,4},{6,5},{7,6},{8,15},{9,8},{10,9... | collective-permute-start | bytes 933896 | tf_op jit(solution)/shard_map/ppermute | solution.py:224
  37.9 3.4 %collective-permute-start.2 = (bf16[304,512]{1,0:T(8,128)(2,1)S(1)}, bf16[304,512]{1,0:T(8,128)(2,1)S(1)}, u32[]{:S(2)}, u32[]{:S(2)}) collective-permute-start(bf16[304,512]{1,0:T(8,128)(2,1)S(1)} %collective-permute-done.refs_1_), channel_id=1, source_target_pairs={{0,1},{1,2},{2,3},{3,4},{4,5},{5,6},{6,7},{7,0},{8,9},{9,10},{10,1... | collective-permute-start | bytes 933896 | tf_op jit(solution)/shard_map/ppermute | solution.py:224
  41.2 0.0 collective-permute-done.5.refs_6_
  41.3 0.0 copy-start.4
  41.3 1.9 %collective-permute-start.9 = (bf16[304,512]{1,0:T(8,128)(2,1)S(1)}, bf16[304,512]{1,0:T(8,128)(2,1)S(1)}, u32[]{:S(2)}, u32[]{:S(2)}) collective-permute-start(bf16[304,512]{1,0:T(8,128)(2,1)S(1)} %collective-permute-done.5.refs_6_), channel_id=1, source_target_pairs={{0,1},{1,2},{2,3},{3,4},{4,5},{5,6},{6,7},{7,0},{8,9},{9,10},{10,1... | collective-permute-start | bytes 933896 | tf_op jit(solution)/shard_map/ppermute | solution.py:224
  43.2 0.0 collective-permute-done.3.refs_4_
  43.2 0.0 copy-start.5
  43.2 4.6 %collective-permute-start.7 = (bf16[304,512]{1,0:T(8,128)(2,1)S(1)}, bf16[304,512]{1,0:T(8,128)(2,1)S(1)}, u32[]{:S(2)}, u32[]{:S(2)}) collective-permute-start(bf16[304,512]{1,0:T(8,128)(2,1)S(1)} %collective-permute-done.3.refs_4_), channel_id=1, source_target_pairs={{0,7},{1,0},{2,1},{3,2},{4,3},{5,4},{6,5},{7,6},{8,15},{9,8},{10,9... | collective-permute-start | bytes 933896 | tf_op jit(solution)/shard_map/ppermute | solution.py:224
  47.8 0.0 collective-permute-done.4.refs_5_
  47.8 0.0 copy-start.6
  47.8 4.9 %collective-permute-start.8 = (bf16[304,512]{1,0:T(8,128)(2,1)S(1)}, bf16[304,512]{1,0:T(8,128)(2,1)S(1)}, u32[]{:S(2)}, u32[]{:S(2)}) collective-permute-start(bf16[304,512]{1,0:T(8,128)(2,1)S(1)} %collective-permute-done.4.refs_5_), channel_id=1, source_target_pairs={{0,7},{1,0},{2,1},{3,2},{4,3},{5,4},{6,5},{7,6},{8,15},{9,8},{10,9... | collective-permute-start | bytes 933896 | tf_op jit(solution)/shard_map/ppermute | solution.py:224
  52.7 0.0 collective-permute-done.2.refs_3_
  52.7 0.0 copy-start.7
  52.7 1.9 %collective-permute-start.6 = (bf16[304,512]{1,0:T(8,128)(2,1)S(1)}, bf16[304,512]{1,0:T(8,128)(2,1)S(1)}, u32[]{:S(2)}, u32[]{:S(2)}) collective-permute-start(bf16[304,512]{1,0:T(8,128)(2,1)S(1)} %collective-permute-done.2.refs_3_), channel_id=1, source_target_pairs={{0,1},{1,2},{2,3},{3,4},{4,5},{5,6},{6,7},{7,0},{8,9},{9,10},{10,1... | collective-permute-start | bytes 933896 | tf_op jit(solution)/shard_map/ppermute | solution.py:224
  54.7 0.0 collective-permute-done.9.refs_10_
  54.7 0.0 copy-start.8
  54.7 2.1 %collective-permute-start.11 = (bf16[304,512]{1,0:T(8,128)(2,1)S(1)}, bf16[304,512]{1,0:T(8,128)(2,1)S(1)}, u32[]{:S(2)}, u32[]{:S(2)}) collective-permute-start(bf16[304,512]{1,0:T(8,128)(2,1)S(1)} %collective-permute-done.9.refs_10_), channel_id=1, source_target_pairs={{0,1},{1,2},{2,3},{3,4},{4,5},{5,6},{6,7},{7,0},{8,9},{9,10},{10,1... | collective-permute-start | bytes 933896 | tf_op jit(solution)/shard_map/ppermute | solution.py:224
  56.8 0.0 collective-permute-done.7.refs_8_
  56.8 0.0 copy-start.9
  56.8 4.4 %collective-permute-start.10 = (bf16[304,512]{1,0:T(8,128)(2,1)S(1)}, bf16[304,512]{1,0:T(8,128)(2,1)S(1)}, u32[]{:S(2)}, u32[]{:S(2)}) collective-permute-start(bf16[304,512]{1,0:T(8,128)(2,1)S(1)} %collective-permute-done.7.refs_8_), channel_id=1, source_target_pairs={{0,7},{1,0},{2,1},{3,2},{4,3},{5,4},{6,5},{7,6},{8,15},{9,8},{10,9... | collective-permute-start | bytes 933896 | tf_op jit(solution)/shard_map/ppermute | solution.py:224
  61.2 0.0 collective-permute-done.8.refs_9_
  61.2 0.0 copy-start.10
  61.2 4.8 %collective-permute-start.13 = (bf16[304,512]{1,0:T(8,128)(2,1)S(1)}, bf16[304,512]{1,0:T(8,128)(2,1)S(1)}, u32[]{:S(2)}, u32[]{:S(2)}) collective-permute-start(bf16[304,512]{1,0:T(8,128)(2,1)S(1)} %collective-permute-done.8.refs_9_), channel_id=1, source_target_pairs={{0,7},{1,0},{2,1},{3,2},{4,3},{5,4},{6,5},{7,6},{8,15},{9,8},{10,9... | collective-permute-start | bytes 933896 | tf_op jit(solution)/shard_map/ppermute | solution.py:224
  66.0 0.0 collective-permute-done.6.refs_7_
  66.0 0.0 copy-start.11
  66.0 1.9 %collective-permute-start.12 = (bf16[304,512]{1,0:T(8,128)(2,1)S(1)}, bf16[304,512]{1,0:T(8,128)(2,1)S(1)}, u32[]{:S(2)}, u32[]{:S(2)}) collective-permute-start(bf16[304,512]{1,0:T(8,128)(2,1)S(1)} %collective-permute-done.6.refs_7_), channel_id=1, source_target_pairs={{0,1},{1,2},{2,3},{3,4},{4,5},{5,6},{6,7},{7,0},{8,9},{9,10},{10,1... | collective-permute-start | bytes 933896 | tf_op jit(solution)/shard_map/ppermute | solution.py:224
  68.0 0.0 collective-permute-done.11.refs_14_
  68.0 0.0 copy-start.12
  68.0 2.2 %collective-permute-start.14 = (bf16[304,512]{1,0:T(8,128)(2,1)S(1)}, bf16[304,512]{1,0:T(8,128)(2,1)}, u32[]{:S(2)}, u32[]{:S(2)}) collective-permute-start(bf16[304,512]{1,0:T(8,128)(2,1)S(1)} %collective-permute-done.11.refs_14_), channel_id=1, source_target_pairs={{0,8},{8,0},{1,9},{9,1},{2,10},{10,2},{3,11},{11,3},{4,12},{12,4},... | collective-permute-start | bytes 933896 | tf_op jit(solution)/shard_map/ppermute | solution.py:224
  70.2 0.0 collective-permute-done.10.refs_12_
  70.2 0.0 copy-start.13
  70.2 2.6 %collective-permute-done.13.refs_13_ = bf16[304,512]{1,0:T(8,128)(2,1)S(1)} collective-permute-done((bf16[304,512]{1,0:T(8,128)(2,1)S(1)}, bf16[304,512]{1,0:T(8,128)(2,1)S(1)}, u32[]{:S(2)}, u32[]{:S(2)}) %collective-permute-start.13) | collective-permute-done | bytes 311328 | tf_op jit(solution)/shard_map/ppermute | solution.py:224
  72.9 2.4 %collective-permute-done.12.refs_11_ = bf16[304,512]{1,0:T(8,128)(2,1)S(1)} collective-permute-done((bf16[304,512]{1,0:T(8,128)(2,1)S(1)}, bf16[304,512]{1,0:T(8,128)(2,1)S(1)}, u32[]{:S(2)}, u32[]{:S(2)}) %collective-permute-start.12) | collective-permute-done | bytes 311328 | tf_op jit(solution)/shard_map/ppermute | solution.py:224
  75.2 0.0 copy-done.4
  75.2 0.0 copy-done.5
  75.2 0.0 copy-done.6
  75.2 0.0 copy-done.7
  75.2 0.0 copy-done.8
  75.3 0.0 copy-done.10
  75.3 0.0 copy-done.11
  75.3 0.0 copy-done.12
  75.3 0.0 copy-done.13
  75.3 0.0 copy-done.14
  75.3 0.0 copy-start.15
  75.3 0.7 copy-done.15
  76.0 5.2 %collective-permute-done.14.refs_15_ = bf16[304,512]{1,0:T(8,128)(2,1)} collective-permute-done((bf16[304,512]{1,0:T(8,128)(2,1)S(1)}, bf16[304,512]{1,0:T(8,128)(2,1)}, u32[]{:S(2)}, u32[]{:S(2)}) %collective-permute-start.14) | collective-permute-done | bytes 311328 | tf_op jit(solution)/shard_map/ppermute | solution.py:224
  81.3 0.0 all-to-all-done.refs_15_.refs_16_
  81.3 3.8 %collective-permute-start.15 = (bf16[16,152,512]{2,1,0:T(8,128)(2,1)S(1)}, bf16[16,152,512]{2,1,0:T(8,128)(2,1)}, u32[]{:S(2)}, u32[]{:S(2)}) collective-permute-start(bf16[16,152,512]{2,1,0:T(8,128)(2,1)S(1)} %all-to-all-done.refs_15_.refs_16_), channel_id=1, source_target_pairs={{0,16},{16,0},{1,17},{17,1},{2,18},{18,2},{3,19},{19,3},{4,20},{20... | collective-permute-start | bytes 7471112 | tf_op jit(solution)/shard_map/ppermute | solution.py:224
  85.1 0.0 copy-done.2
  85.1 0.0 copy-done.3
  85.1 4.5 %shard_map.65.refs_18_ = f32[512,512]{1,0:T(8,128)} custom-call(bf16[304,512]{1,0:T(8,128)(2,1)} %get-tuple-element.14.refs_0_, bf16[304,512]{1,0:T(8,128)(2,1)} %copy-done.3, bf16[304,512]{1,0:T(8,128)(2,1)} %copy-done.2, bf16[304,512]{1,0:T(8,128)(2,1)} %copy-done.7, bf16[304,512]{1,0:T(8,128)(2,1)} %copy-done.5, bf16[304,512]{1,0:T(8,128)(2,1)} %copy-done.6, ...), custom_call_target="tpu_custom_call" | custom-call | flops 1207959552 | bytes 8388608 | tf_op jit(solution)/shard_map/pallas_call | solution.py:190
  89.6 0.0 collective-permute-done.15.refs_17_
  89.6 6.4 %shard_map.66 = f32[512,1024]{1,0:T(8,128)} custom-call(s32[2,8]{1,0:T(2,128)} %bitcast.3, s32[4]{0:T(128)} %down_ref.3, bf16[304,512]{1,0:T(8,128)(2,1)} %get-tuple-element.14.refs_0_, bf16[304,512]{1,0:T(8,128)(2,1)} %copy-done.3, bf16[304,512]{1,0:T(8,128)(2,1)} %copy-done.2, bf16[304,512]{1,0:T(8,128)(2,1)} %copy-done.7, bf16[304,512]{1,0:T(8,128)(2,1)} %copy-done.5, ...), custom_call_target="tpu_custom_call" | custom-call | flops 1207959552 | bytes 8388608 | tf_op jit(solution)/shard_map/pallas_call | solution.py:202
  (5 shorter events, 0.0 us)
Async XLA Ops:
  4.0 13.6 %copy-start.1 = (bf16[304,512]{1,0:T(8,128)(2,1)S(1)}, bf16[304,512]{1,0:T(8,128)(2,1)}, u32[]{:S(2)}) copy-start(bf16[304,512]{1,0:T(8,128)(2,1)} %get-tuple-element.14.refs_0_) | copy-start | bytes 933892
  4.0 77.3 %all-to-all-start = ((bf16[16,152,512]{2,1,0:T(8,128)(2,1)}), bf16[16,152,512]{2,1,0:T(8,128)(2,1)S(1)}, u32[]{:S(2)}, u32[]{:S(2)}) async-start(bf16[16,152,512]{2,1,0:T(8,128)(2,1)} %get-tuple-element.15), calls=%async_computation | async-start | bytes 4980736 | tf_op jit(solution)/shard_map/all_to_all | solution.py:233
  17.6 11.9 %collective-permute-start.1 = (bf16[304,512]{1,0:T(8,128)(2,1)S(1)}, bf16[304,512]{1,0:T(8,128)(2,1)S(1)}, u32[]{:S(2)}, u32[]{:S(2)}) collective-permute-start(bf16[304,512]{1,0:T(8,128)(2,1)S(1)} %copy-done.1), channel_id=1, source_target_pairs={{0,1},{1,2},{2,3},{3,4},{4,5},{5,6},{6,7},{7,0},{8,9},{9,10},{10,1... | collective-permute-start | bytes 933896 | tf_op jit(solution)/shard_map/ppermute | solution.py:224
  20.8 15.1 %collective-permute-start = (bf16[304,512]{1,0:T(8,128)(2,1)S(1)}, bf16[304,512]{1,0:T(8,128)(2,1)S(1)}, u32[]{:S(2)}, u32[]{:S(2)}) collective-permute-start(bf16[304,512]{1,0:T(8,128)(2,1)S(1)} %copy-done.1), channel_id=1, source_target_pairs={{0,8},{8,0},{1,9},{9,1},{2,10},{10,2},{3,11},{11,3},{4,12},{12,4},... | collective-permute-start | bytes 933896 | tf_op jit(solution)/shard_map/ppermute | solution.py:224
  29.4 55.7 %copy-start.2 = (bf16[304,512]{1,0:T(8,128)(2,1)}, bf16[304,512]{1,0:T(8,128)(2,1)S(1)}, u32[]{:S(2)}) copy-start(bf16[304,512]{1,0:T(8,128)(2,1)S(1)} %collective-permute-done.1.refs_2_) | copy-start | bytes 933892
  29.4 11.8 %collective-permute-start.5 = (bf16[304,512]{1,0:T(8,128)(2,1)S(1)}, bf16[304,512]{1,0:T(8,128)(2,1)S(1)}, u32[]{:S(2)}, u32[]{:S(2)}) collective-permute-start(bf16[304,512]{1,0:T(8,128)(2,1)S(1)} %collective-permute-done.1.refs_2_), channel_id=1, source_target_pairs={{0,1},{1,2},{2,3},{3,4},{4,5},{5,6},{6,7},{7,0},{8,9},{9,10},{10,1... | collective-permute-start | bytes 933896 | tf_op jit(solution)/shard_map/ppermute | solution.py:224
  31.3 11.9 %collective-permute-start.3 = (bf16[304,512]{1,0:T(8,128)(2,1)S(1)}, bf16[304,512]{1,0:T(8,128)(2,1)S(1)}, u32[]{:S(2)}, u32[]{:S(2)}) collective-permute-start(bf16[304,512]{1,0:T(8,128)(2,1)S(1)} %copy-done.1), channel_id=1, source_target_pairs={{0,7},{1,0},{2,1},{3,2},{4,3},{5,4},{6,5},{7,6},{8,15},{9,8},{10,9... | collective-permute-start | bytes 933896 | tf_op jit(solution)/shard_map/ppermute | solution.py:224
  35.9 49.2 %copy-start.3 = (bf16[304,512]{1,0:T(8,128)(2,1)}, bf16[304,512]{1,0:T(8,128)(2,1)S(1)}, u32[]{:S(2)}) copy-start(bf16[304,512]{1,0:T(8,128)(2,1)S(1)} %collective-permute-done.refs_1_) | copy-start | bytes 933892
  35.9 11.9 %collective-permute-start.4 = (bf16[304,512]{1,0:T(8,128)(2,1)S(1)}, bf16[304,512]{1,0:T(8,128)(2,1)S(1)}, u32[]{:S(2)}, u32[]{:S(2)}) collective-permute-start(bf16[304,512]{1,0:T(8,128)(2,1)S(1)} %collective-permute-done.refs_1_), channel_id=1, source_target_pairs={{0,7},{1,0},{2,1},{3,2},{4,3},{5,4},{6,5},{7,6},{8,15},{9,8},{10,9... | collective-permute-start | bytes 933896 | tf_op jit(solution)/shard_map/ppermute | solution.py:224
  37.9 14.8 %collective-permute-start.2 = (bf16[304,512]{1,0:T(8,128)(2,1)S(1)}, bf16[304,512]{1,0:T(8,128)(2,1)S(1)}, u32[]{:S(2)}, u32[]{:S(2)}) collective-permute-start(bf16[304,512]{1,0:T(8,128)(2,1)S(1)} %collective-permute-done.refs_1_), channel_id=1, source_target_pairs={{0,1},{1,2},{2,3},{3,4},{4,5},{5,6},{6,7},{7,0},{8,9},{9,10},{10,1... | collective-permute-start | bytes 933896 | tf_op jit(solution)/shard_map/ppermute | solution.py:224
  41.3 34.0 %copy-start.4 = (bf16[304,512]{1,0:T(8,128)(2,1)}, bf16[304,512]{1,0:T(8,128)(2,1)S(1)}, u32[]{:S(2)}) copy-start(bf16[304,512]{1,0:T(8,128)(2,1)S(1)} %collective-permute-done.5.refs_6_) | copy-start | bytes 933892
  41.3 13.4 %collective-permute-start.9 = (bf16[304,512]{1,0:T(8,128)(2,1)S(1)}, bf16[304,512]{1,0:T(8,128)(2,1)S(1)}, u32[]{:S(2)}, u32[]{:S(2)}) collective-permute-start(bf16[304,512]{1,0:T(8,128)(2,1)S(1)} %collective-permute-done.5.refs_6_), channel_id=1, source_target_pairs={{0,1},{1,2},{2,3},{3,4},{4,5},{5,6},{6,7},{7,0},{8,9},{9,10},{10,1... | collective-permute-start | bytes 933896 | tf_op jit(solution)/shard_map/ppermute | solution.py:224
  43.2 32.0 %copy-start.5 = (bf16[304,512]{1,0:T(8,128)(2,1)}, bf16[304,512]{1,0:T(8,128)(2,1)S(1)}, u32[]{:S(2)}) copy-start(bf16[304,512]{1,0:T(8,128)(2,1)S(1)} %collective-permute-done.3.refs_4_) | copy-start | bytes 933892
  43.2 13.6 %collective-permute-start.7 = (bf16[304,512]{1,0:T(8,128)(2,1)S(1)}, bf16[304,512]{1,0:T(8,128)(2,1)S(1)}, u32[]{:S(2)}, u32[]{:S(2)}) collective-permute-start(bf16[304,512]{1,0:T(8,128)(2,1)S(1)} %collective-permute-done.3.refs_4_), channel_id=1, source_target_pairs={{0,7},{1,0},{2,1},{3,2},{4,3},{5,4},{6,5},{7,6},{8,15},{9,8},{10,9... | collective-permute-start | bytes 933896 | tf_op jit(solution)/shard_map/ppermute | solution.py:224
  47.8 27.4 %copy-start.6 = (bf16[304,512]{1,0:T(8,128)(2,1)}, bf16[304,512]{1,0:T(8,128)(2,1)S(1)}, u32[]{:S(2)}) copy-start(bf16[304,512]{1,0:T(8,128)(2,1)S(1)} %collective-permute-done.4.refs_5_) | copy-start | bytes 933892
  47.8 13.4 %collective-permute-start.8 = (bf16[304,512]{1,0:T(8,128)(2,1)S(1)}, bf16[304,512]{1,0:T(8,128)(2,1)S(1)}, u32[]{:S(2)}, u32[]{:S(2)}) collective-permute-start(bf16[304,512]{1,0:T(8,128)(2,1)S(1)} %collective-permute-done.4.refs_5_), channel_id=1, source_target_pairs={{0,7},{1,0},{2,1},{3,2},{4,3},{5,4},{6,5},{7,6},{8,15},{9,8},{10,9... | collective-permute-start | bytes 933896 | tf_op jit(solution)/shard_map/ppermute | solution.py:224
  52.7 22.5 %copy-start.7 = (bf16[304,512]{1,0:T(8,128)(2,1)}, bf16[304,512]{1,0:T(8,128)(2,1)S(1)}, u32[]{:S(2)}) copy-start(bf16[304,512]{1,0:T(8,128)(2,1)S(1)} %collective-permute-done.2.refs_3_) | copy-start | bytes 933892
  52.7 13.3 %collective-permute-start.6 = (bf16[304,512]{1,0:T(8,128)(2,1)S(1)}, bf16[304,512]{1,0:T(8,128)(2,1)S(1)}, u32[]{:S(2)}, u32[]{:S(2)}) collective-permute-start(bf16[304,512]{1,0:T(8,128)(2,1)S(1)} %collective-permute-done.2.refs_3_), channel_id=1, source_target_pairs={{0,1},{1,2},{2,3},{3,4},{4,5},{5,6},{6,7},{7,0},{8,9},{9,10},{10,1... | collective-permute-start | bytes 933896 | tf_op jit(solution)/shard_map/ppermute | solution.py:224
  54.7 20.6 %copy-start.8 = (bf16[304,512]{1,0:T(8,128)(2,1)}, bf16[304,512]{1,0:T(8,128)(2,1)S(1)}, u32[]{:S(2)}) copy-start(bf16[304,512]{1,0:T(8,128)(2,1)S(1)} %collective-permute-done.9.refs_10_) | copy-start | bytes 933892
  54.7 13.3 %collective-permute-start.11 = (bf16[304,512]{1,0:T(8,128)(2,1)S(1)}, bf16[304,512]{1,0:T(8,128)(2,1)S(1)}, u32[]{:S(2)}, u32[]{:S(2)}) collective-permute-start(bf16[304,512]{1,0:T(8,128)(2,1)S(1)} %collective-permute-done.9.refs_10_), channel_id=1, source_target_pairs={{0,1},{1,2},{2,3},{3,4},{4,5},{5,6},{6,7},{7,0},{8,9},{9,10},{10,1... | collective-permute-start | bytes 933896 | tf_op jit(solution)/shard_map/ppermute | solution.py:224
  56.8 28.3 %copy-start.9 = (bf16[304,512]{1,0:T(8,128)(2,1)}, bf16[304,512]{1,0:T(8,128)(2,1)S(1)}, u32[]{:S(2)}) copy-start(bf16[304,512]{1,0:T(8,128)(2,1)S(1)} %collective-permute-done.7.refs_8_) | copy-start | bytes 933892
  56.8 13.4 %collective-permute-start.10 = (bf16[304,512]{1,0:T(8,128)(2,1)S(1)}, bf16[304,512]{1,0:T(8,128)(2,1)S(1)}, u32[]{:S(2)}, u32[]{:S(2)}) collective-permute-start(bf16[304,512]{1,0:T(8,128)(2,1)S(1)} %collective-permute-done.7.refs_8_), channel_id=1, source_target_pairs={{0,7},{1,0},{2,1},{3,2},{4,3},{5,4},{6,5},{7,6},{8,15},{9,8},{10,9... | collective-permute-start | bytes 933896 | tf_op jit(solution)/shard_map/ppermute | solution.py:224
  61.2 14.0 %copy-start.10 = (bf16[304,512]{1,0:T(8,128)(2,1)}, bf16[304,512]{1,0:T(8,128)(2,1)S(1)}, u32[]{:S(2)}) copy-start(bf16[304,512]{1,0:T(8,128)(2,1)S(1)} %collective-permute-done.8.refs_9_) | copy-start | bytes 933892
  61.2 11.6 %collective-permute-start.13 = (bf16[304,512]{1,0:T(8,128)(2,1)S(1)}, bf16[304,512]{1,0:T(8,128)(2,1)S(1)}, u32[]{:S(2)}, u32[]{:S(2)}) collective-permute-start(bf16[304,512]{1,0:T(8,128)(2,1)S(1)} %collective-permute-done.8.refs_9_), channel_id=1, source_target_pairs={{0,7},{1,0},{2,1},{3,2},{4,3},{5,4},{6,5},{7,6},{8,15},{9,8},{10,9... | collective-permute-start | bytes 933896 | tf_op jit(solution)/shard_map/ppermute | solution.py:224
  66.0 9.3 %copy-start.11 = (bf16[304,512]{1,0:T(8,128)(2,1)}, bf16[304,512]{1,0:T(8,128)(2,1)S(1)}, u32[]{:S(2)}) copy-start(bf16[304,512]{1,0:T(8,128)(2,1)S(1)} %collective-permute-done.6.refs_7_) | copy-start | bytes 933892
  66.0 9.2 %collective-permute-start.12 = (bf16[304,512]{1,0:T(8,128)(2,1)S(1)}, bf16[304,512]{1,0:T(8,128)(2,1)S(1)}, u32[]{:S(2)}, u32[]{:S(2)}) collective-permute-start(bf16[304,512]{1,0:T(8,128)(2,1)S(1)} %collective-permute-done.6.refs_7_), channel_id=1, source_target_pairs={{0,1},{1,2},{2,3},{3,4},{4,5},{5,6},{6,7},{7,0},{8,9},{9,10},{10,1... | collective-permute-start | bytes 933896 | tf_op jit(solution)/shard_map/ppermute | solution.py:224
  68.0 7.3 %copy-start.12 = (bf16[304,512]{1,0:T(8,128)(2,1)}, bf16[304,512]{1,0:T(8,128)(2,1)S(1)}, u32[]{:S(2)}) copy-start(bf16[304,512]{1,0:T(8,128)(2,1)S(1)} %collective-permute-done.11.refs_14_) | copy-start | bytes 933892
  68.0 13.3 %collective-permute-start.14 = (bf16[304,512]{1,0:T(8,128)(2,1)S(1)}, bf16[304,512]{1,0:T(8,128)(2,1)}, u32[]{:S(2)}, u32[]{:S(2)}) collective-permute-start(bf16[304,512]{1,0:T(8,128)(2,1)S(1)} %collective-permute-done.11.refs_14_), channel_id=1, source_target_pairs={{0,8},{8,0},{1,9},{9,1},{2,10},{10,2},{3,11},{11,3},{4,12},{12,4},... | collective-permute-start | bytes 933896 | tf_op jit(solution)/shard_map/ppermute | solution.py:224
  70.2 5.1 %copy-start.13 = (bf16[304,512]{1,0:T(8,128)(2,1)}, bf16[304,512]{1,0:T(8,128)(2,1)S(1)}, u32[]{:S(2)}) copy-start(bf16[304,512]{1,0:T(8,128)(2,1)S(1)} %collective-permute-done.10.refs_12_) | copy-start | bytes 933892
  72.9 2.4 %copy-start.14 = (bf16[304,512]{1,0:T(8,128)(2,1)}, bf16[304,512]{1,0:T(8,128)(2,1)S(1)}, u32[]{:S(2)}) copy-start(bf16[304,512]{1,0:T(8,128)(2,1)S(1)} %collective-permute-done.13.refs_13_) | copy-start | bytes 933892
  75.3 0.7 copy-start.15
  81.3 3.8 %copy-start = (bf16[16,152,512]{2,1,0:T(8,128)(2,1)}, bf16[16,152,512]{2,1,0:T(8,128)(2,1)S(1)}, u32[]{:S(2)}) copy-start(bf16[16,152,512]{2,1,0:T(8,128)(2,1)S(1)} %all-to-all-done.refs_15_.refs_16_) | copy-start | bytes 7471108
  81.3 8.3 %collective-permute-start.15 = (bf16[16,152,512]{2,1,0:T(8,128)(2,1)S(1)}, bf16[16,152,512]{2,1,0:T(8,128)(2,1)}, u32[]{:S(2)}, u32[]{:S(2)}) collective-permute-start(bf16[16,152,512]{2,1,0:T(8,128)(2,1)S(1)} %all-to-all-done.refs_15_.refs_16_), channel_id=1, source_target_pairs={{0,16},{16,0},{1,17},{17,1},{2,18},{18,2},{3,19},{19,3},{4,20},{20... | collective-permute-start | bytes 7471112 | tf_op jit(solution)/shard_map/ppermute | solution.py:224
